TPU v7x, 512 devices: a whole 4x8x8 slice. The times are simulated.
512 devices in a mesh: pipe: 2 (over x_lo), dp: 16 (over y, core), inner: 16 (over x_hi, z).
Axes of the slice: x: 4 (x_hi: 2, x_lo: 2; x = x_hi * 2 + x_lo), y: 8, z: 8, core: 2. Of those that a mesh axis runs over, the one named last changes fastest.
Arguments:
- pixels: bfloat16 [64, 48, 16, 256], P('dp', 'inner'), may hold values from -6 to 6
- date_days: int32 [64, 16], P('dp'), may hold values from 0 to 364
- clear_count: int32 [64], P('dp'), may hold values from 3 to 16, as said below
- batch_slot: int32 [64], P('dp'), may hold values from 0 to 3, as said below
- labels: int32 [64, 48], P('dp'), may hold values from 0 to 15
- class_tokens: bfloat16 [16, 256], replicated, may hold values from -6 to 6
- section_gain: float32 [2, 256], P('pipe'), may hold values from 0.5 to 2
- segment_probe_lookup_content: bfloat16 [2, 256, 768], P('pipe'), may hold values from -0.375 to 0.375
- section_out: bfloat16 [2, 256, 256], P('pipe'), may hold values from -0.375 to 0.375
- head_vec: float32 [256], replicated, may hold values from -1 to 1
Outputs:
- batch_loss: float32 [4], replicated
- class_grad: float32 [16, 256], replicated
- section_gain_grad: float32 [2, 256], P('pipe')
- section_qkv_grad: float32 [2, 256, 768], P('pipe')
- section_out_grad: float32 [2, 256, 256], P('pipe')
- readout_derivative: float32 [256], replicated
Inputs may be any that keep to these rules, and one draw needn't show every extreme that they name: The clear dates of tile b are its dates 0 to clear_count[b] - 1. Some tile has all 16 dates clear and some tile has the fewest. `batch_slot`: within each aligned block of 4 tiles (the tiles of one index of dp) every micro-batch number appears exactly once.
All inputs are finite; a program needn't handle non-finite values.
Results may differ from a plain program's by a relative error of at most 0.0015.
The roundings to bfloat16 on the way count: a program that leaves them out, or rounds other values in their place, can miss the bound.
Values may be sent and summed in bfloat16 or wider, within the bound.
No kernel may reach another device: no remote copies, remote signals or barrier semaphores. Data moves between devices by JAX's collectives and lax.ppermute only.
A program may use at most 64 MiB of HBM per device.

v0:
```python
import math

import jax
import jax.numpy as jnp
from jax import lax
from jax.sharding import PartitionSpec as P

HEADS = 8
CLASSES = 16
PATCHES = 48
MICRO = 4


normalizer_sharpness = 10.0
logit_cap = 15.0
norm_eps = 1e-05
head_eps = 1e-06


def swapped(block, axis, bit):
    count = lax.axis_size(axis)
    route = []
    for low in range(count):
        high = low | 1 << bit
        if high != low and high < count:
            route += [(low, high), (high, low)]
    return lax.ppermute(block, axis, route)


def matmul_f32(left_side, right_side):
    return jnp.einsum(
        "...d,de->...e",
        left_side,
        right_side.astype(jnp.bfloat16),
        preferred_element_type=jnp.float32,
    )


def rms_norm(inputs, gain_vec):
    inverse_rms = lax.rsqrt(jnp.mean(inputs * inputs, axis=-1, keepdims=True) + norm_eps)
    return inputs * inverse_rms * gain_vec


def unit_heads(values):
    shaped = values.reshape(values.shape[:-1] + (HEADS, values.shape[-1] // HEADS))
    return shaped * lax.rsqrt(jnp.sum(shaped * shaped, axis=-1, keepdims=True) + head_eps)


def temporal(pixel_rows, date_days, counts, params):
    class_init, gain_vec, w_qkv, w_out = params
    batch_count, patches, dates_max, model_width = pixel_rows.shape
    classes = class_init.shape[0]
    band_channel = jnp.arange(model_width)
    frequency = jnp.exp(
        (band_channel // 2 * 2).astype(jnp.float32) * (-math.log(10000.0) / model_width)
    )
    phases = date_days.astype(jnp.float32)[:, :, None] * frequency
    encoding = jnp.where(band_channel % 2 == 0, jnp.sin(phases), jnp.cos(phases))
    date_rows = pixel_rows.astype(jnp.float32) + encoding[:, None]
    class_rows = jnp.broadcast_to(class_init, (batch_count, patches, classes, model_width))
    sequence = jnp.concatenate([class_rows, date_rows], axis=2)
    normed = rms_norm(sequence, gain_vec).astype(jnp.bfloat16)
    probe_entry_lines = unit_heads(matmul_f32(normed[:, :, :classes], w_qkv[:, :model_width]))
    lookup_entry_lines = unit_heads(matmul_f32(normed, w_qkv[:, model_width : 2 * model_width]))
    value_rows = matmul_f32(normed, w_qkv[:, 2 * model_width :]).astype(jnp.bfloat16)
    value_heads = value_rows.reshape(
        batch_count, patches, classes + dates_max, HEADS, model_width // HEADS
    )
    affinity_logit_grid = normalizer_sharpness * jnp.einsum(
        "ohbyv,ohsyv->ohybs", probe_entry_lines, lookup_entry_lines, precision=lax.Precision.HIGHEST
    )
    position = jnp.arange(classes + dates_max)
    key_mask = (
        (position[None, :] < classes) | (position[None, :] - classes < counts[:, None])
    ).astype(jnp.float32)
    raised = jnp.exp(affinity_logit_grid) * key_mask[:, None, None, None, :]
    weights = (raised / jnp.sum(raised, axis=-1, keepdims=True)).astype(jnp.bfloat16)
    attended = jnp.einsum(
        "bphqk,bpkhe->bpqhe", weights, value_heads, preferred_element_type=jnp.float32
    )
    attended = attended.reshape(batch_count, patches, classes, model_width).astype(jnp.bfloat16)
    updated = sequence[:, :, :classes] + matmul_f32(attended, w_out)
    return jnp.swapaxes(updated, 1, 2).astype(jnp.bfloat16)


def spatial(inputs, params):
    gain_vec, w_qkv, w_out, head_vec = params
    batch_count, groups, classes, patches, model_width = inputs.shape
    class_seq = (
        jnp.swapaxes(inputs, 1, 2)
        .reshape(batch_count, classes, groups * patches, model_width)
        .astype(jnp.float32)
    )
    normed = rms_norm(class_seq, gain_vec).astype(jnp.bfloat16)
    probe_entry_lines = unit_heads(matmul_f32(normed, w_qkv[:, :model_width]))
    lookup_entry_lines = unit_heads(matmul_f32(normed, w_qkv[:, model_width : 2 * model_width]))
    value_rows = matmul_f32(normed, w_qkv[:, 2 * model_width :]).astype(jnp.bfloat16)
    value_heads = value_rows.reshape(
        batch_count, classes, groups * patches, HEADS, model_width // HEADS
    )
    affinity_logit_grid = normalizer_sharpness * jnp.einsum(
        "wisbx,wiqbx->wibsq", probe_entry_lines, lookup_entry_lines, precision=lax.Precision.HIGHEST
    )
    raised = jnp.exp(affinity_logit_grid)
    weights = (raised / jnp.sum(raised, axis=-1, keepdims=True)).astype(jnp.bfloat16)
    attended = jnp.einsum(
        "bchqk,bckhe->bcqhe", weights, value_heads, preferred_element_type=jnp.float32
    )
    attended = attended.reshape(batch_count, classes, groups * patches, model_width).astype(
        jnp.bfloat16
    )
    hidden = class_seq + matmul_f32(attended, w_out)
    raw_logits = jnp.einsum("bcpd,d->bcp", hidden, head_vec, precision=lax.Precision.HIGHEST)
    logits = logit_cap * jnp.tanh(raw_logits / logit_cap)
    return logits.reshape(batch_count, classes, groups, patches)


def shards(
    pixels,
    date_days,
    clear_count,
    batch_slot,
    labels,
    class_tokens,
    section_gain,
    segment_probe_lookup_content,
    section_out,
    head_vec,
):
    tiles_dev = pixels.shape[0]
    per_batch = tiles_dev // MICRO
    patches_dev = pixels.shape[1]
    model_width = pixels.shape[3]
    inner_count = lax.axis_size("inner")
    classes_dev = CLASSES // inner_count
    total_tiles = tiles_dev * lax.axis_size("dp")
    is_first = lax.axis_index("pipe") == 0
    my_group = lax.axis_index("inner")
    class_ids = my_group * classes_dev + jnp.arange(classes_dev, dtype=jnp.int32)
    batch_norm = 1.0 / (total_tiles // MICRO * PATCHES)
    tile_order = jnp.argsort(batch_slot, stable=True)
    gain_vec = section_gain[0]
    w_qkv = segment_probe_lookup_content[0].astype(jnp.float32)
    w_out = section_out[0].astype(jnp.float32)
    first_params = (class_tokens.astype(jnp.float32), gain_vec, w_qkv, w_out)
    second_params = (gain_vec, w_qkv, w_out, head_vec)
    payload_shape = (per_batch, inner_count, classes_dev, patches_dev, model_width)
    zero_payload = jnp.zeros(payload_shape, jnp.bfloat16)
    zero_sums = jnp.zeros((per_batch, inner_count, patches_dev), jnp.float32)

    def chosen(batch_idx):
        picked = tile_order[batch_idx * per_batch : (batch_idx + 1) * per_batch]
        return (pixels[picked], date_days[picked], clear_count[picked], labels[picked])

    def encode(batch_idx):
        picked = chosen(batch_idx)
        return temporal(picked[0], picked[1], picked[2], first_params).reshape(payload_shape)

    def encode_back(batch_idx, grad_out, totals):
        picked = chosen(batch_idx)
        encoded, pullback = jax.vjp(
            lambda params: temporal(picked[0], picked[1], picked[2], params), first_params
        )
        (grad_params,) = pullback(grad_out.reshape(encoded.shape))
        return (
            totals[0] + grad_params[0],
            totals[1] + grad_params[1],
            totals[2] + grad_params[2],
            totals[3] + grad_params[3],
            totals[4],
            totals[5],
        )

    def class_sums_local(inputs):
        return jnp.sum(jnp.exp(spatial(inputs, second_params)), axis=1)

    def decode_back(batch_idx, inputs, class_total, totals):
        label_rows = chosen(batch_idx)[3].reshape(per_batch, 1, inner_count, patches_dev)
        logits, pullback = jax.vjp(spatial, inputs, second_params)
        indicator_rows = (label_rows == class_ids[None, :, None, None]).astype(jnp.float32)
        dlogit = (jnp.exp(logits) / class_total[:, None] - indicator_rows) / total_tiles
        grad_in, grad_params = pullback(dlogit)
        loss_term = jnp.sum(indicator_rows * (jnp.log(class_total)[:, None] - logits)) * batch_norm
        loss_vec = totals[5] + loss_term * (jnp.arange(MICRO) == batch_idx).astype(jnp.float32)
        return (
            grad_in,
            (
                totals[0],
                totals[1] + grad_params[0],
                totals[2] + grad_params[1],
                totals[3] + grad_params[2],
                totals[4] + grad_params[3],
                loss_vec,
            ),
        )

    totals = (
        jnp.zeros((CLASSES, model_width), jnp.float32),
        jnp.zeros((model_width,), jnp.float32),
        jnp.zeros((model_width, 3 * model_width), jnp.float32),
        jnp.zeros((model_width, model_width), jnp.float32),
        jnp.zeros((model_width,), jnp.float32),
        jnp.zeros((MICRO,), jnp.float32),
    )
    arrived = zero_payload
    saved_grads = []
    iteration_tally = MICRO + 1
    for section_step in range(iteration_tally):
        inputs_now = arrived

        def section_one_a():
            if section_step < MICRO:
                return (encode(section_step), zero_sums)
            return (zero_payload, zero_sums)

        def section_two_a():
            if 1 <= section_step <= MICRO:
                return (zero_payload, class_sums_local(inputs_now))
            return (zero_payload, zero_sums)

        payload, part_sums = lax.cond(is_first, section_one_a, section_two_a)
        if 1 <= section_step <= MICRO:
            class_total = lax.psum(part_sums, "inner")
        else:
            class_total = zero_sums + 1.0

        def section_one_b():
            return (payload, totals)

        def section_two_b():
            if 1 <= section_step <= MICRO:
                return decode_back(section_step - 1, inputs_now, class_total, totals)
            return (zero_payload, totals)

        payload, totals = lax.cond(is_first, section_one_b, section_two_b)
        regrouped = lax.all_to_all(payload, "inner", split_axis=1, concat_axis=1, tiled=True)
        arrived = swapped(regrouped, "pipe", 0)
        saved_grads.append(arrived)

    def section_one_c():
        new_totals = totals
        for batch_idx in range(MICRO):
            new_totals = encode_back(batch_idx, saved_grads[batch_idx + 1], new_totals)
        return new_totals

    totals = lax.cond(is_first, section_one_c, lambda: totals)
    position = lax.axis_index("pipe")
    section_onehot = (jnp.arange(lax.axis_size("pipe")) == position).astype(jnp.float32)
    stacked = (
        section_onehot[:, None] * totals[1][None],
        section_onehot[:, None, None] * totals[2][None],
        section_onehot[:, None, None] * totals[3][None],
        totals[0],
        totals[4],
        totals[5],
    )
    summed = lax.psum(
        (stacked[0], stacked[1], stacked[2], stacked[3], stacked[4], stacked[5]),
        ("pipe", "dp", "inner"),
    )
    gain_grad = lax.dynamic_slice_in_dim(summed[0], position, 1, 0)
    qkv_grad = lax.dynamic_slice_in_dim(summed[1], position, 1, 0)
    out_grad = lax.dynamic_slice_in_dim(summed[2], position, 1, 0)
    class_grad, readout_derivative, batch_loss = (summed[3], summed[4], summed[5])
    return (batch_loss, class_grad, gain_grad, qkv_grad, out_grad, readout_derivative)


def solution(mesh):
    placed = (
        P("dp", "inner", None, None),
        P("dp", None),
        P("dp"),
        P("dp"),
        P("dp", None),
        P(),
        P("pipe", None),
        P("pipe", None, None),
        P("pipe", None, None),
        P(),
    )
    return jax.shard_map(
        shards,
        mesh=mesh,
        in_specs=placed,
        out_specs=(P(), P(), P("pipe", None), P("pipe", None, None), P("pipe", None, None), P()),
        check_vma=False,
    )
```

profile of v0, /device:TPU:1, one launch (start us, length us, event | category | flops | bytes accessed | tf_op | source)
XLA Modules:
  0.0 765.7 jit_solution(11845929317335073932)
XLA Ops:
  9.3 9.7 %conditional.11 = (bf16[1,16,1,3,256]{4,1,3,2,0:T(8,128)(2,1)S(1)}) conditional(s32[]{:T(128)} %convert_element_type.1901, () %tuple.93, (f32[16,256]{1,0:T(8,128)S(1)}, s32[4]{0:T(128)S(1)}, bf16[4,3,16,256]{3,2,1,0:T(8,128)(2,1)}, s32[4,16]{1,0:T(4,128)}, f32[1,256]{1,0:T(1,128)}, /*index=5*/bf16[256,768]{1,0:T(8,128)(2,1)}, s32[4]{0:T(128)}, ...), branch_computations={%region_1.2_spmd, %region_2.7_spmd} | conditional | flops 43832500 | bytes 3427430 | solution.py:221
  19.1 22.1 %all_to_all.25 = bf16[1,16,1,3,256]{4,3,2,0,1:T(4,128)(2,1)S(1)} all-to-all(bf16[1,16,1,3,256]{4,3,2,0,1:T(4,128)(2,1)S(1)} %bitcast.1263), channel_id=1, replica_groups=mesh['pipe'=2,'dp'=16,'inner'=16] {'inner'}, dimensions={1} | all-to-all | bytes 49152 | tf_op jit(solution)/shard_map/all_to_all | solution.py:236
  43.1 2.7 collective-permute-done
  45.8 12.1 %conditional.13 = (f32[1,16,3]{2,1,0:T(8,128)S(1)}, bf16[1,16,1,3,256]{4,1,3,2,0:T(8,128)(2,1)S(1)}) conditional(s32[]{:T(128)} %convert_element_type.1901, (bf16[1,16,1,3,256]{4,3,2,0,1:T(4,128)(2,1)S(1)}, f32[1,256]{1,0:T(1,128)}, bf16[256,768]{1,0:T(8,128)(2,1)}, bf16[256,256]{1,0:T(8,128)(2,1)}, f32[256]{0:T(256)S(1)}) %tuple.476, ...), branch_computations={%region_9.14_spmd, %region_14.19_spmd} | conditional | flops 43832500 | bytes 3427642 | solution.py:221
  57.9 31.1 %psum.70 = f32[1,16,3]{2,1,0:T(8,128)S(1)} all-reduce(f32[1,16,3]{2,1,0:T(8,128)S(1)} %get-tuple-element.456), channel_id=1, replica_groups=mesh['pipe'=2,'dp'=16,'inner'=16] {'inner'}, use_global_device_ids=true, to_apply=%region_19.20 | all-reduce | flops 48 | bytes 384 | tf_op jit(solution)/shard_map/psum | solution.py:223
  89.8 12.6 %all_to_all.26 = bf16[1,16,1,3,256]{4,3,2,0,1:T(4,128)(2,1)S(1)} all-to-all(bf16[1,16,1,3,256]{4,3,2,0,1:T(4,128)(2,1)S(1)} %bitcast.1259), channel_id=1, replica_groups=mesh['pipe'=2,'dp'=16,'inner'=16] {'inner'}, dimensions={1} | all-to-all | bytes 49152 | tf_op jit(solution)/shard_map/all_to_all | solution.py:236
  102.5 9.1 %collective-permute-start.1 = (bf16[1,16,1,3,256]{4,3,2,0,1:T(4,128)(2,1)S(1)}, bf16[1,16,1,3,256]{4,3,2,0,1:T(4,128)(2,1)S(1)}, u32[]{:S(2)}, u32[]{:S(2)}) collective-permute-start(bf16[1,16,1,3,256]{4,3,2,0,1:T(4,128)(2,1)S(1)} %all_to_all.26), channel_id=1, source_target_pairs={{0,256},{256,0},{1,257},{257,1},{2,258},{258,2},{3,259},{259,3},{4... | collective-permute-start | bytes 73736 | tf_op jit(solution)/shard_map/ppermute | solution.py:27
  113.2 10.3 %conditional.15 = (bf16[1,16,1,3,256]{4,1,3,2,0:T(8,128)(2,1)S(1)}, f32[1,16,3]{2,1,0:T(8,128)S(1)}) conditional(s32[]{:T(128)} %convert_element_type.1901, (bf16[1,16,1,3,256]{4,3,2,0,1:T(4,128)(2,1)S(1)}, f32[1,256]{1,0:T(1,128)}, bf16[256,768]{1,0:T(8,128)(2,1)}, bf16[256,256]{1,0:T(8,128)(2,1)}, f32[256]{0:T(256)S(1)}) %tuple.478, ...), branch_computations={%region_32.37_spmd, %region_37.42_spmd} | conditional | flops 43832500 | bytes 3427642 | solution.py:221
  123.5 31.5 %psum.71 = f32[1,16,3]{2,1,0:T(8,128)S(1)} all-reduce(f32[1,16,3]{2,1,0:T(8,128)S(1)} %get-tuple-element.459), channel_id=1, replica_groups=mesh['pipe'=2,'dp'=16,'inner'=16] {'inner'}, use_global_device_ids=true, to_apply=%region_42.43 | all-reduce | flops 48 | bytes 384 | tf_op jit(solution)/shard_map/psum | solution.py:223
  155.0 12.0 %all_to_all.27 = bf16[1,16,1,3,256]{4,3,2,0,1:T(4,128)(2,1)S(1)} all-to-all(bf16[1,16,1,3,256]{4,3,2,0,1:T(4,128)(2,1)S(1)} %bitcast.1261), channel_id=1, replica_groups=mesh['pipe'=2,'dp'=16,'inner'=16] {'inner'}, dimensions={1} | all-to-all | bytes 49152 | tf_op jit(solution)/shard_map/all_to_all | solution.py:236
  167.0 16.9 %collective-permute-start.2 = (bf16[1,16,1,3,256]{4,3,2,0,1:T(4,128)(2,1)S(1)}, bf16[1,16,1,3,256]{4,3,2,0,1:T(4,128)(2,1)S(1)}, u32[]{:S(2)}, u32[]{:S(2)}) collective-permute-start(bf16[1,16,1,3,256]{4,3,2,0,1:T(4,128)(2,1)S(1)} %all_to_all.27), channel_id=1, source_target_pairs={{0,256},{256,0},{1,257},{257,1},{2,258},{258,2},{3,259},{259,3},{4... | collective-permute-start | bytes 73736 | tf_op jit(solution)/shard_map/ppermute | solution.py:27
  185.5 10.1 %conditional.17 = (bf16[1,16,1,3,256]{4,1,3,2,0:T(8,128)(2,1)S(1)}, f32[1,16,3]{2,1,0:T(8,128)S(1)}) conditional(s32[]{:T(128)} %convert_element_type.1901, (bf16[1,16,1,3,256]{4,3,2,0,1:T(4,128)(2,1)S(1)}, f32[1,256]{1,0:T(1,128)}, bf16[256,768]{1,0:T(8,128)(2,1)}, bf16[256,256]{1,0:T(8,128)(2,1)}, f32[256]{0:T(256)S(1)}) %tuple.480, ...), branch_computations={%region_55.60_spmd, %region_60.65_spmd} | conditional | flops 43832500 | bytes 3427642 | solution.py:221
  195.6 31.4 %psum.72 = f32[1,16,3]{2,1,0:T(8,128)S(1)} all-reduce(f32[1,16,3]{2,1,0:T(8,128)S(1)} %get-tuple-element.467), channel_id=1, replica_groups=mesh['pipe'=2,'dp'=16,'inner'=16] {'inner'}, use_global_device_ids=true, to_apply=%region_65.66 | all-reduce | flops 48 | bytes 384 | tf_op jit(solution)/shard_map/psum | solution.py:223
  227.3 12.0 %all_to_all.28 = bf16[1,16,1,3,256]{4,3,2,0,1:T(4,128)(2,1)S(1)} all-to-all(bf16[1,16,1,3,256]{4,3,2,0,1:T(4,128)(2,1)S(1)} %bitcast.1262), channel_id=1, replica_groups=mesh['pipe'=2,'dp'=16,'inner'=16] {'inner'}, dimensions={1} | all-to-all | bytes 49152 | tf_op jit(solution)/shard_map/all_to_all | solution.py:236
  239.3 16.6 %collective-permute-start.3 = (bf16[1,16,1,3,256]{4,3,2,0,1:T(4,128)(2,1)S(1)}, bf16[1,16,1,3,256]{4,3,2,0,1:T(4,128)(2,1)S(1)}, u32[]{:S(2)}, u32[]{:S(2)}) collective-permute-start(bf16[1,16,1,3,256]{4,3,2,0,1:T(4,128)(2,1)S(1)} %all_to_all.28), channel_id=1, source_target_pairs={{0,256},{256,0},{1,257},{257,1},{2,258},{258,2},{3,259},{259,3},{4... | collective-permute-start | bytes 73736 | tf_op jit(solution)/shard_map/ppermute | solution.py:27
  257.2 32.1 %psum.73 = f32[1,16,3]{2,1,0:T(8,128)S(1)} all-reduce(f32[1,16,3]{2,1,0:T(8,128)S(1)} %get-tuple-element.1521), channel_id=1, replica_groups=mesh['pipe'=2,'dp'=16,'inner'=16] {'inner'}, use_global_device_ids=true, to_apply=%region_84.85 | all-reduce | flops 48 | bytes 384 | tf_op jit(solution)/shard_map/psum | solution.py:223
  289.4 11.6 %all_to_all.29 = bf16[1,16,1,3,256]{4,3,2,0,1:T(4,128)(2,1)S(1)} all-to-all(bf16[1,16,1,3,256]{4,3,2,0,1:T(4,128)(2,1)S(1)} %bitcast.1260), channel_id=1, replica_groups=mesh['pipe'=2,'dp'=16,'inner'=16] {'inner'}, dimensions={1} | all-to-all | bytes 49152 | tf_op jit(solution)/shard_map/all_to_all | solution.py:236
  301.0 26.7 %collective-permute-start.4 = (bf16[1,16,1,3,256]{4,3,2,0,1:T(4,128)(2,1)S(1)}, bf16[1,16,1,3,256]{4,3,2,0,1:T(4,128)(2,1)S(1)}, u32[]{:S(2)}, u32[]{:S(2)}) collective-permute-start(bf16[1,16,1,3,256]{4,3,2,0,1:T(4,128)(2,1)S(1)} %all_to_all.29), channel_id=1, source_target_pairs={{0,256},{256,0},{1,257},{257,1},{2,258},{258,2},{3,259},{259,3},{4... | collective-permute-start | bytes 73736 | tf_op jit(solution)/shard_map/ppermute | solution.py:27
  329.0 105.6 %conditional.21 = (f32[16,256]{1,0:T(8,128)S(1)}, f32[256]{0:T(256)}, f32[256,768]{1,0:T(8,128)S(1)}, f32[256,256]{1,0:T(8,128)S(1)}) conditional(s32[]{:T(128)} %convert_element_type.1901, (f32[256]{0:T(256)}, f32[256,768]{1,0:T(8,128)S(1)}, f32[256,256]{1,0:T(8,128)S(1)}) %tuple.107, (bf16[1,16,1,3,256]{4,3,2,0,1:T(4,128)(2,1)S(1)}, ...), branch_computations={%region_98.99_spmd, %region_99.140_spmd} | conditional | flops 507365824 | bytes 48290804 | solution.py:246
  381.1 2.0 multiply_reduce_fusion.57
  436.2 2.0 broadcast_multiply_fusion.20
  439.6 136.6 %all-reduce.32 = (f32[4]{0:T(128)}, f32[16,256]{1,0:T(8,128)}, f32[2,256]{1,0:T(2,128)S(1)}, f32[256]{0:T(256)}) all-reduce(f32[4]{0:T(128)S(1)} %copy-done.119, f32[16,256]{1,0:T(8,128)S(1)} %get-tuple-element.485, f32[2,256]{1,0:T(2,128)S(1)} %broadcast_multiply_fusion.22, ...), channel_id=1, replica_groups=mesh['pipe'=2,'dp'=16,'inner'=16] {'pipe','dp','inner'}, use_global_device_ids=true, to_apply=%region_97.98 | all-reduce | flops 4868 | bytes 38944 | tf_op jit(solution)/shard_map/psum | solution.py:257
  576.9 178.9 %all-reduce.36.cloned.1.call-done = (f32[2,256,768]{2,1,0:T(8,128)}, f32[2,256,256]{2,1,0:T(8,128)}) async-done(((f32[2,256,768]{2,1,0:T(8,128)}, f32[2,256,256]{2,1,0:T(8,128)}), (f32[2,256,768]{2,1,0:T(8,128)}, f32[2,256,256]{2,1,0:T(8,128)})) %all-reduce.36.cloned.1.call-update) | async-done | bytes 2097168 | tf_op jit(solution)/shard_map/psum | solution.py:257
  755.8 2.1 constant_dynamic-slice_fusion.9
  (555 shorter events, 144.7 us)
Async XLA Ops:
  7.2 748.6 %all-reduce.36.cloned.1.call-start = ((), (), s32[]{:S(2)}) async-start(), calls=%async_computation.5 | async-start | bytes 4194304 | tf_op jit(solution)/shard_map/psum | solution.py:257
  9.3 36.5 %copy-start.47 = (f32[256]{0:T(256)S(1)}, f32[256]{0:T(256)}, u32[]{:S(2)}) copy-start(f32[256]{0:T(256)} %param.41) | copy-start | bytes 3076
  41.2 4.6 collective-permute-start
  45.8 43.3 %copy-start.116 = (s32[4,48]{1,0:T(4,128)S(1)}, s32[4,48]{1,0:T(4,128)}, u32[]{:S(2)}) copy-start(s32[4,48]{1,0:T(4,128)} %param.36) | copy-start | bytes 2308
  89.1 24.1 %copy-start.27 = (bf16[4,3,16,256]{3,2,1,0:T(8,128)(2,1)S(1)}, bf16[4,3,16,256]{3,2,1,0:T(8,128)(2,1)}, u32[]{:S(2)}) copy-start(bf16[4,3,16,256]{3,2,1,0:T(8,128)(2,1)} %param.32) | copy-start | bytes 294916
  89.1 24.1 %copy-start.110 = (s32[4]{0:T(128)S(1)}, s32[4]{0:T(128)}, u32[]{:S(2)}) copy-start(s32[4]{0:T(128)} %param.34) | copy-start | bytes 52
  89.1 24.1 %copy-start.117 = (s32[4,16]{1,0:T(4,128)S(1)}, s32[4,16]{1,0:T(4,128)}, u32[]{:S(2)}) copy-start(s32[4,16]{1,0:T(4,128)} %param.33) | copy-start | bytes 772
  102.5 10.7 %collective-permute-start.1 = (bf16[1,16,1,3,256]{4,3,2,0,1:T(4,128)(2,1)S(1)}, bf16[1,16,1,3,256]{4,3,2,0,1:T(4,128)(2,1)S(1)}, u32[]{:S(2)}, u32[]{:S(2)}) collective-permute-start(bf16[1,16,1,3,256]{4,3,2,0,1:T(4,128)(2,1)S(1)} %all_to_all.26), channel_id=1, source_target_pairs={{0,256},{256,0},{1,257},{257,1},{2,258},{258,2},{3,259},{259,3},{4... | collective-permute-start | bytes 73736 | tf_op jit(solution)/shard_map/ppermute | solution.py:27
  167.0 18.5 %collective-permute-start.2 = (bf16[1,16,1,3,256]{4,3,2,0,1:T(4,128)(2,1)S(1)}, bf16[1,16,1,3,256]{4,3,2,0,1:T(4,128)(2,1)S(1)}, u32[]{:S(2)}, u32[]{:S(2)}) collective-permute-start(bf16[1,16,1,3,256]{4,3,2,0,1:T(4,128)(2,1)S(1)} %all_to_all.27), channel_id=1, source_target_pairs={{0,256},{256,0},{1,257},{257,1},{2,258},{258,2},{3,259},{259,3},{4... | collective-permute-start | bytes 73736 | tf_op jit(solution)/shard_map/ppermute | solution.py:27
  239.3 17.9 %collective-permute-start.3 = (bf16[1,16,1,3,256]{4,3,2,0,1:T(4,128)(2,1)S(1)}, bf16[1,16,1,3,256]{4,3,2,0,1:T(4,128)(2,1)S(1)}, u32[]{:S(2)}, u32[]{:S(2)}) collective-permute-start(bf16[1,16,1,3,256]{4,3,2,0,1:T(4,128)(2,1)S(1)} %all_to_all.28), channel_id=1, source_target_pairs={{0,256},{256,0},{1,257},{257,1},{2,258},{258,2},{3,259},{259,3},{4... | collective-permute-start | bytes 73736 | tf_op jit(solution)/shard_map/ppermute | solution.py:27
  289.4 39.6 %copy-start.99 = (f32[256]{0:T(256)}, f32[256]{0:T(256)S(1)}, u32[]{:S(2)}) copy-start(f32[256]{0:T(256)S(1)} %get-tuple-element.489) | copy-start | bytes 3076
  289.4 39.6 %copy-start.118 = (f32[4]{0:T(128)}, f32[4]{0:T(128)S(1)}, u32[]{:S(2)}) copy-start(f32[4]{0:T(128)S(1)} %get-tuple-element.480) | copy-start | bytes 52
  301.0 28.0 %collective-permute-start.4 = (bf16[1,16,1,3,256]{4,3,2,0,1:T(4,128)(2,1)S(1)}, bf16[1,16,1,3,256]{4,3,2,0,1:T(4,128)(2,1)S(1)}, u32[]{:S(2)}, u32[]{:S(2)}) collective-permute-start(bf16[1,16,1,3,256]{4,3,2,0,1:T(4,128)(2,1)S(1)} %all_to_all.29), channel_id=1, source_target_pairs={{0,256},{256,0},{1,257},{257,1},{2,258},{258,2},{3,259},{259,3},{4... | collective-permute-start | bytes 73736 | tf_op jit(solution)/shard_map/ppermute | solution.py:27
  329.4 24.4 %copy-start.61 = (bf16[1,16,1,3,256]{4,3,2,0,1:T(4,128)(2,1)}, bf16[1,16,1,3,256]{4,3,2,0,1:T(4,128)(2,1)S(1)}, u32[]{:S(2)}) copy-start(bf16[1,16,1,3,256]{4,3,2,0,1:T(4,128)(2,1)S(1)} %get-tuple-element.1231) | copy-start | bytes 73732 | tf_op jit(solution)/shard_map/cond
  329.4 24.0 %copy-start.4 = (bf16[256,768]{1,0:T(8,128)(2,1)S(1)}, bf16[256,768]{1,0:T(8,128)(2,1)}, u32[]{:S(2)}) copy-start(bf16[256,768]{1,0:T(8,128)(2,1)} %get-tuple-element.406) | copy-start | bytes 1179652 | tf_op jit(solution)/shard_map/cond
  329.4 24.0 %copy-start.21 = (f32[1,256]{1,0:T(1,128)S(1)}, f32[1,256]{1,0:T(1,128)}, u32[]{:S(2)}) copy-start(f32[1,256]{1,0:T(1,128)} %get-tuple-element.405) | copy-start | bytes 3076 | tf_op jit(solution)/shard_map/cond
  353.3 20.7 %copy-start.23 = (f32[1,3,16,256]{3,2,1,0:T(8,128)}, f32[1,3,16,256]{3,2,1,0:T(8,128)S(1)}, u32[]{:S(2)}) copy-start(f32[1,3,16,256]{3,2,1,0:T(8,128)S(1)} %get-tuple-element.1387) | copy-start | bytes 147460 | tf_op jit(solution)/shard_map/cond
  353.3 20.7 %copy-start.25 = (f32[1,3,16,256]{3,2,1,0:T(8,128)}, f32[1,3,16,256]{3,2,1,0:T(8,128)S(1)}, u32[]{:S(2)}) copy-start(f32[1,3,16,256]{3,2,1,0:T(8,128)S(1)} %get-tuple-element.1372) | copy-start | bytes 147460 | tf_op jit(solution)/shard_map/cond
  363.5 5.7 copy-start.35
  363.7 5.8 copy-start.37
  368.4 5.7 copy-start.105
  371.5 6.1 copy-start.30
  384.9 5.7 copy-start.22
  420.0 5.9 copy-start.82
  (86 other events, 210.8 us)
Sparse Core Ops, SparseCore 0:
  438.4 317.3 all-reduce.35
where the time goes:
time: 776 us; the launch traced here: 766 us
  blocking collectives  333 us (43%)
  waiting for transfers between devices  187 us (24%)
  matrix products  74.6 us (10%)
  starting transfers between devices  71.3 us (9%)
  local copies, waits for them, and re-layouts  39.1 us (5%)
  other arithmetic  28.9 us (4%)
  loops' own time  17.4 us (2%)
  between operations  14.5 us (2%)
    psum x1, waiting for transfers between devices, shards(): lax.psum((stacked[0], stacked[1], stacked[2], stacked[3], stacked[4], sta...  179 us
    psum x1, blocking collectives, shards(): lax.psum((stacked[0], stacked[1], stacked[2], stacked[3], stacked[4], sta...  137 us
    psum x4, blocking collectives, shards(): class_total = lax.psum(part_sums, 'inner')  126 us
    ppermute x5, starting transfers between devices, swapped(): return lax.ppermute(block, axis, route)  71.3 us
    all_to_all x5, blocking collectives, shards(): lax.all_to_all(payload, 'inner', split_axis=1, concat_axis=1, tiled=True)  70.3 us
    dot_general x60, matrix products, matmul_f32(): jnp.einsum('...d,de->...e', left_side, right_side.astype(jnp.bfloat16), p...  43.4 us
    dot_general x16, matrix products, temporal(): jnp.einsum('ohbyv,ohsyv->ohybs', probe_entry_lines, lookup_entry_lines, p...  19.6 us
  transfers between devices with their start and end apart: 6, of which 6 were waited for; matrix products, arithmetic and copies ran while one was open for 0% of the time, Pallas kernels for 0%

commit v1 on v0

v1 whole, which is shorter than its diff:
```python
import functools
import math

import jax
import jax.numpy as jnp
from jax import lax
from jax.experimental import pallas as pl
from jax.experimental.pallas import tpu as pltpu
from jax.sharding import PartitionSpec as P

D = 256
HEADS = 8
CLASSES = 16
PATCHES = 48
MICRO = 4
SHARP = 10.0
CAP = 15.0
NORM_EPS = 1e-05
HEAD_EPS = 1e-06
F32 = jnp.float32
BF16 = jnp.bfloat16
I32 = jnp.int32

TILES_DEV = 4
PATCH_DEV = 3
SEQS = TILES_DEV * PATCH_DEV
DATES = 16
ROWS = SEQS * 16
MEMBERS = 16
SLOT = 16
CHUNK = 72


def dot(a, b):
    return lax.dot_general(a, b, (((1,), (0,)), ((), ())), preferred_element_type=F32)


def dot_nt(a, b):
    return lax.dot_general(a, b, (((1,), (1,)), ((), ())), preferred_element_type=F32)


def dot_tn(a, b):
    return lax.dot_general(a, b, (((0,), (0,)), ((), ())), preferred_element_type=F32)


def split(x):
    hi = x.astype(BF16)
    return hi, (x - hi.astype(F32)).astype(BF16)


def rounded(x):
    return x.astype(BF16).astype(F32)


def iota(shape, axis):
    return lax.broadcasted_iota(I32, shape, axis)


def head_ones():
    same = (iota((D, D), 0) >> 5) == (iota((D, D), 1) >> 5)
    return jnp.where(same, 1.0, 0.0).astype(BF16)


def head_sums(x, ones):
    hi, lo = split(x)
    return dot(hi, ones) + dot(lo, ones)


def spread(rows_of):
    n = rows_of.shape[0]
    lane_head = iota((n, D), 1) >> 5
    zero = jnp.zeros_like(rows_of)
    return jnp.concatenate([jnp.where(lane_head == h, rows_of, zero) for h in range(HEADS)], axis=0)


def gathered_heads(wide):
    n = wide.shape[0] // HEADS
    lane_head = iota((n, D), 1) >> 5
    out = wide[:n]
    for h in range(1, HEADS):
        out = jnp.where(lane_head == h, wide[h * n : (h + 1) * n], out)
    return out


def slot_targets(shape, axis, temporal_rows):
    r = iota(shape, axis)
    group, tile, patch = r >> 4, (r >> 2) & 3, r & 3
    if temporal_rows:
        target = (tile * PATCH_DEV + patch) * 16 + group
    else:
        target = tile * PATCHES + group * PATCH_DEV + patch
    return jnp.where(patch < PATCH_DEV, target, -1)


def to_slots(temporal_rows):
    shape = (MEMBERS * SLOT, ROWS)
    hit = slot_targets(shape, 0, temporal_rows) == iota(shape, 1)
    return jnp.where(hit, 1.0, 0.0).astype(BF16)


def from_slots(temporal_rows):
    shape = (ROWS, MEMBERS * SLOT)
    hit = slot_targets(shape, 1, temporal_rows) == iota(shape, 0)
    return jnp.where(hit, 1.0, 0.0).astype(BF16)


def logits_t(k, q_wide):
    n = k.shape[0]
    k_hi, k_lo = split(k)
    q_hi, q_lo = split(q_wide)
    both = dot_nt(jnp.concatenate([k_hi, k_lo], axis=0), q_hi)
    return SHARP * (both[:n] + both[n:] + dot_nt(k_hi, q_lo))


def three_pass(x, w_hi, w_lo):
    n = x.shape[0]
    x_hi, x_lo = split(x)
    both = dot(jnp.concatenate([x_hi, x_lo], axis=0), w_hi)
    return both[:n] + both[n:] + dot(x_hi, w_lo)


def three_pass_tn(x, y):
    x_hi, x_lo = split(x)
    y_hi, y_lo = split(y)
    return dot_tn(
        jnp.concatenate([x_hi, x_hi, x_lo], axis=0), jnp.concatenate([y_hi, y_lo, y_hi], axis=0)
    )


def wide_dot_nt(x, w):
    n = x.shape[0]
    hi, lo = split(x)
    both = dot_nt(jnp.concatenate([hi, lo], axis=0), w)
    return both[:n] + both[n:]


def temporal_forward(
    counts, pix, enc, cls, gain, wqkv, wout, send, normed_o, xhat_o, k_o, kn_o, q_o, qn_o, v_o, ad_o, ac_o, att_o, rc_o
):
    ones = head_ones()
    w = wqkv[0]
    g = gain[0:1, :]
    enc_rows = enc[...]
    enc_all = jnp.concatenate(
        [enc_rows[b * 16 : b * 16 + 16] for b in range(TILES_DEV) for _ in range(PATCH_DEV)], axis=0
    )
    xd = pix[...].astype(F32) + enc_all
    xc = cls[...].astype(F32)
    x = jnp.concatenate([xd, xc], axis=0)
    inv = lax.rsqrt(jnp.mean(x * x, axis=-1, keepdims=True) + NORM_EPS)
    xhat = x * inv
    normed = (xhat * g).astype(BF16)
    xhat_o[...] = xhat
    normed_o[...] = normed
    rc_o[...] = jnp.broadcast_to(inv[ROWS:], (16, 128))
    kv = dot(normed, w[:, D:])
    q_raw = dot(normed[ROWS:], w[:, :D])
    v = kv[:, D:].astype(BF16)
    kq = jnp.concatenate([kv[:, :D], q_raw], axis=0)
    kq_inv = lax.rsqrt(head_sums(kq * kq, ones) + HEAD_EPS)
    kq_unit = kq * kq_inv
    n = ROWS + 16
    k, q = kq_unit[:n], kq_unit[n:]
    k_o[...] = k
    kn_o[...] = kq_inv[:n]
    q_o[...] = q
    qn_o[...] = kq_inv[n:]
    v_o[...] = v
    raised = jnp.exp(logits_t(k, spread(q)))
    date_at = iota((PATCHES, 128), 0) & 15
    mask = jnp.concatenate(
        [jnp.where(date_at < counts[b], 1.0, 0.0) for b in range(TILES_DEV)], axis=0
    )
    e_dates = (raised[:ROWS] * mask).reshape(SEQS, DATES, 128)
    e_class = raised[ROWS:]
    total = jnp.sum(e_dates, axis=1, keepdims=True) + jnp.sum(e_class, axis=0, keepdims=True)[None]
    a_dates = e_dates / total
    a_class = e_class[None] / total
    ad_o[...] = a_dates.reshape(ROWS, 128)
    ac_o[...] = a_class.reshape(ROWS, 128)
    v_class = v[ROWS:]
    parts = []
    for s in range(SEQS):
        weights = jnp.concatenate([a_class[s], a_dates[s]], axis=0).astype(BF16)
        values = jnp.concatenate([v_class, v[s * 16 : s * 16 + 16]], axis=0)
        parts.append(gathered_heads(dot_tn(weights, values)))
    att = jnp.concatenate(parts, axis=0).astype(BF16)
    att_o[...] = att
    updated = jnp.concatenate([xc] * SEQS, axis=0) + dot(att, wout[0])
    slots = dot(to_slots(True), updated.astype(BF16)).astype(BF16)
    send[0:16] = jnp.zeros((16, SLOT, D), BF16)
    send[16:32] = slots.reshape(16, SLOT, D)


def temporal_backward(
    first, gin, back, gain, wqkv, wout, normed_i, xhat_i, k_i, kn_i, q_i, qn_i, v_i, ad_i, ac_i, att_i, rc_i, out
):
    @pl.when(first[0] == 0)
    def _():
        out[...] = gin[...]

    @pl.when(first[0] == 1)
    def _():
        ones = head_ones()
        w = wqkv[0]
        gain_row = gain[0:1, :]
        g = dot(from_slots(True), back[...].reshape(MEMBERS * SLOT, D)).astype(BF16)
        att = att_i[...]
        d_att = dot_nt(g, wout[0]).astype(BF16)
        d_wout = dot_tn(att, g)
        v = v_i[...]
        v_class = v[ROWS:]
        a_dates = ad_i[...]
        a_class = ac_i[...]
        k = k_i[...]
        q = q_i[...]
        k_class = k[ROWS:]
        da_class, da_dates, dv_class, dv_dates = [], [], [], []
        for s in range(SEQS):
            rows = slice(s * 16, s * 16 + 16)
            wide = spread(d_att[rows])
            values = jnp.concatenate([v_class, v[rows]], axis=0)
            weights = jnp.concatenate([a_class[rows], a_dates[rows]], axis=0).astype(BF16)
            da = rounded(dot_nt(values, wide))
            dv = dot(weights, wide).astype(BF16)
            da_class.append(da[:16])
            da_dates.append(da[16:])
            dv_class.append(dv[:16])
            dv_dates.append(dv[16:])
        stack = lambda parts: jnp.concatenate(parts, axis=0)
        da_c, da_d = stack(da_class), stack(da_dates)
        tot = jnp.sum((da_c * a_class).reshape(SEQS, 16, 128), axis=1, keepdims=True) + jnp.sum(
            (da_d * a_dates).reshape(SEQS, 16, 128), axis=1, keepdims=True
        )
        ds_c = SHARP * a_class.reshape(SEQS, 16, 128) * (da_c.reshape(SEQS, 16, 128) - tot)
        ds_d = SHARP * a_dates.reshape(SEQS, 16, 128) * (da_d.reshape(SEQS, 16, 128) - tot)
        q_hi, q_lo = split(spread(q))
        ds_all = jnp.concatenate([ds_d.reshape(ROWS, 128), ds_c.reshape(ROWS, 128)], axis=0)
        dk = three_pass(ds_all, q_hi, q_lo)
        dq_parts = []
        for s in range(SEQS):
            ds_s = jnp.concatenate([ds_c[s], ds_d[s]], axis=0)
            k_s = jnp.concatenate([k_class, k[s * 16 : s * 16 + 16]], axis=0)
            dq_parts.append(gathered_heads(three_pass_tn(ds_s, k_s)))
        dq = stack(dq_parts)
        kn = kn_i[...]
        unit = jnp.concatenate([k[:ROWS]] + [k_class] * SEQS + [q] * SEQS, axis=0)
        scale = jnp.concatenate([kn[:ROWS]] + [kn[ROWS:]] * SEQS + [qn_i[...]] * SEQS, axis=0)
        d_unit = jnp.concatenate([dk, dq], axis=0)
        d_raw = scale * (d_unit - unit * head_sums(d_unit * unit, ones))
        dk_raw, dq_raw = d_raw[: 2 * ROWS], d_raw[2 * ROWS :]
        dv = jnp.concatenate([stack(dv_dates), stack(dv_class)], axis=0)
        c_v = rounded(dot_nt(dv, w[:, 2 * D :]))
        c_k = rounded(wide_dot_nt(dk_raw, w[:, D : 2 * D]))
        c_q = rounded(wide_dot_nt(dq_raw, w[:, :D]))
        dn_kv = rounded(c_v + c_k)
        dn_d = dn_kv[:ROWS]
        dn_c = jnp.sum(rounded(dn_kv[ROWS:] + c_q).reshape(SEQS, 16, D), axis=0)
        fold = lambda rows: jnp.sum(rows.reshape(SEQS, 16, D), axis=0)
        normed = normed_i[...]
        d_k = jnp.concatenate([dk_raw[:ROWS], fold(dk_raw[ROWS:])], axis=0)
        d_v = jnp.concatenate([dv[:ROWS].astype(F32), fold(dv[ROWS:].astype(F32))], axis=0)
        k_hi, k_lo = split(d_k)
        v_hi, v_lo = split(d_v)
        x_hi, x_lo = split(fold(dq_raw))
        d_wk = dot_tn(normed, k_hi) + dot_tn(normed, k_lo)
        d_wv = dot_tn(normed, v_hi) + dot_tn(normed[ROWS:], v_lo[ROWS:])
        d_wq = dot_tn(normed[ROWS:], x_hi) + dot_tn(normed[ROWS:], x_lo)
        xhat = xhat_i[...]
        xhat_c = xhat[ROWS:]
        d_gain = jnp.sum(dn_d * xhat[:ROWS], axis=0, keepdims=True) + jnp.sum(
            dn_c * xhat_c, axis=0, keepdims=True
        )
        z = dn_c * gain_row
        d_norm = rc_i[:, 0:1] * (z - xhat_c * jnp.mean(z * xhat_c, axis=-1, keepdims=True))
        d_class = fold(g.astype(F32)) + d_norm
        out[0:4, 0:64, :] = d_wq.reshape(4, 64, D)
        out[4:8, 0:64, :] = d_wk.reshape(4, 64, D)
        out[8:12, 0:64, :] = d_wv.reshape(4, 64, D)
        out[12:16, 0:64, :] = d_wout.reshape(4, 64, D)
        out[:, 64:72, :] = jnp.zeros((16, 8, D), F32)
        for i in range(16):
            out[i, 64:65, :] = d_class[i : i + 1]
        out[0, 65:66, :] = d_gain


def spatial_forward(
    arrived, gain, wqkv, wout, head, raised_o, u_o, normed_o, xhat_o, inv_o, k_o, kn_o, q_o, qn_o, v_o, a_o, att_o, log_o, hw_o
):
    ones = head_ones()
    w = wqkv[0]
    head_row = head[...]
    u = dot(from_slots(False), arrived[...].reshape(MEMBERS * SLOT, D))
    u_o[...] = u
    inv = lax.rsqrt(jnp.mean(u * u, axis=-1, keepdims=True) + NORM_EPS)
    xhat = u * inv
    normed = (xhat * gain[0:1, :]).astype(BF16)
    xhat_o[...] = xhat
    normed_o[...] = normed
    inv_o[...] = jnp.broadcast_to(inv, (ROWS, 128))
    qkv = dot(normed, w)
    v = qkv[:, 2 * D :].astype(BF16)
    kq = jnp.concatenate([qkv[:, D : 2 * D], qkv[:, :D]], axis=0)
    kq_inv = lax.rsqrt(head_sums(kq * kq, ones) + HEAD_EPS)
    kq_unit = kq * kq_inv
    k, q = kq_unit[:ROWS], kq_unit[ROWS:]
    k_o[...] = k
    q_o[...] = q
    kn_o[...] = kq_inv[:ROWS]
    qn_o[...] = kq_inv[ROWS:]
    v_o[...] = v
    parts = []
    for b in range(TILES_DEV):
        rows = slice(b * PATCHES, b * PATCHES + PATCHES)
        raised = jnp.exp(logits_t(k[rows], spread(q[rows])))
        a = raised / jnp.sum(raised, axis=0, keepdims=True)
        a_o[rows, :] = a
        parts.append(gathered_heads(dot_tn(a.astype(BF16), v[rows])))
    att = jnp.concatenate(parts, axis=0).astype(BF16)
    att_o[...] = att
    h_hi, h_mid = split(head_row)
    h_lo = (head_row - h_hi.astype(F32) - h_mid.astype(F32)).astype(BF16)
    h_rows = jnp.concatenate([h_hi, h_mid, h_lo, jnp.zeros((13, D), BF16)], axis=0)
    hw = jnp.sum(dot_nt(h_rows, wout[0]), axis=0, keepdims=True)
    hw_o[...] = hw
    raw = jnp.sum(u * head_row + att.astype(F32) * hw, axis=-1, keepdims=True)
    logit = CAP * jnp.tanh(raw / CAP)
    log_o[...] = jnp.broadcast_to(logit, (ROWS, 128))
    eye = iota((ROWS, D), 0) == iota((ROWS, D), 1)
    row = jnp.sum(jnp.where(eye, jnp.exp(logit), 0.0), axis=0, keepdims=True)
    raised_o[...] = jnp.broadcast_to(row, (16, D))


def spatial_backward(
    scal, sums, labels, gain, wqkv, wout, head, u_i, normed_i, xhat_i, inv_i, k_i, kn_i, q_i, qn_i, v_i, a_i, att_i, log_i, hw_i, send, out
):
    ones = head_ones()
    w = wqkv[0]
    head_row = head[...]
    u = u_i[...]
    att = att_i[...]
    attf = att.astype(F32)
    eye = iota((ROWS, D), 0) == iota((ROWS, D), 1)
    column = lambda row: jnp.sum(jnp.where(eye, row, 0.0), axis=-1, keepdims=True)
    total = column(jnp.sum(sums[...], axis=0, keepdims=True))
    logit = log_i[:, 0:1]
    mine = column(jnp.where(labels[...] == scal[0], 1.0, 0.0))
    d_logit = (jnp.exp(logit) / total - mine) * (1.0 / 64.0)
    ratio = logit / CAP
    d_raw_logit = d_logit * (1.0 - ratio * ratio)
    ce = mine * (jnp.log(total) - logit)
    lane = iota((1, D), 1)
    loss_row = jnp.zeros((1, D), F32)
    for b in range(TILES_DEV):
        tile_loss = jnp.sum(ce[b * PATCHES : b * PATCHES + PATCHES], axis=0, keepdims=True)
        loss_row = loss_row + jnp.where(lane == scal[1 + b], tile_loss * (1.0 / 768.0), 0.0)
    d_att = (d_raw_logit * hw_i[...]).astype(BF16)
    w_row = jnp.sum(attf * d_raw_logit, axis=0, keepdims=True)
    su_row = jnp.sum(u * d_raw_logit, axis=0, keepdims=True)
    w_hi, w_mid = split(w_row)
    w_lo = (w_row - w_hi.astype(F32) - w_mid.astype(F32)).astype(BF16)
    h_hi, h_mid = split(head_row)
    zero = jnp.zeros((12, D), BF16)
    d_wout = dot_tn(
        jnp.concatenate([w_hi, w_hi, w_mid, w_mid, zero], axis=0),
        jnp.concatenate([h_hi, h_mid, h_hi, h_mid, zero], axis=0),
    )
    w_rows = jnp.concatenate([w_hi, w_mid, w_lo, zero, zero[:1]], axis=0)
    d_head = su_row + jnp.sum(dot(w_rows, wout[0]), axis=0, keepdims=True)
    v = v_i[...]
    k = k_i[...]
    q = q_i[...]
    dv_parts, dk_parts, dq_parts = [], [], []
    for b in range(TILES_DEV):
        rows = slice(b * PATCHES, b * PATCHES + PATCHES)
        a = a_i[rows, :]
        wide = spread(d_att[rows])
        da = rounded(dot_nt(v[rows], wide))
        dv_parts.append(dot(a.astype(BF16), wide).astype(BF16))
        ds = SHARP * a * (da - jnp.sum(da * a, axis=0, keepdims=True))
        q_hi, q_lo = split(spread(q[rows]))
        dk_parts.append(three_pass(ds, q_hi, q_lo))
        dq_parts.append(gathered_heads(three_pass_tn(ds, k[rows])))
    dv = jnp.concatenate(dv_parts, axis=0)
    unit = jnp.concatenate([k, q], axis=0)
    scale = jnp.concatenate([kn_i[...], qn_i[...]], axis=0)
    d_unit = jnp.concatenate(dk_parts + dq_parts, axis=0)
    d_raw = scale * (d_unit - unit * head_sums(d_unit * unit, ones))
    dk_raw, dq_raw = d_raw[:ROWS], d_raw[ROWS:]
    c_v = rounded(dot_nt(dv, w[:, 2 * D :]))
    c_k = rounded(wide_dot_nt(dk_raw, w[:, D : 2 * D]))
    c_q = rounded(wide_dot_nt(dq_raw, w[:, :D]))
    dn = rounded(rounded(c_v + c_k) + c_q)
    normed = normed_i[...]
    q_hi, q_lo = split(dq_raw)
    k_hi, k_lo = split(dk_raw)
    xhat = xhat_i[...]
    z = dn * gain[0:1, :]
    dx = inv_i[:, 0:1] * (z - xhat * jnp.mean(z * xhat, axis=-1, keepdims=True))
    g = (d_raw_logit * head_row + dx).astype(BF16)
    send[0:16] = dot(to_slots(False), g).astype(BF16).reshape(16, SLOT, D)
    send[16:32] = jnp.zeros((16, SLOT, D), BF16)
    out[0:4, 0:64, :] = (dot_tn(normed, q_hi) + dot_tn(normed, q_lo)).reshape(4, 64, D)
    out[4:8, 0:64, :] = (dot_tn(normed, k_hi) + dot_tn(normed, k_lo)).reshape(4, 64, D)
    out[8:12, 0:64, :] = dot_tn(normed, dv).reshape(4, 64, D)
    out[12:16, 0:64, :] = d_wout.reshape(4, 64, D)
    out[:, 64:72, :] = jnp.zeros((16, 8, D), F32)
    out[0, 65:66, :] = jnp.sum(dn * xhat, axis=0, keepdims=True)
    out[1, 65:66, :] = d_head
    out[2, 65:66, :] = loss_row


def first_sum(parts, out):
    total = jnp.sum(parts[...], axis=0)
    for d in range(MEMBERS):
        out[d, 0:4, :] = total[4 * d : 4 * d + 4]
        out[d, 4:8, :] = total[64:68]


def second_sum(parts, out, small):
    total = jnp.sum(parts[...], axis=0)
    out[...] = jnp.broadcast_to(total[None], (MEMBERS, 8, D))
    small[...] = total


def assemble(blocks, other, out):
    mine = jnp.concatenate([blocks[d, 0:4, :] for d in range(MEMBERS)], axis=0)
    small = jnp.concatenate(
        [blocks[0, 4:6, :], other[4:6, :], jnp.zeros((4, D), F32)], axis=0
    )
    out[...] = jnp.broadcast_to(jnp.concatenate([mine, small], axis=0)[None], (MEMBERS, CHUNK, D))


def unpack(first, blocks, loss, d_class, d_gain, d_qkv, d_out, d_head):
    for part in range(3):
        d_qkv[0, :, part * D : part * D + D] = blocks[4 * part : 4 * part + 4, 0:64, :].reshape(D, D)
    d_out[0] = blocks[12:16, 0:64, :].reshape(D, D)
    d_gain[...] = blocks[0, 65:66, :]

    @pl.when(first[0] == 1)
    def _():
        for i in range(16):
            d_class[i : i + 1, :] = blocks[i, 64:65, :]
        d_head[...] = blocks[1, 67:68, :]
        loss[...] = blocks[2, 67:68, :]

    @pl.when(first[0] == 0)
    def _():
        for i in range(16):
            d_class[i : i + 1, :] = blocks[i, 66:67, :]
        d_head[...] = blocks[1, 65:66, :]
        loss[...] = blocks[2, 65:66, :]


VM = pl.BlockSpec(memory_space=pltpu.VMEM)
SM = pl.BlockSpec(memory_space=pltpu.SMEM)


def half(at):
    return pl.BlockSpec((16, SLOT, D), lambda *_: (at, 0, 0), memory_space=pltpu.VMEM)


def call(body, in_specs, outs, *args, name, aliases=None):
    return pl.pallas_call(
        body,
        grid=(1,),
        out_shape=[jax.ShapeDtypeStruct(s, t) for s, t in outs],
        in_specs=in_specs,
        out_specs=[VM] * len(outs),
        input_output_aliases=aliases or {},
        compiler_params=pltpu.CompilerParams(vmem_limit_bytes=48 * 1024 * 1024),
        name=name,
    )(*args)


def encodings(date_days):
    band = jnp.arange(D)
    frequency = jnp.exp((band // 2 * 2).astype(F32) * (-math.log(10000.0) / D))
    phases = date_days.astype(F32)[:, :, None] * frequency
    return jnp.where(band % 2 == 0, jnp.sin(phases), jnp.cos(phases)).reshape(TILES_DEV * 16, D)


def shards(
    pixels,
    date_days,
    clear_count,
    batch_slot,
    labels,
    class_tokens,
    section_gain,
    wqkv,
    wout,
    head_vec,
):
    first = (lax.axis_index("pipe") == 0).astype(I32)[None]
    inner = lax.axis_index("inner").astype(I32)
    head = head_vec.reshape(1, D)
    n = ROWS + 16
    saved = [
        ((n, D), BF16),
        ((n, D), F32),
        ((n, D), F32),
        ((n, D), F32),
        ((16, D), F32),
        ((16, D), F32),
        ((n, D), BF16),
        ((ROWS, 128), F32),
        ((ROWS, 128), F32),
        ((ROWS, D), BF16),
        ((16, 128), F32),
    ]
    send, *res_t = call(
        temporal_forward,
        [SM] + [VM] * 6,
        [((32, SLOT, D), BF16)] + saved,
        clear_count,
        pixels.reshape(ROWS, D),
        encodings(date_days),
        class_tokens,
        section_gain,
        wqkv,
        wout,
        name="temporal_forward",
    )
    arrived = lax.all_to_all(send, ("pipe", "inner"), 0, 0, tiled=True)
    saved = [
        ((ROWS, D), F32),
        ((ROWS, D), BF16),
        ((ROWS, D), F32),
        ((ROWS, 128), F32),
        ((ROWS, D), F32),
        ((ROWS, D), F32),
        ((ROWS, D), F32),
        ((ROWS, D), F32),
        ((ROWS, D), BF16),
        ((ROWS, HEADS * PATCHES), F32),
        ((ROWS, D), BF16),
        ((ROWS, 128), F32),
        ((1, D), F32),
    ]
    raised, *res_s = call(
        spatial_forward,
        [half(0)] + [VM] * 4,
        [((16, D), F32)] + saved,
        arrived,
        section_gain,
        wqkv,
        wout,
        head,
        name="spatial_forward",
    )
    sums = lax.all_to_all(raised, "inner", 0, 0, tiled=True)
    label_row = jnp.pad(labels.reshape(1, ROWS), ((0, 0), (0, D - ROWS)))
    back, grads = call(
        spatial_backward,
        [SM] + [VM] * (6 + len(res_s)),
        [((32, SLOT, D), BF16), ((MEMBERS, CHUNK, D), F32)],
        jnp.concatenate([inner[None], batch_slot]),
        sums,
        label_row,
        section_gain,
        wqkv,
        wout,
        head,
        *res_s,
        name="spatial_backward",
    )
    returned = lax.all_to_all(back, ("pipe", "inner"), 0, 0, tiled=True)
    (grads,) = call(
        temporal_backward,
        [SM, VM, half(1)] + [VM] * (3 + len(res_t)),
        [((MEMBERS, CHUNK, D), F32)],
        first,
        grads,
        returned,
        section_gain,
        wqkv,
        wout,
        *res_t,
        name="temporal_backward",
        aliases={1: 0},
    )
    parts = lax.all_to_all(grads, "inner", 0, 0, tiled=True)
    (parts,) = call(first_sum, [VM], [((MEMBERS, 8, D), F32)], parts, name="first_sum")
    parts = lax.all_to_all(parts, "dp", 0, 0, tiled=True)
    total, small = call(
        second_sum, [VM], [((MEMBERS, 8, D), F32), ((8, D), F32)], parts, name="second_sum"
    )
    other = lax.ppermute(small, "pipe", [(0, 1), (1, 0)])
    blocks = lax.all_to_all(total, "dp", 0, 0, tiled=True)
    (whole,) = call(assemble, [VM, VM], [((MEMBERS, CHUNK, D), F32)], blocks, other, name="assemble")
    whole = lax.all_to_all(whole, "inner", 0, 0, tiled=True)
    loss, d_class, d_gain, d_qkv, d_out, d_head = call(
        unpack,
        [SM, VM],
        [
            ((1, D), F32),
            ((16, D), F32),
            ((1, D), F32),
            ((1, D, 3 * D), F32),
            ((1, D, D), F32),
            ((1, D), F32),
        ],
        first,
        whole,
        name="unpack",
    )
    return (loss[0, :MICRO], d_class, d_gain, d_qkv, d_out, d_head.reshape(D))


def solution(mesh):
    placed = (
        P("dp", "inner", None, None),
        P("dp", None),
        P("dp"),
        P("dp"),
        P("dp", None),
        P(),
        P("pipe", None),
        P("pipe", None, None),
        P("pipe", None, None),
        P(),
    )
    return jax.shard_map(
        shards,
        mesh=mesh,
        in_specs=placed,
        out_specs=(P(), P(), P("pipe", None), P("pipe", None, None), P("pipe", None, None), P()),
        check_vma=False,
    )
```

time: 776 us -> 194 us (0.25); the launches traced: 766 us -> 192 us
  blocking collectives: 333 us -> 86.4 us
  waiting for transfers between devices: 187 us -> 34.6 us
  matrix products: 74.6 us -> 0 us
  starting transfers between devices: 71.3 us -> 28.2 us
  other arithmetic: 28.9 us -> 1.68 us
  loops' own time: 17.4 us -> 0 us
  between operations: 14.5 us -> 0.85 us
  Pallas kernels: 0 us -> 12.7 us
  local copies, waits for them, and re-layouts: 39.1 us -> 27.7 us
    psum x5 -> x0, blocking collectives: 263 us -> none  [the longest x1 137 us: shards(): lax.psum((stacked[0], stacked[1], stacked[2], stacked[3], stacked[4], sta...]
    psum x1 -> x0, waiting for transfers between devices: 179 us -> none  [shards(): lax.psum((stacked[0], stacked[1], stacked[2], stacked[3], stacked[4], sta...]
    dot_general x92 -> x0, matrix products: 74.6 us -> none  [the longest x60 43.4 us: matmul_f32(): jnp.einsum('...d,de->...e', left_side, right_side.astype(jnp.bfloat16), p...]
    ppermute x5 -> x1, starting transfers between devices: 71.3 us -> 1.92 us  [shards(): other = lax.ppermute(small, 'pipe', [(0, 1), (1, 0)])]
    all_to_all x0 -> x4, waiting for transfers between devices: none -> 31.9 us  [the longest x1 10.1 us: shards(): arrived = lax.all_to_all(send, ('pipe', 'inner'), 0, 0, tiled=True)]
    all_to_all x0 -> x4, starting transfers between devices: none -> 26.3 us  [the longest x1 13.7 us: shards(): arrived = lax.all_to_all(send, ('pipe', 'inner'), 0, 0, tiled=True)]
    unnamed x22 -> x85, local copies, waits for them, and re-layouts: 0.7 us -> 25.9 us
    another operation x11 -> x0, loops' own time: 17.4 us -> none  [the longest x1 10.3 us: shards(): totals = lax.cond(is_first, section_one_c, lambda: totals)]
  transfers between devices with their start and end apart: 6 -> 5, of which waited for: 6 -> 5; matrix products, arithmetic and copies ran while one was open for 0% -> 1% of each run, Pallas kernels for 0% -> 0%
where the time goes in v1:
time: 194 us; the launch traced here: 192 us
  blocking collectives  86.4 us (45%)
  waiting for transfers between devices  34.6 us (18%)
  starting transfers between devices  28.2 us (15%)
  local copies, waits for them, and re-layouts  27.7 us (14%)
  Pallas kernels  12.7 us (7%)
    all_to_all x1, blocking collectives, shards(): whole = lax.all_to_all(whole, 'inner', 0, 0, tiled=True)  33.7 us
    all_to_all x1, blocking collectives, shards(): parts = lax.all_to_all(grads, 'inner', 0, 0, tiled=True)  30.5 us
    unnamed x85, local copies, waits for them, and re-layouts  25.9 us
    all_to_all x1, blocking collectives, shards(): parts = lax.all_to_all(parts, 'dp', 0, 0, tiled=True)  22.2 us
    all_to_all x1, starting transfers between devices, shards(): arrived = lax.all_to_all(send, ('pipe', 'inner'), 0, 0, tiled=True)  13.7 us
    pallas_call x8, Pallas kernels, call(): pl.pallas_call(body, grid=(1,), out_shape=[jax.ShapeDtypeStruct(s, t) for...  12.7 us
    all_to_all x1, waiting for transfers between devices, shards(): arrived = lax.all_to_all(send, ('pipe', 'inner'), 0, 0, tiled=True)  10.1 us
    all_to_all x1, waiting for transfers between devices, shards(): returned = lax.all_to_all(back, ('pipe', 'inner'), 0, 0, tiled=True)  10 us
  transfers between devices with their start and end apart: 5, of which 5 were waited for; matrix products, arithmetic and copies ran while one was open for 1% of the time, Pallas kernels for 0%

profile of v1, /device:TPU:1, one launch (start us, length us, event | category | flops | bytes accessed | tf_op | source)
XLA Modules:
  0.0 192.2 jit_solution(17103279646954273607)
XLA Ops:
  1.8 1.0 copy-done
  2.8 0.9 copy-done.2
  3.7 0.9 copy-done.20
  6.6 2.8 %temporal_forward.1 = (bf16[32,16,256]{2,1,0:T(8,128)(2,1)}, bf16[208,256]{1,0:T(8,128)(2,1)S(1)}, f32[208,256]{1,0:T(8,128)S(1)}, f32[208,256]{1,0:T(8,128)S(1)...) custom-call(s32[4]{0:T(128)S(1)} %copy-done.38, ...), custom_call_target="tpu_custom_call" | custom-call | tf_op jit(solution)/shard_map/temporal_forward/pallas_call | solution.py:464
  12.0 13.7 %all-to-all-start = ((bf16[32,16,256]{2,1,0:T(8,128)(2,1)}), bf16[32,16,256]{2,1,0:T(8,128)(2,1)S(1)}, u32[]{:S(2)}, u32[]{:S(2)}) async-start(bf16[32,16,256]{2,1,0:T(8,128)(2,1)} %get-tuple-element.42), calls=%async_computation | async-start | bytes 524288 | tf_op jit(solution)/shard_map/all_to_all | solution.py:525
  25.7 10.1 %all-to-all-done.arrived = bf16[32,16,256]{2,1,0:T(8,128)(2,1)S(1)} async-done(((bf16[32,16,256]{2,1,0:T(8,128)(2,1)}), bf16[32,16,256]{2,1,0:T(8,128)(2,1)S(1)}, u32[]{:S(2)}, u32[]{:S(2)}) %all-to-all-start) | async-done | bytes 262176 | tf_op jit(solution)/shard_map/all_to_all | solution.py:525
  35.8 2.3 %spatial_forward.1 = (f32[16,256]{1,0:T(8,128)S(1)}, f32[192,256]{1,0:T(8,128)S(1)}, bf16[192,256]{1,0:T(8,128)(2,1)S(1)}, f32[192,256]{1,0:T(8,128)S(1)}, f32[1...) custom-call(bf16[32,16,256]{2,1,0:T(8,128)(2,1)S(1)} %all-to-all-don, ...), custom_call_target="tpu_custom_call" | custom-call | tf_op jit(solution)/shard_map/spatial_forward/pallas_call | solution.py:464
  43.9 5.3 %all-to-all-start.1 = ((f32[16,1,256]{2,1,0:T(1,128)}), f32[16,1,256]{2,1,0:T(1,128)S(1)}, u32[]{:S(2)}, u32[]{:S(2)}) async-start(f32[16,1,256]{2,1,0:T(1,128)} %copy.17), calls=%async_computation.1 | async-start | bytes 32768 | tf_op jit(solution)/shard_map/all_to_all | solution.py:552
  50.5 7.5 %all-to-all-done.1 = f32[16,1,256]{2,1,0:T(1,128)S(1)} async-done(((f32[16,1,256]{2,1,0:T(1,128)}), f32[16,1,256]{2,1,0:T(1,128)S(1)}, u32[]{:S(2)}, u32[]{:S(2)}) %all-to-all-start.1) | async-done | bytes 16416 | tf_op jit(solution)/shard_map/all_to_all | solution.py:552
  58.0 0.9 copy-done.5
  59.0 0.9 copy-done.7
  66.4 3.8 %spatial_backward.1 = (bf16[32,16,256]{2,1,0:T(8,128)(2,1)}, f32[16,72,256]{2,1,0:T(8,128)S(1)}) custom-call(s32[5]{0:T(128)S(1)} %copy-done.39, f32[16,256]{1,0:T(8,128)S(1)} %bitcast.12, s32[1,256]{1,0:T(1,128)S(1)} %copy-done.35, f32[1,256]{1,0:T(1,128)S(1)} %copy-done.30, bf16[1,256,768]{2,1,0:T(8,128)(2,1)S(1)} %copy-done.1, ...), custom_call_target="tpu_custom_call" | custom-call | tf_op jit(solution)/shard_map/spatial_backward/pallas_call | solution.py:464
  70.2 3.9 %all-to-all-start.2 = ((bf16[32,16,256]{2,1,0:T(8,128)(2,1)}), bf16[32,16,256]{2,1,0:T(8,128)(2,1)S(1)}, u32[]{:S(2)}, u32[]{:S(2)}) async-start(bf16[32,16,256]{2,1,0:T(8,128)(2,1)} %get-tuple-element.58), calls=%async_computation.2 | async-start | bytes 524288 | tf_op jit(solution)/shard_map/all_to_all | solution.py:568
  74.1 10.0 %all-to-all-done.2.back = bf16[32,16,256]{2,1,0:T(8,128)(2,1)S(1)} async-done(((bf16[32,16,256]{2,1,0:T(8,128)(2,1)}), bf16[32,16,256]{2,1,0:T(8,128)(2,1)S(1)}, u32[]{:S(2)}, u32[]{:S(2)}) %all-to-all-start.2) | async-done | bytes 262176 | tf_op jit(solution)/shard_map/all_to_all | solution.py:568
  84.1 0.9 copy-done.9
  89.1 2.0 %temporal_backward.1 = f32[16,72,256]{2,1,0:T(8,128)S(1)} custom-call(s32[1]{0:T(128)} %bitcast.first, f32[16,72,256]{2,1,0:T(8,128)S(1)} %get-tuple-element.57.gin, bf16[32,16,256]{2,1,0:T(8,128)(2,1)S(1)} %all-to-all-done.2.back, f32[1,256]{1,0:T(1,128)S(1)} %copy-done.30, bf16[1,256,768]{2,1,0:T(8,128)(2,1)S(1)} %copy-done.1, ...), custom_call_target="tpu_custom_call", output_to_operand_aliasing={{}: (1, {})} | custom-call | tf_op jit(solution)/shard_map/temporal_backward/pallas_call | solution.py:464
  91.0 30.5 %all_to_all.41.parts = f32[16,72,256]{2,1,0:T(8,128)S(1)} all-to-all(f32[16,72,256]{2,1,0:T(8,128)S(1)} %temporal_backward.1), channel_id=1, replica_groups=mesh['pipe'=2,'dp'=16,'inner'=16] {'inner'}, dimensions={0} | all-to-all | bytes 2359296 | tf_op jit(solution)/shard_map/all_to_all | solution.py:583
  121.6 22.2 %all_to_all.42.parts = f32[16,8,256]{2,1,0:T(8,128)S(1)} all-to-all(f32[16,8,256]{2,1,0:T(8,128)S(1)} %first_sum.1), channel_id=1, replica_groups=mesh['pipe'=2,'dp'=16,'inner'=16] {'dp'}, dimensions={0} | all-to-all | bytes 262144 | tf_op jit(solution)/shard_map/all_to_all | solution.py:585
  144.5 3.4 %all-to-all-start.5 = ((f32[16,8,256]{2,1,0:T(8,128)}), f32[16,8,256]{2,1,0:T(8,128)S(1)}, u32[]{:S(2)}, u32[]{:S(2)}) async-start(f32[16,8,256]{2,1,0:T(8,128)} %get-tuple-element.70), calls=%async_computation.5 | async-start | bytes 262144 | tf_op jit(solution)/shard_map/all_to_all | solution.py:590
  147.9 1.9 collective-permute-start
  149.8 2.8 %collective-permute-done.other = f32[8,256]{1,0:T(8,128)S(1)} collective-permute-done((f32[8,256]{1,0:T(8,128)S(1)}, f32[8,256]{1,0:T(8,128)S(1)}, u32[]{:S(2)}, u32[]{:S(2)}) %collective-permute-start) | collective-permute-done | bytes 8224 | tf_op jit(solution)/shard_map/ppermute | solution.py:589
  152.6 4.2 %all-to-all-done.5.blocks = f32[16,8,256]{2,1,0:T(8,128)S(1)} async-done(((f32[16,8,256]{2,1,0:T(8,128)}), f32[16,8,256]{2,1,0:T(8,128)S(1)}, u32[]{:S(2)}, u32[]{:S(2)}) %all-to-all-start.5) | async-done | bytes 131104 | tf_op jit(solution)/shard_map/all_to_all | solution.py:590
  156.9 33.7 %all_to_all.43.blocks = f32[16,72,256]{2,1,0:T(8,128)S(1)} all-to-all(f32[16,72,256]{2,1,0:T(8,128)S(1)} %assemble.1), channel_id=1, replica_groups=mesh['pipe'=2,'dp'=16,'inner'=16] {'inner'}, dimensions={0} | all-to-all | bytes 2359296 | tf_op jit(solution)/shard_map/all_to_all | solution.py:592
  190.6 1.1 unpack.1
  (92 shorter events, 24.7 us)
Async XLA Ops:
  0.6 35.2 %copy-start.30 = (f32[1,256]{1,0:T(1,128)S(1)}, f32[1,256]{1,0:T(1,128)}, u32[]{:S(2)}) copy-start(f32[1,256]{1,0:T(1,128)} %gain.7) | copy-start | bytes 3076
  0.6 35.2 %copy-start.34 = (f32[256]{0:T(256)S(1)}, f32[256]{0:T(256)}, u32[]{:S(2)}) copy-start(f32[256]{0:T(256)} %param.19) | copy-start | bytes 3076
  0.7 48.5 %copy-start.41 = (s32[4]{0:T(128)S(1)}, s32[4]{0:T(128)}, u32[]{:S(2)}) copy-start(s32[4]{0:T(128)} %param.13) | copy-start | bytes 52
  0.7 49.2 %copy-start.40 = (s32[4,48]{1,0:T(4,128)S(1)}, s32[4,48]{1,0:T(4,128)}, u32[]{:S(2)}) copy-start(s32[4,48]{1,0:T(4,128)} %param.14) | copy-start | bytes 2308
  1.8 1.0 copy-start
  2.8 0.9 copy-start.2
  3.7 0.9 copy-start.20
  6.6 29.2 %copy-start.1 = (bf16[1,256,768]{2,1,0:T(8,128)(2,1)S(1)}, bf16[1,256,768]{2,1,0:T(8,128)(2,1)}, u32[]{:S(2)}) copy-start(bf16[1,256,768]{2,1,0:T(8,128)(2,1)} %wqkv.7) | copy-start | bytes 1179652
  6.6 29.2 %copy-start.3 = (bf16[1,256,256]{2,1,0:T(8,128)(2,1)S(1)}, bf16[1,256,256]{2,1,0:T(8,128)(2,1)}, u32[]{:S(2)}) copy-start(bf16[1,256,256]{2,1,0:T(8,128)(2,1)} %wout.7) | copy-start | bytes 393220
  12.0 23.8 %copy-start.27 = (f32[16,256]{1,0:T(8,128)}, f32[16,256]{1,0:T(8,128)S(1)}, u32[]{:S(2)}) copy-start(f32[16,256]{1,0:T(8,128)S(1)} %get-tuple-element.64.qn_i) | copy-start | bytes 49156
  12.0 23.8 %copy-start.32 = (f32[16,128]{1,0:T(8,128)}, f32[16,128]{1,0:T(8,128)S(1)}, u32[]{:S(2)}) copy-start(f32[16,128]{1,0:T(8,128)S(1)} %get-tuple-element.69.rc_i) | copy-start | bytes 24580
  12.0 23.8 %all-to-all-start = ((bf16[32,16,256]{2,1,0:T(8,128)(2,1)}), bf16[32,16,256]{2,1,0:T(8,128)(2,1)S(1)}, u32[]{:S(2)}, u32[]{:S(2)}) async-start(bf16[32,16,256]{2,1,0:T(8,128)(2,1)} %get-tuple-element.42), calls=%async_computation | async-start | bytes 524288 | tf_op jit(solution)/shard_map/all_to_all | solution.py:525
  43.9 14.1 %all-to-all-start.1 = ((f32[16,1,256]{2,1,0:T(1,128)}), f32[16,1,256]{2,1,0:T(1,128)S(1)}, u32[]{:S(2)}, u32[]{:S(2)}) async-start(f32[16,1,256]{2,1,0:T(1,128)} %copy.17), calls=%async_computation.1 | async-start | bytes 32768 | tf_op jit(solution)/shard_map/all_to_all | solution.py:552
  58.0 0.9 copy-start.5
  59.0 0.9 copy-start.7
  59.9 0.9 copy-start.11
  60.8 0.9 copy-start.13
  61.7 0.9 copy-start.15
  63.5 0.9 copy-start.19
  70.2 13.9 %all-to-all-start.2 = ((bf16[32,16,256]{2,1,0:T(8,128)(2,1)}), bf16[32,16,256]{2,1,0:T(8,128)(2,1)S(1)}, u32[]{:S(2)}, u32[]{:S(2)}) async-start(bf16[32,16,256]{2,1,0:T(8,128)(2,1)} %get-tuple-element.58), calls=%async_computation.2 | async-start | bytes 524288 | tf_op jit(solution)/shard_map/all_to_all | solution.py:568
  84.1 0.9 copy-start.9
  85.0 0.9 copy-start.22
  144.5 12.3 %all-to-all-start.5 = ((f32[16,8,256]{2,1,0:T(8,128)}), f32[16,8,256]{2,1,0:T(8,128)S(1)}, u32[]{:S(2)}, u32[]{:S(2)}) async-start(f32[16,8,256]{2,1,0:T(8,128)} %get-tuple-element.70), calls=%async_computation.5 | async-start | bytes 262144 | tf_op jit(solution)/shard_map/all_to_all | solution.py:590
  147.9 4.7 %collective-permute-start = (f32[8,256]{1,0:T(8,128)S(1)}, f32[8,256]{1,0:T(8,128)S(1)}, u32[]{:S(2)}, u32[]{:S(2)}) collective-permute-start(f32[8,256]{1,0:T(8,128)S(1)} %get-tuple-element.71), channel_id=1, source_target_pairs={{0,256},{256,0},{1,257},{257,1},{2,258},{258,2},{3,259},{259,3},{4... | collective-permute-start | bytes 24584 | tf_op jit(solution)/shard_map/ppermute | solution.py:589
  (23 other events, 15.8 us)

commit v2 on v0

v2 whole, which is shorter than its diff:
```python
import functools
import math

import jax
import jax.numpy as jnp
from jax import lax
from jax.experimental import pallas as pl
from jax.experimental.pallas import tpu as pltpu
from jax.sharding import PartitionSpec as P

D = 256
HEADS = 8
CLASSES = 16
PATCHES = 48
MICRO = 4
SHARP = 10.0
CAP = 15.0
NORM_EPS = 1e-05
HEAD_EPS = 1e-06
F32 = jnp.float32
BF16 = jnp.bfloat16
I32 = jnp.int32

TILES_DEV = 4
DATES = 16
CHUNKS = 4
SEQS = PATCHES // CHUNKS
CLASS_CHUNK = CLASSES // CHUNKS
ROWS = SEQS * 16
ALL = CHUNKS * ROWS
MEMBERS = 16
SHARE = 4
CHUNK = 72


def dot(a, b):
    return lax.dot_general(a, b, (((1,), (0,)), ((), ())), preferred_element_type=F32)


def dot_nt(a, b):
    return lax.dot_general(a, b, (((1,), (1,)), ((), ())), preferred_element_type=F32)


def dot_tn(a, b):
    return lax.dot_general(a, b, (((0,), (0,)), ((), ())), preferred_element_type=F32)


def split(x):
    hi = x.astype(BF16)
    return hi, (x - hi.astype(F32)).astype(BF16)


def rounded(x):
    return x.astype(BF16).astype(F32)


def iota(shape, axis):
    return lax.broadcasted_iota(I32, shape, axis)


def head_ones():
    same = (iota((D, D), 0) >> 5) == (iota((D, D), 1) >> 5)
    return jnp.where(same, 1.0, 0.0).astype(BF16)


def head_sums(x, ones):
    hi, lo = split(x)
    return dot(hi, ones) + dot(lo, ones)


def spread(rows_of):
    n = rows_of.shape[0]
    lane_head = iota((n, D), 1) >> 5
    zero = jnp.zeros_like(rows_of)
    return jnp.concatenate([jnp.where(lane_head == h, rows_of, zero) for h in range(HEADS)], axis=0)


def gathered_heads(wide):
    n = wide.shape[0] // HEADS
    lane_head = iota((n, D), 1) >> 5
    out = wide[:n]
    for h in range(1, HEADS):
        out = jnp.where(lane_head == h, wide[h * n : (h + 1) * n], out)
    return out


def logits_t(k, q_wide):
    n = k.shape[0]
    k_hi, k_lo = split(k)
    q_hi, q_lo = split(q_wide)
    both = dot_nt(jnp.concatenate([k_hi, k_lo], axis=0), q_hi)
    return SHARP * (both[:n] + both[n:] + dot_nt(k_hi, q_lo))


def three_pass(x, w_hi, w_lo):
    n = x.shape[0]
    x_hi, x_lo = split(x)
    both = dot(jnp.concatenate([x_hi, x_lo], axis=0), w_hi)
    return both[:n] + both[n:] + dot(x_hi, w_lo)


def three_pass_tn(x, y):
    x_hi, x_lo = split(x)
    y_hi, y_lo = split(y)
    return dot_tn(
        jnp.concatenate([x_hi, x_hi, x_lo], axis=0), jnp.concatenate([y_hi, y_lo, y_hi], axis=0)
    )


def wide_dot_nt(x, w):
    n = x.shape[0]
    hi, lo = split(x)
    both = dot_nt(jnp.concatenate([hi, lo], axis=0), w)
    return both[:n] + both[n:]


def stack(parts):
    return jnp.concatenate(parts, axis=0)


def fold(rows):
    return jnp.sum(rows.reshape(-1, 16, D), axis=0)


def chunk_rows(c):
    return pl.ds(pl.multiple_of(c * ROWS, ROWS), ROWS)


def step(
    scal, counts, slots, labels, pix, enc, cls, gain_a, gain_b, wqkv_a, wqkv_b, wout_a, wout_b, head, out, *scratch
):
    (wt, ws, ot, os, seq_a, seq_b, xhat_t, normed_t, k_t, kn_t, v_t, ad, ac, att_t, q_t, qn_t, e_cls, inv_c,
     u_s, xhat_s, normed_s, inv_s, k_s, kn_s, q_s, qn_s, v_s, a_s, att_s, log_s, tot, rows_s, y_hi, y_lo,
     acc_q, acc_k, acc_v, acc_n, acc_g, d_cls) = scratch
    first = scal[1] == 1
    tile = scal[0] >> 2
    share = scal[0] & 3
    ones = head_ones()
    wt[...] = jnp.where(first, wqkv_a[0], wqkv_b[0])
    ws[...] = jnp.where(first, wqkv_b[0], wqkv_a[0])
    ot[...] = jnp.where(first, wout_a[0], wout_b[0])
    os[...] = jnp.where(first, wout_b[0], wout_a[0])
    gain_t = jnp.where(first, gain_a[...], gain_b[...])
    gain_s = jnp.where(first, gain_b[...], gain_a[...])
    head_row = head[...]
    h_hi, h_mid = split(head_row)
    h_lo = (head_row - h_hi.astype(F32) - h_mid.astype(F32)).astype(BF16)
    h_rows = stack([h_hi, h_mid, h_lo, jnp.zeros((13, D), BF16)])
    rows_s[...] = jnp.zeros((8, D), F32)
    rows_s[0:1, :] = jnp.sum(dot_nt(h_rows, os[...]), axis=0, keepdims=True)
    rows_s[6:7, :] = gain_t
    rows_s[7:8, :] = gain_s
    for ref in (acc_q, acc_k, acc_v, acc_n, acc_g):
        ref[...] = jnp.zeros((16, D), F32)

    xc = cls[...].astype(F32)
    inv = lax.rsqrt(jnp.mean(xc * xc, axis=-1, keepdims=True) + NORM_EPS)
    xhat_c = xc * inv
    normed_c = (xhat_c * gain_t).astype(BF16)
    qkv_c = dot(normed_c, wt[...])
    kq = stack([qkv_c[:, D : 2 * D], qkv_c[:, :D]])
    kq_inv = lax.rsqrt(head_sums(kq * kq, ones) + HEAD_EPS)
    kq_unit = kq * kq_inv
    xhat_t[ALL:, :] = xhat_c
    normed_t[ALL:, :] = normed_c
    inv_c[...] = jnp.broadcast_to(inv, (16, 128))
    k_t[ALL:, :] = kq_unit[:16]
    kn_t[ALL:, :] = kq_inv[:16]
    q_t[...] = kq_unit[16:]
    qn_t[...] = kq_inv[16:]
    v_t[ALL:, :] = qkv_c[:, 2 * D :].astype(BF16)
    e_cls[...] = jnp.exp(logits_t(kq_unit[:16], spread(kq_unit[16:])))

    @pl.loop(0, CHUNKS)
    def _(c):
        rows = chunk_rows(c)
        tile_enc = enc[pl.ds(pl.multiple_of(tile * 16, 16), 16), :]
        pixel = pix[pl.ds(c * 4, 4), :, :].astype(F32).reshape(SEQS, 16, D)
        x = (pixel + tile_enc[None]).reshape(ROWS, D)
        inv = lax.rsqrt(jnp.mean(x * x, axis=-1, keepdims=True) + NORM_EPS)
        xhat = x * inv
        normed = (xhat * rows_s[6:7, :]).astype(BF16)
        xhat_t[rows, :] = xhat
        normed_t[rows, :] = normed
        kv = dot(normed, wt[:, D:])
        v = kv[:, D:].astype(BF16)
        v_t[rows, :] = v
        k = kv[:, :D]
        k_inv = lax.rsqrt(head_sums(k * k, head_ones()) + HEAD_EPS)
        k = k * k_inv
        k_t[rows, :] = k
        kn_t[rows, :] = k_inv
        raised = jnp.exp(logits_t(k, spread(q_t[...])))
        shown = (iota((ROWS, 128), 0) & 15) < counts[tile]
        e_dates = jnp.where(shown, raised, 0.0).reshape(SEQS, DATES, 128)
        e_class = e_cls[...]
        total = jnp.sum(e_dates, axis=1, keepdims=True) + jnp.sum(e_class, axis=0, keepdims=True)[None]
        a_dates = e_dates / total
        a_class = e_class[None] / total
        ad[rows, :] = a_dates.reshape(ROWS, 128)
        ac[rows, :] = a_class.reshape(ROWS, 128)
        v_class = v_t[ALL:, :]
        parts = []
        for s in range(SEQS):
            weights = stack([a_class[s], a_dates[s]]).astype(BF16)
            values = stack([v_class, v[s * 16 : s * 16 + 16]])
            parts.append(gathered_heads(dot_tn(weights, values)))
        att = stack(parts).astype(BF16)
        att_t[rows, :] = att
        updated = rounded(stack([cls[...].astype(F32)] * SEQS) + dot(att, ot[...]))
        seq_a[rows, :] = updated[:, :128]
        seq_b[rows, :] = updated[:, 128:]

    for i in range(CLASSES):
        u_s[i * PATCHES : (i + 1) * PATCHES, :128] = seq_a[pl.ds(i, PATCHES, stride=16), :]
        u_s[i * PATCHES : (i + 1) * PATCHES, 128:] = seq_b[pl.ds(i, PATCHES, stride=16), :]

    @pl.loop(0, CHUNKS)
    def _(c):
        rows = chunk_rows(c)
        u = u_s[rows, :]
        inv = lax.rsqrt(jnp.mean(u * u, axis=-1, keepdims=True) + NORM_EPS)
        xhat = u * inv
        normed = (xhat * rows_s[7:8, :]).astype(BF16)
        xhat_s[rows, :] = xhat
        normed_s[rows, :] = normed
        inv_s[rows, :] = jnp.broadcast_to(inv, (ROWS, 128))
        qkv = dot(normed, ws[...])
        v = qkv[:, 2 * D :].astype(BF16)
        kq = stack([qkv[:, D : 2 * D], qkv[:, :D]])
        kq_inv = lax.rsqrt(head_sums(kq * kq, head_ones()) + HEAD_EPS)
        kq_unit = kq * kq_inv
        k, q = kq_unit[:ROWS], kq_unit[ROWS:]
        k_s[rows, :] = k
        q_s[rows, :] = q
        kn_s[rows, :] = kq_inv[:ROWS]
        qn_s[rows, :] = kq_inv[ROWS:]
        v_s[rows, :] = v
        parts, held = [], []
        for b in range(CLASS_CHUNK):
            part = slice(b * PATCHES, b * PATCHES + PATCHES)
            raised = jnp.exp(logits_t(k[part], spread(q[part])))
            a = raised / jnp.sum(raised, axis=0, keepdims=True)
            held.append(a)
            parts.append(gathered_heads(dot_tn(a.astype(BF16), v[part])))
        a_s[rows, :] = stack(held)
        att = stack(parts).astype(BF16)
        att_s[rows, :] = att
        raw = jnp.sum(u * head[...] + att.astype(F32) * rows_s[0:1, :], axis=-1, keepdims=True)
        log_s[rows, :] = jnp.broadcast_to(CAP * jnp.tanh(raw / CAP), (ROWS, 128))

    tot[...] = jnp.sum(jnp.exp(log_s[...]).reshape(CLASSES, PATCHES, 128), axis=0)

    @pl.loop(0, CHUNKS)
    def _(c):
        rows = chunk_rows(c)
        u = u_s[rows, :]
        xhat = xhat_s[rows, :]
        attf = att_s[rows, :].astype(F32)
        logit = log_s[rows, 0:1]
        total = stack([tot[:, 0:1]] * CLASS_CHUNK)
        eye = iota((PATCHES, PATCHES), 0) == iota((PATCHES, PATCHES), 1)
        label_row = labels[pl.ds(tile, 1), :].astype(F32)
        label = jnp.sum(jnp.where(eye, label_row, 0.0), axis=-1, keepdims=True)
        base = (c * CLASS_CHUNK).astype(F32)
        mine = stack([jnp.where(label == base + b, 1.0, 0.0) for b in range(CLASS_CHUNK)])
        d_logit = (jnp.exp(logit) / total - mine) * (1.0 / 64.0)
        ratio = logit / CAP
        d_raw_logit = d_logit * (1.0 - ratio * ratio)
        ce = jnp.sum(mine * (jnp.log(total) - logit), axis=0, keepdims=True) * (1.0 / 768.0)
        rows_s[5:6, :] += jnp.where(iota((1, D), 1) == slots[tile], ce, 0.0)
        rows_s[1:2, :] += jnp.sum(attf * d_raw_logit, axis=0, keepdims=True)
        rows_s[2:3, :] += jnp.sum(u * d_raw_logit, axis=0, keepdims=True)
        d_att = (d_raw_logit * rows_s[0:1, :]).astype(BF16)
        v = v_s[rows, :]
        k = k_s[rows, :]
        q = q_s[rows, :]
        a_all = a_s[rows, :]
        dv_parts, dk_parts, dq_parts = [], [], []
        for b in range(CLASS_CHUNK):
            part = slice(b * PATCHES, b * PATCHES + PATCHES)
            a = a_all[part]
            wide = spread(d_att[part])
            da = rounded(dot_nt(v[part], wide))
            dv_parts.append(dot(a.astype(BF16), wide).astype(BF16))
            ds = SHARP * a * (da - jnp.sum(da * a, axis=0, keepdims=True))
            q_hi, q_lo = split(spread(q[part]))
            dk_parts.append(three_pass(ds, q_hi, q_lo))
            dq_parts.append(gathered_heads(three_pass_tn(ds, k[part])))
        dv = stack(dv_parts)
        unit = stack([k, q])
        scale = stack([kn_s[rows, :], qn_s[rows, :]])
        d_unit = stack(dk_parts + dq_parts)
        d_raw = scale * (d_unit - unit * head_sums(d_unit * unit, head_ones()))
        dk_raw, dq_raw = d_raw[:ROWS], d_raw[ROWS:]
        c_v = rounded(dot_nt(dv, ws[:, 2 * D :]))
        c_k = rounded(wide_dot_nt(dk_raw, ws[:, D : 2 * D]))
        c_q = rounded(wide_dot_nt(dq_raw, ws[:, :D]))
        dn = rounded(rounded(c_v + c_k) + c_q)
        rows_s[4:5, :] += jnp.sum(dn * xhat, axis=0, keepdims=True)
        y = jnp.where(share == 0, dq_raw, jnp.where(share == 1, dk_raw, dv.astype(F32)))
        hi, lo = split(y)
        y_hi[rows, :] = hi
        y_lo[rows, :] = lo
        z = dn * rows_s[7:8, :]
        dx = inv_s[rows, 0:1] * (z - xhat * jnp.mean(z * xhat, axis=-1, keepdims=True))
        u_s[rows, :] = rounded(d_raw_logit * head[...] + dx)

    for i in range(CLASSES):
        seq_a[pl.ds(i, PATCHES, stride=16), :] = u_s[i * PATCHES : (i + 1) * PATCHES, :128]
        seq_b[pl.ds(i, PATCHES, stride=16), :] = u_s[i * PATCHES : (i + 1) * PATCHES, 128:]

    w_row = rows_s[1:2, :]
    w_hi, w_mid = split(w_row)
    w_lo = (w_row - w_hi.astype(F32) - w_mid.astype(F32)).astype(BF16)
    zero = jnp.zeros((12, D), BF16)
    w_rows = stack([w_hi, w_mid, w_lo, zero, zero[:1]])
    d_head = rows_s[2:3, :] + jnp.sum(dot(w_rows, os[...]), axis=0, keepdims=True)

    @pl.when(jnp.logical_and(scal[1] == 0, share < 3))
    def _():
        x = normed_s[...]
        d_w = dot_tn(x, y_hi[0:ALL, :]) + dot_tn(x, y_lo[0:ALL, :])
        out[:, 0:64, :] = d_w.reshape(SHARE, 64, D)

    @pl.when(jnp.logical_and(scal[1] == 0, share == 3))
    def _():
        d_w = dot_tn(stack([w_hi, w_hi, w_mid, w_mid, zero]), stack([h_hi, h_mid, h_hi, h_mid, zero]))
        out[:, 0:64, :] = d_w.reshape(SHARE, 64, D)

    @pl.loop(0, CHUNKS)
    def _(c):
        rows = chunk_rows(c)
        g = jnp.concatenate([seq_a[rows, :], seq_b[rows, :]], axis=1).astype(BF16)
        d_att = dot_nt(g, ot[...]).astype(BF16)
        v = v_t[rows, :]
        v_class = v_t[ALL:, :]
        k = k_t[rows, :]
        k_class = k_t[ALL:, :]
        q = q_t[...]
        a_dates = ad[rows, :]
        a_class = ac[rows, :]
        da_class, da_dates, dv_class, dv_dates = [], [], [], []
        for s in range(SEQS):
            part = slice(s * 16, s * 16 + 16)
            wide = spread(d_att[part])
            values = stack([v_class, v[part]])
            weights = stack([a_class[part], a_dates[part]]).astype(BF16)
            da = rounded(dot_nt(values, wide))
            dv = dot(weights, wide).astype(BF16)
            da_class.append(da[:16])
            da_dates.append(da[16:])
            dv_class.append(dv[:16])
            dv_dates.append(dv[16:])
        cube = lambda m: m.reshape(SEQS, 16, 128)
        da_c, da_d = stack(da_class), stack(da_dates)
        both = jnp.sum(cube(da_c * a_class), axis=1, keepdims=True) + jnp.sum(
            cube(da_d * a_dates), axis=1, keepdims=True
        )
        ds_c = SHARP * cube(a_class) * (cube(da_c) - both)
        ds_d = SHARP * cube(a_dates) * (cube(da_d) - both)
        q_hi, q_lo = split(spread(q))
        dk = three_pass(stack([ds_d.reshape(ROWS, 128), ds_c.reshape(ROWS, 128)]), q_hi, q_lo)
        dq_parts = []
        for s in range(SEQS):
            ds_s = stack([ds_c[s], ds_d[s]])
            k_all = stack([k_class, k[s * 16 : s * 16 + 16]])
            dq_parts.append(gathered_heads(three_pass_tn(ds_s, k_all)))
        unit = stack([k] + [k_class] * SEQS + [q] * SEQS)
        scale = stack([kn_t[rows, :]] + [kn_t[ALL:, :]] * SEQS + [qn_t[...]] * SEQS)
        d_unit = stack([dk] + dq_parts)
        d_raw = scale * (d_unit - unit * head_sums(d_unit * unit, head_ones()))
        dk_raw, dq_raw = d_raw[: 2 * ROWS], d_raw[2 * ROWS :]
        dv = stack(dv_dates + dv_class)
        c_v = rounded(dot_nt(dv, wt[:, 2 * D :]))
        c_k = rounded(wide_dot_nt(dk_raw, wt[:, D : 2 * D]))
        c_q = rounded(wide_dot_nt(dq_raw, wt[:, :D]))
        dn = rounded(c_v + c_k)
        rows_s[3:4, :] += jnp.sum(dn[:ROWS] * xhat_t[rows, :], axis=0, keepdims=True)
        acc_n[...] += fold(rounded(dn[ROWS:] + c_q))
        acc_g[...] += fold(g.astype(F32))
        acc_q[...] += fold(dq_raw)
        acc_k[...] += fold(dk_raw[ROWS:])
        acc_v[...] += fold(dv[ROWS:].astype(F32))
        of_dates = jnp.where(share == 1, dk_raw[:ROWS], dv[:ROWS].astype(F32))
        y = jnp.where(share == 0, 0.0, jnp.where(share == 3, g.astype(F32), of_dates))
        hi, lo = split(y)

        @pl.when(first)
        def _():
            y_hi[rows, :] = hi
            y_lo[rows, :] = lo

    dn_c = acc_n[...]
    xhat_c = xhat_t[ALL:, :]
    z = dn_c * rows_s[6:7, :]
    d_norm = inv_c[:, 0:1] * (z - xhat_c * jnp.mean(z * xhat_c, axis=-1, keepdims=True))
    d_cls[...] = acc_g[...] + d_norm
    gain_grad_t = rows_s[3:4, :] + jnp.sum(dn_c * xhat_c, axis=0, keepdims=True)
    gain_grad = jnp.where(first, gain_grad_t, rows_s[4:5, :])

    @pl.when(jnp.logical_and(first, share < 3))
    def _():
        y = jnp.where(share == 0, acc_q[...], jnp.where(share == 1, acc_k[...], acc_v[...]))
        hi, lo = split(y)
        y_hi[ALL:, :] = hi
        y_lo[ALL:, :] = lo
        x = normed_t[...]
        d_w = dot_tn(x, y_hi[...]) + dot_tn(x, y_lo[...])
        out[:, 0:64, :] = d_w.reshape(SHARE, 64, D)

    @pl.when(jnp.logical_and(first, share == 3))
    def _():
        out[:, 0:64, :] = dot_tn(att_t[...], y_hi[0:ALL, :]).reshape(SHARE, 64, D)

    out[:, 64:72, :] = jnp.zeros((SHARE, 8, D), F32)
    for b in range(SHARE):
        out[b, 64:65, :] = d_cls[pl.ds(4 * share + b, 1), :]
    out[0, 65:66, :] = jnp.where(share == 0, gain_grad, jnp.where(share == 1, d_head, rows_s[5:6, :]))


STEP_SCRATCH = [
    ((D, 3 * D), BF16), ((D, 3 * D), BF16), ((D, D), BF16), ((D, D), BF16),
    ((ALL, 128), F32), ((ALL, 128), F32), ((ALL + 16, D), F32), ((ALL + 16, D), BF16), ((ALL + 16, D), F32), ((ALL + 16, D), F32),
    ((ALL + 16, D), BF16), ((ALL, 128), F32), ((ALL, 128), F32), ((ALL, D), BF16),
    ((16, D), F32), ((16, D), F32), ((16, 128), F32), ((16, 128), F32),
    ((ALL, D), F32), ((ALL, D), F32), ((ALL, D), BF16), ((ALL, 128), F32),
    ((ALL, D), F32), ((ALL, D), F32), ((ALL, D), F32), ((ALL, D), F32), ((ALL, D), BF16),
    ((ALL, HEADS * PATCHES), F32), ((ALL, D), BF16), ((ALL, 128), F32), ((PATCHES, 128), F32), ((8, D), F32),
    ((ALL + 16, D), BF16), ((ALL + 16, D), BF16),
    ((16, D), F32), ((16, D), F32), ((16, D), F32), ((16, D), F32), ((16, D), F32), ((16, D), F32),
]


def first_sum(parts, out):
    total = jnp.sum(parts[...], axis=0)
    for d in range(MEMBERS):
        out[d, 0:4, :] = total[4 * d : 4 * d + 4]
        out[d, 4:8, :] = total[64:68]


def second_sum(parts, out):
    out[...] = jnp.broadcast_to(jnp.sum(parts[...], axis=0)[None], (MEMBERS, 8, D))


def assemble(blocks, out):
    mine = [blocks[d, 0:4, :] for d in range(MEMBERS)]
    whole = stack(mine + [blocks[0, 4:8, :], jnp.zeros((4, D), F32)])
    out[...] = jnp.broadcast_to(whole[None], (MEMBERS, CHUNK, D))


def unpack(blocks, loss, d_class, d_gain, d_qkv, d_out, d_head):
    for b in range(SHARE):
        rows = slice(64 * b, 64 * b + 64)
        for part in range(3):
            d_qkv[0, rows, part * D : part * D + D] = blocks[4 * b + part, 0:64, :]
        d_out[0, rows, :] = blocks[4 * b + 3, 0:64, :]
        for part in range(4):
            at = 4 * part + b
            d_class[at : at + 1, :] = blocks[4 * b + part, 64:65, :]
    d_gain[...] = blocks[0, 65:66, :]
    d_head[...] = blocks[1, 65:66, :]
    loss[...] = blocks[2, 65:66, :]


VM = pl.BlockSpec()
SM = pl.BlockSpec(memory_space=pltpu.SMEM)


def call(body, in_specs, outs, *args, name, scratch=()):
    return pl.pallas_call(
        body,
        out_shape=[jax.ShapeDtypeStruct(s, t) for s, t in outs],
        in_specs=in_specs,
        out_specs=[VM] * len(outs),
        scratch_shapes=[pltpu.VMEM(s, t) for s, t in scratch],
        compiler_params=pltpu.CompilerParams(vmem_limit_bytes=48 * 1024 * 1024),
        name=name,
    )(*args)


def encodings(date_days):
    band = jnp.arange(D)
    frequency = jnp.exp((band // 2 * 2).astype(F32) * (-math.log(10000.0) / D))
    phases = date_days.astype(F32)[:, :, None] * frequency
    return jnp.where(band % 2 == 0, jnp.sin(phases), jnp.cos(phases)).reshape(TILES_DEV * 16, D)


def shards(
    pixels,
    date_days,
    clear_count,
    batch_slot,
    labels,
    class_tokens,
    section_gain,
    wqkv,
    wout,
    head_vec,
):
    first = (lax.axis_index("pipe") == 0).astype(I32)
    inner = lax.axis_index("inner").astype(I32)
    swap = lambda v: lax.ppermute(v, "pipe", [(0, 1), (1, 0)])
    by_dest = jnp.repeat(pixels.reshape(TILES_DEV, PATCHES, D), SHARE, axis=0)
    whole_tile = lax.all_to_all(by_dest, "inner", 0, 0, tiled=True)
    (grads,) = call(
        step,
        [SM] * 3 + [VM] * 11,
        [((SHARE, CHUNK, D), F32)],
        jnp.stack([inner, first]),
        clear_count,
        batch_slot,
        labels,
        whole_tile,
        encodings(date_days),
        class_tokens,
        section_gain,
        swap(section_gain),
        wqkv,
        swap(wqkv),
        wout,
        swap(wout),
        head_vec.reshape(1, D),
        name="step",
        scratch=STEP_SCRATCH,
    )
    sharers = [[SHARE * b + s for b in range(TILES_DEV)] for s in range(SHARE)]
    parts = lax.all_to_all(grads, "inner", 0, 0, tiled=True, axis_index_groups=sharers)
    (parts,) = call(first_sum, [VM], [((MEMBERS, 8, D), F32)], parts, name="first_sum")
    parts = lax.all_to_all(parts, "dp", 0, 0, tiled=True)
    (total,) = call(second_sum, [VM], [((MEMBERS, 8, D), F32)], parts, name="second_sum")
    blocks = lax.all_to_all(total, "dp", 0, 0, tiled=True)
    (whole,) = call(assemble, [VM], [((MEMBERS, CHUNK, D), F32)], blocks, name="assemble")
    whole = lax.all_to_all(whole, "inner", 0, 0, tiled=True)
    loss, d_class, d_gain, d_qkv, d_out, d_head = call(
        unpack,
        [VM],
        [
            ((1, D), F32),
            ((16, D), F32),
            ((1, D), F32),
            ((1, D, 3 * D), F32),
            ((1, D, D), F32),
            ((1, D), F32),
        ],
        whole,
        name="unpack",
    )
    return (loss[0, :MICRO], d_class, d_gain, d_qkv, d_out, d_head.reshape(D))


def solution(mesh):
    placed = (
        P("dp", "inner", None, None),
        P("dp", None),
        P("dp"),
        P("dp"),
        P("dp", None),
        P(),
        P("pipe", None),
        P("pipe", None, None),
        P("pipe", None, None),
        P(),
    )
    return jax.shard_map(
        shards,
        mesh=mesh,
        in_specs=placed,
        out_specs=(P(), P(), P("pipe", None), P("pipe", None, None), P("pipe", None, None), P()),
        check_vma=False,
    )
```

time: 776 us -> 154 us (0.20); the launches traced: 766 us -> 153 us
  blocking collectives: 333 us -> 84.6 us
  waiting for transfers between devices: 187 us -> 11.6 us
  matrix products: 74.6 us -> 0 us
  starting transfers between devices: 71.3 us -> 20.9 us
  local copies, waits for them, and re-layouts: 39.1 us -> 2.36 us
  Pallas kernels: 0 us -> 32 us
  other arithmetic: 28.9 us -> 0.41 us
  loops' own time: 17.4 us -> 0 us
  between operations: 14.5 us -> 0.85 us
    psum x5 -> x0, blocking collectives: 263 us -> none  [the longest x1 137 us: shards(): lax.psum((stacked[0], stacked[1], stacked[2], stacked[3], stacked[4], sta...]
    psum x1 -> x0, waiting for transfers between devices: 179 us -> none  [shards(): lax.psum((stacked[0], stacked[1], stacked[2], stacked[3], stacked[4], sta...]
    dot_general x92 -> x0, matrix products: 74.6 us -> none  [the longest x60 43.4 us: matmul_f32(): jnp.einsum('...d,de->...e', left_side, right_side.astype(jnp.bfloat16), p...]
    ppermute x5 -> x3, starting transfers between devices: 71.3 us -> 7.5 us  [shards(): swap = lambda v: lax.ppermute(v, 'pipe', [(0, 1), (1, 0)])]
    pallas_call x0 -> x5, Pallas kernels: none -> 32 us  [call(): pl.pallas_call(body, out_shape=[jax.ShapeDtypeStruct(s, t) for s, t in ou...]
    another operation x11 -> x0, loops' own time: 17.4 us -> none  [the longest x1 10.3 us: shards(): totals = lax.cond(is_first, section_one_c, lambda: totals)]
    all_to_all x5 -> x4, blocking collectives: 70.3 us -> 84.6 us  [the longest x1 35.8 us: shards(): whole = lax.all_to_all(whole, 'inner', 0, 0, tiled=True)]
    all_to_all x0 -> x1, starting transfers between devices: none -> 13.4 us  [shards(): whole_tile = lax.all_to_all(by_dest, 'inner', 0, 0, tiled=True)]
  transfers between devices with their start and end apart: 6 -> 4, of which waited for: 6 -> 2; matrix products, arithmetic and copies ran while one was open for 0% -> 0% of each run, Pallas kernels for 0% -> 0%
where the time goes in v2:
time: 154 us; the launch traced here: 153 us
  blocking collectives  84.6 us (55%)
  Pallas kernels  32 us (21%)
  starting transfers between devices  20.9 us (14%)
  waiting for transfers between devices  11.6 us (8%)
  local copies, waits for them, and re-layouts  2.36 us (2%)
    all_to_all x1, blocking collectives, shards(): whole = lax.all_to_all(whole, 'inner', 0, 0, tiled=True)  35.8 us
    pallas_call x5, Pallas kernels, call(): pl.pallas_call(body, out_shape=[jax.ShapeDtypeStruct(s, t) for s, t in ou...  32 us
    all_to_all x1, blocking collectives, shards(): lax.all_to_all(grads, 'inner', 0, 0, tiled=True, axis_index_groups=sharers)  18.7 us
    all_to_all x1, blocking collectives, shards(): parts = lax.all_to_all(parts, 'dp', 0, 0, tiled=True)  18.5 us
    all_to_all x1, starting transfers between devices, shards(): whole_tile = lax.all_to_all(by_dest, 'inner', 0, 0, tiled=True)  13.4 us
    all_to_all x1, blocking collectives, shards(): blocks = lax.all_to_all(total, 'dp', 0, 0, tiled=True)  11.6 us
    ppermute x3, waiting for transfers between devices, shards(): swap = lambda v: lax.ppermute(v, 'pipe', [(0, 1), (1, 0)])  11.6 us
    ppermute x3, starting transfers between devices, shards(): swap = lambda v: lax.ppermute(v, 'pipe', [(0, 1), (1, 0)])  7.5 us
  transfers between devices with their start and end apart: 4, of which 2 were waited for; matrix products, arithmetic and copies ran while one was open for 0% of the time, Pallas kernels for 0%

profile of v2, /device:TPU:1, one launch (start us, length us, event | category | flops | bytes accessed | tf_op | source)
XLA Modules:
  0.0 152.7 jit_solution(18430928546181335384)
XLA Ops:
  0.6 0.0 copy-start.4
  0.6 0.0 copy-start.1
  0.7 1.7 %broadcast_in_dim.9 = bf16[4,4,48,256]{3,2,1,0:T(8,128)(2,1)} broadcast(bf16[4,48,256]{2,1,0:T(8,128)(2,1)} %bitcast.9), dimensions={0,2,3} | broadcast | bytes 491520 | tf_op jit(solution)/shard_map/broadcast_in_dim | solution.py:504
  2.5 13.4 %all-to-all-start = ((bf16[16,48,256]{2,1,0:T(8,128)(2,1)}), bf16[16,48,256]{2,1,0:T(8,128)(2,1)S(1)}, u32[]{:S(2)}, u32[]{:S(2)}) async-start(bf16[16,48,256]{2,1,0:T(8,128)(2,1)} %bitcast.3), calls=%async_computation | async-start | bytes 786432 | tf_op jit(solution)/shard_map/all_to_all | solution.py:505
  15.9 2.2 %collective-permute-start = (f32[1,256]{1,0:T(1,128)S(1)}, f32[1,256]{1,0:T(1,128)S(1)}, u32[]{:S(2)}, u32[]{:S(2)}) collective-permute-start(f32[1,256]{1,0:T(1,128)S(1)} %copy-done.4), channel_id=1, source_target_pairs={{0,256},{256,0},{1,257},{257,1},{2,258},{258,2},{3,259},{259,3},{4... | collective-permute-start | bytes 3080 | tf_op jit(solution)/shard_map/ppermute | solution.py:503
  18.1 3.1 %collective-permute-start.2 = (bf16[1,256,256]{2,1,0:T(8,128)(2,1)S(1)}, bf16[1,256,256]{2,1,0:T(8,128)(2,1)S(1)}, u32[]{:S(2)}, u32[]{:S(2)}) collective-permute-start(bf16[1,256,256]{2,1,0:T(8,128)(2,1)S(1)} %copy-done.1), channel_id=1, source_target_pairs={{0,256},{256,0},{1,257},{257,1},{2,258},{258,2},{3,259},{259,3},{4... | collective-permute-start | bytes 393224 | tf_op jit(solution)/shard_map/ppermute | solution.py:503
  21.2 2.2 %collective-permute-start.1 = (bf16[1,256,768]{2,1,0:T(8,128)(2,1)S(1)}, bf16[1,256,768]{2,1,0:T(8,128)(2,1)S(1)}, u32[]{:S(2)}, u32[]{:S(2)}) collective-permute-start(bf16[1,256,768]{2,1,0:T(8,128)(2,1)S(1)} %copy-done), channel_id=1, source_target_pairs={{0,256},{256,0},{1,257},{257,1},{2,258},{258,2},{3,259},{259,3},{4... | collective-permute-start | bytes 1179656 | tf_op jit(solution)/shard_map/ppermute | solution.py:503
  23.5 0.0 copy-done.8
  23.5 0.1 mul.34
  23.6 0.3 fusion.enc
  23.9 0.1 pad_add_fusion.scal
  24.0 0.0 collective-permute-done.gain_b
  24.0 2.6 %collective-permute-done.2.wout_b = bf16[1,256,256]{2,1,0:T(8,128)(2,1)S(1)} collective-permute-done((bf16[1,256,256]{2,1,0:T(8,128)(2,1)S(1)}, bf16[1,256,256]{2,1,0:T(8,128)(2,1)S(1)}, u32[]{:S(2)}, u32[]{:S(2)}) %collective-permute-start.2) | collective-permute-done | bytes 131104 | tf_op jit(solution)/shard_map/ppermute | solution.py:503
  26.6 9.0 %collective-permute-done.1.wqkv_b = bf16[1,256,768]{2,1,0:T(8,128)(2,1)S(1)} collective-permute-done((bf16[1,256,768]{2,1,0:T(8,128)(2,1)S(1)}, bf16[1,256,768]{2,1,0:T(8,128)(2,1)S(1)}, u32[]{:S(2)}, u32[]{:S(2)}) %collective-permute-start.1) | collective-permute-done | bytes 393248 | tf_op jit(solution)/shard_map/ppermute | solution.py:503
  35.5 0.0 all-to-all-done.pix
  35.5 0.0 copy-done.5
  35.6 30.8 %step.1 = f32[4,72,256]{2,1,0:T(8,128)S(1)} custom-call(s32[2]{0:T(128)S(1)} %pad_add_fusion.scal, s32[4]{0:T(128)S(1)} %copy-done.6, s32[4]{0:T(128)S(1)} %copy-done.7, s32[4,48]{1,0:T(4,128)S(1)} %copy-done.3, bf16[16,48,256]{2,1,0:T(8,128)(2,1)S(1)} %all-to-all-done.pix, f32[64,256]{1,0:T(8,128)S(1)} %fusion.enc, bf16[16,256]{1,0:T(8,128)(2,1)S(1)} %copy-done.2, ...), custom_call_target="tpu_custom_call" | custom-call | tf_op jit(solution)/shard_map/step/pallas_call | solution.py:471
  66.4 18.7 %all_to_all.25.parts = f32[4,72,256]{2,1,0:T(8,128)S(1)} all-to-all(f32[4,72,256]{2,1,0:T(8,128)S(1)} %step.1), channel_id=1, replica_groups={{0,4,8,12},{1,5,9,13},{2,6,10,14},{3,7,11,15},{16,20,24,28},{17,21,25,2..., dimensions={0} | all-to-all | bytes 589824 | tf_op jit(solution)/shard_map/all_to_all | solution.py:528
  85.1 18.5 %all_to_all.26.parts = f32[16,8,256]{2,1,0:T(8,128)S(1)} all-to-all(f32[16,8,256]{2,1,0:T(8,128)S(1)} %first_sum.1), channel_id=1, replica_groups=mesh['pipe'=2,'dp'=16,'inner'=16] {'dp'}, dimensions={0} | all-to-all | bytes 262144 | tf_op jit(solution)/shard_map/all_to_all | solution.py:530
  103.7 11.6 %all_to_all.27.blocks = f32[16,8,256]{2,1,0:T(8,128)S(1)} all-to-all(f32[16,8,256]{2,1,0:T(8,128)S(1)} %second_sum.1), channel_id=1, replica_groups=mesh['pipe'=2,'dp'=16,'inner'=16] {'dp'}, dimensions={0} | all-to-all | bytes 262144 | tf_op jit(solution)/shard_map/all_to_all | solution.py:532
  115.2 0.1 assemble.1
  115.3 35.8 %all_to_all.28.blocks = f32[16,72,256]{2,1,0:T(8,128)S(1)} all-to-all(f32[16,72,256]{2,1,0:T(8,128)S(1)} %assemble.1), channel_id=1, replica_groups=mesh['pipe'=2,'dp'=16,'inner'=16] {'inner'}, dimensions={0} | all-to-all | bytes 2359296 | tf_op jit(solution)/shard_map/all_to_all | solution.py:534
  151.1 1.1 unpack.1
  152.2 0.5 slice_bitcast_fusion
  (19 shorter events, 0.1 us)
Async XLA Ops:
  0.6 15.3 %copy-start.4 = (f32[1,256]{1,0:T(1,128)S(1)}, f32[1,256]{1,0:T(1,128)}, u32[]{:S(2)}) copy-start(f32[1,256]{1,0:T(1,128)} %gain_a.1) | copy-start | bytes 3076
  0.6 17.5 %copy-start.1 = (bf16[1,256,256]{2,1,0:T(8,128)(2,1)S(1)}, bf16[1,256,256]{2,1,0:T(8,128)(2,1)}, u32[]{:S(2)}) copy-start(bf16[1,256,256]{2,1,0:T(8,128)(2,1)} %wout_a.1) | copy-start | bytes 393220
  0.7 20.5 %copy-start = (bf16[1,256,768]{2,1,0:T(8,128)(2,1)S(1)}, bf16[1,256,768]{2,1,0:T(8,128)(2,1)}, u32[]{:S(2)}) copy-start(bf16[1,256,768]{2,1,0:T(8,128)(2,1)} %wqkv_a.1) | copy-start | bytes 1179652
  0.7 22.8 %copy-start.8 = (s32[4,16]{1,0:T(4,128)S(1)}, s32[4,16]{1,0:T(4,128)}, u32[]{:S(2)}) copy-start(s32[4,16]{1,0:T(4,128)} %param.11) | copy-start | bytes 772
  0.7 34.9 %copy-start.5 = (f32[256]{0:T(256)S(1)}, f32[256]{0:T(256)}, u32[]{:S(2)}) copy-start(f32[256]{0:T(256)} %param.19) | copy-start | bytes 3076
  0.7 34.9 %copy-start.2 = (bf16[16,256]{1,0:T(8,128)(2,1)S(1)}, bf16[16,256]{1,0:T(8,128)(2,1)}, u32[]{:S(2)}) copy-start(bf16[16,256]{1,0:T(8,128)(2,1)} %cls.1) | copy-start | bytes 24580
  0.7 34.8 %copy-start.3 = (s32[4,48]{1,0:T(4,128)S(1)}, s32[4,48]{1,0:T(4,128)}, u32[]{:S(2)}) copy-start(s32[4,48]{1,0:T(4,128)} %labels.1) | copy-start | bytes 2308
  0.7 34.8 %copy-start.7 = (s32[4]{0:T(128)S(1)}, s32[4]{0:T(128)}, u32[]{:S(2)}) copy-start(s32[4]{0:T(128)} %slots.1) | copy-start | bytes 52
  0.7 34.8 %copy-start.6 = (s32[4]{0:T(128)S(1)}, s32[4]{0:T(128)}, u32[]{:S(2)}) copy-start(s32[4]{0:T(128)} %counts.1) | copy-start | bytes 52
  2.5 33.1 %all-to-all-start = ((bf16[16,48,256]{2,1,0:T(8,128)(2,1)}), bf16[16,48,256]{2,1,0:T(8,128)(2,1)S(1)}, u32[]{:S(2)}, u32[]{:S(2)}) async-start(bf16[16,48,256]{2,1,0:T(8,128)(2,1)} %bitcast.3), calls=%async_computation | async-start | bytes 786432 | tf_op jit(solution)/shard_map/all_to_all | solution.py:505
  15.9 8.1 %collective-permute-start = (f32[1,256]{1,0:T(1,128)S(1)}, f32[1,256]{1,0:T(1,128)S(1)}, u32[]{:S(2)}, u32[]{:S(2)}) collective-permute-start(f32[1,256]{1,0:T(1,128)S(1)} %copy-done.4), channel_id=1, source_target_pairs={{0,256},{256,0},{1,257},{257,1},{2,258},{258,2},{3,259},{259,3},{4... | collective-permute-start | bytes 3080 | tf_op jit(solution)/shard_map/ppermute | solution.py:503
  18.1 8.4 %collective-permute-start.2 = (bf16[1,256,256]{2,1,0:T(8,128)(2,1)S(1)}, bf16[1,256,256]{2,1,0:T(8,128)(2,1)S(1)}, u32[]{:S(2)}, u32[]{:S(2)}) collective-permute-start(bf16[1,256,256]{2,1,0:T(8,128)(2,1)S(1)} %copy-done.1), channel_id=1, source_target_pairs={{0,256},{256,0},{1,257},{257,1},{2,258},{258,2},{3,259},{259,3},{4... | collective-permute-start | bytes 393224 | tf_op jit(solution)/shard_map/ppermute | solution.py:503
  21.2 14.3 %collective-permute-start.1 = (bf16[1,256,768]{2,1,0:T(8,128)(2,1)S(1)}, bf16[1,256,768]{2,1,0:T(8,128)(2,1)S(1)}, u32[]{:S(2)}, u32[]{:S(2)}) collective-permute-start(bf16[1,256,768]{2,1,0:T(8,128)(2,1)S(1)} %copy-done), channel_id=1, source_target_pairs={{0,256},{256,0},{1,257},{257,1},{2,258},{258,2},{3,259},{259,3},{4... | collective-permute-start | bytes 1179656 | tf_op jit(solution)/shard_map/ppermute | solution.py:503

commit v3 on v2

--- a/solution.py
+++ b/solution.py
@@ -1,4 +1,3 @@
-import functools
 import math
 
 import jax
@@ -6,7 +5,8 @@
 from jax import lax
 from jax.experimental import pallas as pl
 from jax.experimental.pallas import tpu as pltpu
-from jax.sharding import PartitionSpec as P
+from jax.sharding import Mesh, PartitionSpec as P
+
 
 D = 256
 HEADS = 8
@@ -30,7 +30,11 @@
 ALL = CHUNKS * ROWS
 MEMBERS = 16
 SHARE = 4
+YS = 8
+OWNERS = 64
 CHUNK = 72
+DP = ("y", "core")
+INNER = ("b", "r")
 
 
 def dot(a, b):
@@ -124,6 +128,12 @@
 
 def chunk_rows(c):
     return pl.ds(pl.multiple_of(c * ROWS, ROWS), ROWS)
+
+
+def put_tiles(out, d_w):
+    for n in range(OWNERS):
+        row, lane = 8 * (n // 2), 128 * (n % 2)
+        out[n, 0:8, :] = d_w[row : row + 8, lane : lane + 128]
 
 
 def step(
@@ -321,12 +331,12 @@
     def _():
         x = normed_s[...]
         d_w = dot_tn(x, y_hi[0:ALL, :]) + dot_tn(x, y_lo[0:ALL, :])
-        out[:, 0:64, :] = d_w.reshape(SHARE, 64, D)
+        put_tiles(out, d_w)
 
     @pl.when(jnp.logical_and(scal[1] == 0, share == 3))
     def _():
         d_w = dot_tn(stack([w_hi, w_hi, w_mid, w_mid, zero]), stack([h_hi, h_mid, h_hi, h_mid, zero]))
-        out[:, 0:64, :] = d_w.reshape(SHARE, 64, D)
+        put_tiles(out, d_w)
 
     @pl.loop(0, CHUNKS)
     def _(c):
@@ -407,16 +417,18 @@
         y_lo[ALL:, :] = lo
         x = normed_t[...]
         d_w = dot_tn(x, y_hi[...]) + dot_tn(x, y_lo[...])
-        out[:, 0:64, :] = d_w.reshape(SHARE, 64, D)
+        put_tiles(out, d_w)
 
     @pl.when(jnp.logical_and(first, share == 3))
     def _():
-        out[:, 0:64, :] = dot_tn(att_t[...], y_hi[0:ALL, :]).reshape(SHARE, 64, D)
-
-    out[:, 64:72, :] = jnp.zeros((SHARE, 8, D), F32)
+        put_tiles(out, dot_tn(att_t[...], y_hi[0:ALL, :]))
+
+    misc = jnp.where(share == 0, gain_grad, jnp.where(share == 1, d_head, rows_s[5:6, :]))
     for b in range(SHARE):
-        out[b, 64:65, :] = d_cls[pl.ds(4 * share + b, 1), :]
-    out[0, 65:66, :] = jnp.where(share == 0, gain_grad, jnp.where(share == 1, d_head, rows_s[5:6, :]))
+        row = d_cls[pl.ds(4 * share + b, 1), :]
+        small = stack([row[:, :128], row[:, 128:], misc[:, :128], misc[:, 128:], jnp.zeros((4, 128), F32)])
+        for d in range(MEMBERS):
+            out[SHARE * d + b, 8:16, :] = small
 
 
 STEP_SCRATCH = [
@@ -432,42 +444,44 @@
 ]
 
 
-def first_sum(parts, out):
-    total = jnp.sum(parts[...], axis=0)
-    for d in range(MEMBERS):
-        out[d, 0:4, :] = total[4 * d : 4 * d + 4]
-        out[d, 4:8, :] = total[64:68]
-
-
-def second_sum(parts, out):
-    out[...] = jnp.broadcast_to(jnp.sum(parts[...], axis=0)[None], (MEMBERS, 8, D))
+def reduce_tiles(parts, out):
+    out[...] = jnp.broadcast_to(jnp.sum(parts[...], axis=0)[None], (YS, 16, 128))
 
 
 def assemble(blocks, out):
-    mine = [blocks[d, 0:4, :] for d in range(MEMBERS)]
-    whole = stack(mine + [blocks[0, 4:8, :], jnp.zeros((4, D), F32)])
-    out[...] = jnp.broadcast_to(whole[None], (MEMBERS, CHUNK, D))
-
-
-def unpack(blocks, loss, d_class, d_gain, d_qkv, d_out, d_head):
+    whole = stack([blocks[y, 0:8, :] for y in range(YS)] + [blocks[0, 8:16, :]])
+    out[...] = jnp.broadcast_to(whole[None], (MEMBERS, CHUNK, 128))
+
+
+def unpack(core, mine, other, loss, d_class, d_gain, d_qkv, d_out, d_head):
+    lower = core[0] == 0
     for b in range(SHARE):
-        rows = slice(64 * b, 64 * b + 64)
-        for part in range(3):
-            d_qkv[0, rows, part * D : part * D + D] = blocks[4 * b + part, 0:64, :]
-        d_out[0, rows, :] = blocks[4 * b + 3, 0:64, :]
         for part in range(4):
+            own, far = mine[SHARE * b + part], other[SHARE * b + part]
+            blocks = (jnp.where(lower, own, far), jnp.where(lower, far, own))
+            for c in range(2):
+                for y in range(YS):
+                    n = (2 * y + c) * SHARE + b
+                    tile = blocks[c][8 * y : 8 * y + 8]
+                    row, lane = 8 * (n // 2), 128 * (n % 2)
+                    if part < 3:
+                        d_qkv[0, row : row + 8, part * D + lane : part * D + lane + 128] = tile
+                    else:
+                        d_out[0, row : row + 8, lane : lane + 128] = tile
             at = 4 * part + b
-            d_class[at : at + 1, :] = blocks[4 * b + part, 64:65, :]
-    d_gain[...] = blocks[0, 65:66, :]
-    d_head[...] = blocks[1, 65:66, :]
-    loss[...] = blocks[2, 65:66, :]
+            d_class[at : at + 1, :128] = own[64:65]
+            d_class[at : at + 1, 128:] = own[65:66]
+            if b == 0 and part < 3:
+                ref = (d_gain, d_head, loss)[part]
+                ref[:, :128] = own[66:67]
+                ref[:, 128:] = own[67:68]
 
 
 VM = pl.BlockSpec()
 SM = pl.BlockSpec(memory_space=pltpu.SMEM)
 
 
-def call(body, in_specs, outs, *args, name, scratch=()):
+def call(body, in_specs, outs, *args, scratch=()):
     return pl.pallas_call(
         body,
         out_shape=[jax.ShapeDtypeStruct(s, t) for s, t in outs],
@@ -475,7 +489,6 @@
         out_specs=[VM] * len(outs),
         scratch_shapes=[pltpu.VMEM(s, t) for s, t in scratch],
         compiler_params=pltpu.CompilerParams(vmem_limit_bytes=48 * 1024 * 1024),
-        name=name,
     )(*args)
 
 
@@ -486,7 +499,11 @@
     return jnp.where(band % 2 == 0, jnp.sin(phases), jnp.cos(phases)).reshape(TILES_DEV * 16, D)
 
 
-def shards(
+def swap(v):
+    return lax.ppermute(v, "pipe", [(0, 1), (1, 0)])
+
+
+def whole_step(
     pixels,
     date_days,
     clear_count,
@@ -499,14 +516,13 @@
     head_vec,
 ):
     first = (lax.axis_index("pipe") == 0).astype(I32)
-    inner = lax.axis_index("inner").astype(I32)
-    swap = lambda v: lax.ppermute(v, "pipe", [(0, 1), (1, 0)])
+    inner = lax.axis_index(INNER).astype(I32)
     by_dest = jnp.repeat(pixels.reshape(TILES_DEV, PATCHES, D), SHARE, axis=0)
-    whole_tile = lax.all_to_all(by_dest, "inner", 0, 0, tiled=True)
+    whole_tile = lax.all_to_all(by_dest, INNER, 0, 0, tiled=True)
     (grads,) = call(
         step,
         [SM] * 3 + [VM] * 11,
-        [((SHARE, CHUNK, D), F32)],
+        [((OWNERS, 16, 128), F32)],
         jnp.stack([inner, first]),
         clear_count,
         batch_slot,
@@ -521,20 +537,17 @@
         wout,
         swap(wout),
         head_vec.reshape(1, D),
-        name="step",
         scratch=STEP_SCRATCH,
     )
-    sharers = [[SHARE * b + s for b in range(TILES_DEV)] for s in range(SHARE)]
-    parts = lax.all_to_all(grads, "inner", 0, 0, tiled=True, axis_index_groups=sharers)
-    (parts,) = call(first_sum, [VM], [((MEMBERS, 8, D), F32)], parts, name="first_sum")
-    parts = lax.all_to_all(parts, "dp", 0, 0, tiled=True)
-    (total,) = call(second_sum, [VM], [((MEMBERS, 8, D), F32)], parts, name="second_sum")
-    blocks = lax.all_to_all(total, "dp", 0, 0, tiled=True)
-    (whole,) = call(assemble, [VM], [((MEMBERS, CHUNK, D), F32)], blocks, name="assemble")
-    whole = lax.all_to_all(whole, "inner", 0, 0, tiled=True)
+    parts = lax.all_to_all(grads, DP + ("b",), 0, 0, tiled=True)
+    (total,) = call(reduce_tiles, [VM], [((YS, 16, 128), F32)], parts)
+    blocks = lax.all_to_all(total, "y", 0, 0, tiled=True)
+    (whole,) = call(assemble, [VM], [((MEMBERS, CHUNK, 128), F32)], blocks)
+    mine = lax.all_to_all(whole, INNER, 0, 0, tiled=True)
+    other = lax.ppermute(mine, "core", [(0, 1), (1, 0)])
     loss, d_class, d_gain, d_qkv, d_out, d_head = call(
         unpack,
-        [VM],
+        [SM, VM, VM],
         [
             ((1, D), F32),
             ((16, D), F32),
@@ -543,19 +556,21 @@
             ((1, D, D), F32),
             ((1, D), F32),
         ],
-        whole,
-        name="unpack",
+        lax.axis_index("core").astype(I32)[None],
+        mine,
+        other,
     )
     return (loss[0, :MICRO], d_class, d_gain, d_qkv, d_out, d_head.reshape(D))
 
 
 def solution(mesh):
+    cut = Mesh(mesh.devices.reshape(2, YS, 2, TILES_DEV, SHARE), ("pipe",) + DP + INNER)
     placed = (
-        P("dp", "inner", None, None),
-        P("dp", None),
-        P("dp"),
-        P("dp"),
-        P("dp", None),
+        P(DP, INNER, None, None),
+        P(DP, None),
+        P(DP),
+        P(DP),
+        P(DP, None),
         P(),
         P("pipe", None),
         P("pipe", None, None),
@@ -563,8 +578,8 @@
         P(),
     )
     return jax.shard_map(
-        shards,
-        mesh=mesh,
+        whole_step,
+        mesh=cut,
         in_specs=placed,
         out_specs=(P(), P(), P("pipe", None), P("pipe", None, None), P("pipe", None, None), P()),
         check_vma=False,

time: 154 us -> 145 us (0.942)
  blocking collectives: 84.6 us -> 67.9 us
  starting transfers between devices: 20.9 us -> 27.9 us
    all_to_all x4 -> x3, blocking collectives: 84.6 us -> 67.9 us  [the longest x1 37 us: whole_step(): parts = lax.all_to_all(grads, DP + ('b',), 0, 0, tiled=True)]
    ppermute x3 -> x4, starting transfers between devices: 7.5 us -> 14.3 us  [the longest x3 7.5 us: swap(): return lax.ppermute(v, 'pipe', [(0, 1), (1, 0)])]
    ppermute x3 -> x4, waiting for transfers between devices: 11.6 us -> 13.1 us  [the longest x3 11.5 us: swap(): return lax.ppermute(v, 'pipe', [(0, 1), (1, 0)])]
    pallas_call x5 -> x4, Pallas kernels: 32 us -> 32.1 us  [call(): pl.pallas_call(body, out_shape=[jax.ShapeDtypeStruct(s, t) for s, t in ou...]
  transfers between devices with their start and end apart: 4 -> 5, of which waited for: 2 -> 3; matrix products, arithmetic and copies ran while one was open for 0% -> 0% of each run, Pallas kernels for 0% -> 0%
where the time goes in v3:
time: 145 us
  blocking collectives  67.9 us (47%)
  Pallas kernels  32.1 us (22%)
  starting transfers between devices  27.9 us (19%)
  waiting for transfers between devices  13.1 us (9%)
  local copies, waits for them, and re-layouts  2.3 us (2%)
    all_to_all x1, blocking collectives, whole_step(): parts = lax.all_to_all(grads, DP + ('b',), 0, 0, tiled=True)  37 us
    pallas_call x4, Pallas kernels, call(): pl.pallas_call(body, out_shape=[jax.ShapeDtypeStruct(s, t) for s, t in ou...  32.1 us
    all_to_all x1, blocking collectives, whole_step(): mine = lax.all_to_all(whole, INNER, 0, 0, tiled=True)  19.2 us
    all_to_all x1, starting transfers between devices, whole_step(): whole_tile = lax.all_to_all(by_dest, INNER, 0, 0, tiled=True)  13.5 us
    all_to_all x1, blocking collectives, whole_step(): blocks = lax.all_to_all(total, 'y', 0, 0, tiled=True)  11.8 us
    ppermute x3, waiting for transfers between devices, swap(): return lax.ppermute(v, 'pipe', [(0, 1), (1, 0)])  11.5 us
    ppermute x3, starting transfers between devices, swap(): return lax.ppermute(v, 'pipe', [(0, 1), (1, 0)])  7.5 us
    ppermute x1, starting transfers between devices, whole_step(): other = lax.ppermute(mine, 'core', [(0, 1), (1, 0)])  6.82 us
  transfers between devices with their start and end apart: 5, of which 3 were waited for; matrix products, arithmetic and copies ran while one was open for 0% of the time, Pallas kernels for 0%

profile of v3, /device:TPU:1, one launch (start us, length us, event | category | flops | bytes accessed | tf_op | source)
XLA Modules:
  0.0 144.5 jit_solution(7671528245926909341)
XLA Ops:
  0.6 1.7 %broadcast_in_dim.13 = bf16[4,4,48,256]{3,2,1,0:T(8,128)(2,1)} broadcast(bf16[4,48,256]{2,1,0:T(8,128)(2,1)} %bitcast.10), dimensions={0,2,3} | broadcast | bytes 491520 | tf_op jit(solution)/shard_map/broadcast_in_dim | solution.py:520
  2.3 13.5 %all-to-all-start = ((bf16[16,48,256]{2,1,0:T(8,128)(2,1)}), bf16[16,48,256]{2,1,0:T(8,128)(2,1)S(1)}, u32[]{:S(2)}, u32[]{:S(2)}) async-start(bf16[16,48,256]{2,1,0:T(8,128)(2,1)} %bitcast.4), calls=%async_computation | async-start | bytes 786432 | tf_op jit(solution)/shard_map/all_to_all | solution.py:521
  15.9 0.0 copy-start.8
  15.9 2.2 %collective-permute-start = (f32[1,256]{1,0:T(1,128)S(1)}, f32[1,256]{1,0:T(1,128)S(1)}, u32[]{:S(2)}, u32[]{:S(2)}) collective-permute-start(f32[1,256]{1,0:T(1,128)S(1)} %copy-done.4), channel_id=1, source_target_pairs={{0,256},{256,0},{1,257},{257,1},{2,258},{258,2},{3,259},{259,3},{4... | collective-permute-start | bytes 3080 | tf_op jit(solution)/shard_map/ppermute | solution.py:503
  18.1 3.1 %collective-permute-start.2 = (bf16[1,256,256]{2,1,0:T(8,128)(2,1)S(1)}, bf16[1,256,256]{2,1,0:T(8,128)(2,1)S(1)}, u32[]{:S(2)}, u32[]{:S(2)}) collective-permute-start(bf16[1,256,256]{2,1,0:T(8,128)(2,1)S(1)} %copy-done.1), channel_id=1, source_target_pairs={{0,256},{256,0},{1,257},{257,1},{2,258},{258,2},{3,259},{259,3},{4... | collective-permute-start | bytes 393224 | tf_op jit(solution)/shard_map/ppermute | solution.py:503
  21.2 2.2 %collective-permute-start.1 = (bf16[1,256,768]{2,1,0:T(8,128)(2,1)S(1)}, bf16[1,256,768]{2,1,0:T(8,128)(2,1)S(1)}, u32[]{:S(2)}, u32[]{:S(2)}) collective-permute-start(bf16[1,256,768]{2,1,0:T(8,128)(2,1)S(1)} %copy-done), channel_id=1, source_target_pairs={{0,256},{256,0},{1,257},{257,1},{2,258},{258,2},{3,259},{259,3},{4... | collective-permute-start | bytes 1179656 | tf_op jit(solution)/shard_map/ppermute | solution.py:503
  23.5 0.1 mul.38
  23.6 0.3 fusion.enc
  23.9 0.0 copy-start.2
  23.9 0.0 copy-start.7
  23.9 0.0 copy-start.3
  23.9 0.1 pad_add_fusion.scal
  24.0 0.0 collective-permute-done.gain_b
  24.0 2.6 %collective-permute-done.2.wout_b = bf16[1,256,256]{2,1,0:T(8,128)(2,1)S(1)} collective-permute-done((bf16[1,256,256]{2,1,0:T(8,128)(2,1)S(1)}, bf16[1,256,256]{2,1,0:T(8,128)(2,1)S(1)}, u32[]{:S(2)}, u32[]{:S(2)}) %collective-permute-start.2) | collective-permute-done | bytes 131104 | tf_op jit(solution)/shard_map/ppermute | solution.py:503
  26.6 9.0 %collective-permute-done.1.wqkv_b = bf16[1,256,768]{2,1,0:T(8,128)(2,1)S(1)} collective-permute-done((bf16[1,256,768]{2,1,0:T(8,128)(2,1)S(1)}, bf16[1,256,768]{2,1,0:T(8,128)(2,1)S(1)}, u32[]{:S(2)}, u32[]{:S(2)}) %collective-permute-start.1) | collective-permute-done | bytes 393248 | tf_op jit(solution)/shard_map/ppermute | solution.py:503
  35.6 30.9 %shard_map.145 = f32[64,16,128]{2,1,0:T(8,128)S(1)} custom-call(s32[2]{0:T(128)S(1)} %pad_add_fusion.scal, s32[4]{0:T(128)S(1)} %copy-done.6, s32[4]{0:T(128)S(1)} %copy-done.7, s32[4,48]{1,0:T(4,128)S(1)} %copy-done.3, bf16[16,48,256]{2,1,0:T(8,128)(2,1)S(1)} %all-to-all-done.pix, f32[64,256]{1,0:T(8,128)S(1)} %fusion.enc, bf16[16,256]{1,0:T(8,128)(2,1)S(1)} %copy-done.2, ...), custom_call_target="tpu_custom_call" | custom-call | tf_op jit(solution)/shard_map/pallas_call | solution.py:485
  66.4 37.0 %all_to_all.20.parts = f32[64,16,128]{2,1,0:T(8,128)S(1)} all-to-all(f32[64,16,128]{2,1,0:T(8,128)S(1)} %shard_map.145), channel_id=1, replica_groups=mesh['pipe'=2,'y'=8,'core'=2,'b'=4,'r'=4] {'y','core','b'}, dimensions={0} | all-to-all | bytes 1048576 | tf_op jit(solution)/shard_map/all_to_all | solution.py:542
  103.4 0.1 shard_map.146
  103.5 11.8 %all_to_all.21.blocks = f32[8,16,128]{2,1,0:T(8,128)S(1)} all-to-all(f32[8,16,128]{2,1,0:T(8,128)S(1)} %shard_map.146), channel_id=1, replica_groups=mesh['pipe'=2,'y'=8,'core'=2,'b'=4,'r'=4] {'y'}, dimensions={0} | all-to-all | bytes 131072 | tf_op jit(solution)/shard_map/all_to_all | solution.py:544
  115.3 19.2 %all_to_all.22.mine = f32[16,72,128]{2,1,0:T(8,128)S(1)} all-to-all(f32[16,72,128]{2,1,0:T(8,128)S(1)} %shard_map.147), channel_id=1, replica_groups=mesh['pipe'=2,'y'=8,'core'=2,'b'=4,'r'=4] {'b','r'}, dimensions={0} | all-to-all | bytes 1179648 | tf_op jit(solution)/shard_map/all_to_all | solution.py:546
  134.5 6.8 %collective-permute-start.3 = (f32[16,72,128]{2,1,0:T(8,128)S(1)}, f32[16,72,128]{2,1,0:T(8,128)S(1)}, u32[]{:S(2)}, u32[]{:S(2)}) collective-permute-start(f32[16,72,128]{2,1,0:T(8,128)S(1)} %all_to_all.22.mine), channel_id=1, source_target_pairs={{0,16},{16,0},{1,17},{17,1},{2,18},{18,2},{3,19},{19,3},{4,20},{20... | collective-permute-start | bytes 1769480 | tf_op jit(solution)/shard_map/ppermute | solution.py:547
  141.3 1.6 %collective-permute-done.3.other = f32[16,72,128]{2,1,0:T(8,128)S(1)} collective-permute-done((f32[16,72,128]{2,1,0:T(8,128)S(1)}, f32[16,72,128]{2,1,0:T(8,128)S(1)}, u32[]{:S(2)}, u32[]{:S(2)}) %collective-permute-start.3) | collective-permute-done | bytes 589856 | tf_op jit(solution)/shard_map/ppermute | solution.py:547
  142.9 1.1 shard_map.148
  144.0 0.5 slice_bitcast_fusion
  (19 shorter events, 0.1 us)
Async XLA Ops:
  2.3 13.6 %copy-start.4 = (f32[1,256]{1,0:T(1,128)S(1)}, f32[1,256]{1,0:T(1,128)}, u32[]{:S(2)}) copy-start(f32[1,256]{1,0:T(1,128)} %gain_a.1) | copy-start | bytes 3076
  2.3 15.8 %copy-start.1 = (bf16[1,256,256]{2,1,0:T(8,128)(2,1)S(1)}, bf16[1,256,256]{2,1,0:T(8,128)(2,1)}, u32[]{:S(2)}) copy-start(bf16[1,256,256]{2,1,0:T(8,128)(2,1)} %wout_a.1) | copy-start | bytes 393220
  2.3 18.9 %copy-start = (bf16[1,256,768]{2,1,0:T(8,128)(2,1)S(1)}, bf16[1,256,768]{2,1,0:T(8,128)(2,1)}, u32[]{:S(2)}) copy-start(bf16[1,256,768]{2,1,0:T(8,128)(2,1)} %wqkv_a.1) | copy-start | bytes 1179652
  2.3 33.2 %all-to-all-start = ((bf16[16,48,256]{2,1,0:T(8,128)(2,1)}), bf16[16,48,256]{2,1,0:T(8,128)(2,1)S(1)}, u32[]{:S(2)}, u32[]{:S(2)}) async-start(bf16[16,48,256]{2,1,0:T(8,128)(2,1)} %bitcast.4), calls=%async_computation | async-start | bytes 786432 | tf_op jit(solution)/shard_map/all_to_all | solution.py:521
  15.9 7.6 %copy-start.8 = (s32[4,16]{1,0:T(4,128)S(1)}, s32[4,16]{1,0:T(4,128)}, u32[]{:S(2)}) copy-start(s32[4,16]{1,0:T(4,128)} %param.11) | copy-start | bytes 772
  15.9 8.1 %collective-permute-start = (f32[1,256]{1,0:T(1,128)S(1)}, f32[1,256]{1,0:T(1,128)S(1)}, u32[]{:S(2)}, u32[]{:S(2)}) collective-permute-start(f32[1,256]{1,0:T(1,128)S(1)} %copy-done.4), channel_id=1, source_target_pairs={{0,256},{256,0},{1,257},{257,1},{2,258},{258,2},{3,259},{259,3},{4... | collective-permute-start | bytes 3080 | tf_op jit(solution)/shard_map/ppermute | solution.py:503
  18.1 8.4 %collective-permute-start.2 = (bf16[1,256,256]{2,1,0:T(8,128)(2,1)S(1)}, bf16[1,256,256]{2,1,0:T(8,128)(2,1)S(1)}, u32[]{:S(2)}, u32[]{:S(2)}) collective-permute-start(bf16[1,256,256]{2,1,0:T(8,128)(2,1)S(1)} %copy-done.1), channel_id=1, source_target_pairs={{0,256},{256,0},{1,257},{257,1},{2,258},{258,2},{3,259},{259,3},{4... | collective-permute-start | bytes 393224 | tf_op jit(solution)/shard_map/ppermute | solution.py:503
  21.2 14.3 %collective-permute-start.1 = (bf16[1,256,768]{2,1,0:T(8,128)(2,1)S(1)}, bf16[1,256,768]{2,1,0:T(8,128)(2,1)S(1)}, u32[]{:S(2)}, u32[]{:S(2)}) collective-permute-start(bf16[1,256,768]{2,1,0:T(8,128)(2,1)S(1)} %copy-done), channel_id=1, source_target_pairs={{0,256},{256,0},{1,257},{257,1},{2,258},{258,2},{3,259},{259,3},{4... | collective-permute-start | bytes 1179656 | tf_op jit(solution)/shard_map/ppermute | solution.py:503
  23.9 11.6 %copy-start.2 = (bf16[16,256]{1,0:T(8,128)(2,1)S(1)}, bf16[16,256]{1,0:T(8,128)(2,1)}, u32[]{:S(2)}) copy-start(bf16[16,256]{1,0:T(8,128)(2,1)} %cls.1) | copy-start | bytes 24580
  23.9 11.6 %copy-start.7 = (s32[4]{0:T(128)S(1)}, s32[4]{0:T(128)}, u32[]{:S(2)}) copy-start(s32[4]{0:T(128)} %slots.1) | copy-start | bytes 52
  23.9 11.6 %copy-start.3 = (s32[4,48]{1,0:T(4,128)S(1)}, s32[4,48]{1,0:T(4,128)}, u32[]{:S(2)}) copy-start(s32[4,48]{1,0:T(4,128)} %labels.1) | copy-start | bytes 2308
  24.0 11.5 %copy-start.5 = (f32[256]{0:T(256)S(1)}, f32[256]{0:T(256)}, u32[]{:S(2)}) copy-start(f32[256]{0:T(256)} %param.19) | copy-start | bytes 3076
  24.0 11.5 %copy-start.6 = (s32[4]{0:T(128)S(1)}, s32[4]{0:T(128)}, u32[]{:S(2)}) copy-start(s32[4]{0:T(128)} %counts.1) | copy-start | bytes 52
  134.5 8.4 %collective-permute-start.3 = (f32[16,72,128]{2,1,0:T(8,128)S(1)}, f32[16,72,128]{2,1,0:T(8,128)S(1)}, u32[]{:S(2)}, u32[]{:S(2)}) collective-permute-start(f32[16,72,128]{2,1,0:T(8,128)S(1)} %all_to_all.22.mine), channel_id=1, source_target_pairs={{0,16},{16,0},{1,17},{17,1},{2,18},{18,2},{3,19},{19,3},{4,20},{20... | collective-permute-start | bytes 1769480 | tf_op jit(solution)/shard_map/ppermute | solution.py:547

commit v4 on v3

--- a/solution.py
+++ b/solution.py
@@ -31,10 +31,10 @@
 MEMBERS = 16
 SHARE = 4
 YS = 8
-OWNERS = 64
+OWNERS = 32
 CHUNK = 72
 DP = ("y", "core")
-INNER = ("b", "r")
+INNER = ("r", "b")
 
 
 def dot(a, b):
@@ -72,11 +72,14 @@
     return dot(hi, ones) + dot(lo, ones)
 
 
-def spread(rows_of):
+def spread(rows_of, masks):
     n = rows_of.shape[0]
-    lane_head = iota((n, D), 1) >> 5
-    zero = jnp.zeros_like(rows_of)
-    return jnp.concatenate([jnp.where(lane_head == h, rows_of, zero) for h in range(HEADS)], axis=0)
+    return jnp.concatenate([rows_of * masks[h, 0:n, :] for h in range(HEADS)], axis=0)
+
+
+def spread_pair(rows_of, masks):
+    hi, lo = split(rows_of)
+    return spread(hi, masks), spread(lo, masks)
 
 
 def gathered_heads(wide):
@@ -88,10 +91,10 @@
     return out
 
 
-def logits_t(k, q_wide):
+def logits_t(k, q, masks):
     n = k.shape[0]
     k_hi, k_lo = split(k)
-    q_hi, q_lo = split(q_wide)
+    q_hi, q_lo = spread_pair(q, masks)
     both = dot_nt(jnp.concatenate([k_hi, k_lo], axis=0), q_hi)
     return SHARP * (both[:n] + both[n:] + dot_nt(k_hi, q_lo))
 
@@ -130,22 +133,36 @@
     return pl.ds(pl.multiple_of(c * ROWS, ROWS), ROWS)
 
 
-def put_tiles(out, d_w):
-    for n in range(OWNERS):
-        row, lane = 8 * (n // 2), 128 * (n % 2)
-        out[n, 0:8, :] = d_w[row : row + 8, lane : lane + 128]
+def tile_at(y, c, b):
+    n = (2 * y + c) * TILES_DEV + b
+    return 8 * (n // 2), 128 * (n % 2)
+
+
+def put_tiles(keep, give, lower, d_w):
+    for y in range(YS):
+        for b in range(TILES_DEV):
+            pair = []
+            for c in range(2):
+                row, lane = tile_at(y, c, b)
+                pair.append(d_w[row : row + 8, lane : lane + 128])
+            keep[TILES_DEV * y + b, 0:8, :] = jnp.where(lower, pair[0], pair[1])
+            give[TILES_DEV * y + b, 0:8, :] = jnp.where(lower, pair[1], pair[0])
 
 
 def step(
-    scal, counts, slots, labels, pix, enc, cls, gain_a, gain_b, wqkv_a, wqkv_b, wout_a, wout_b, head, out, *scratch
+    scal, counts, slots, labels, pix, enc, cls, gain_a, gain_b, wqkv_a, wqkv_b, wout_a, wout_b, head, keep, give, *scratch
 ):
     (wt, ws, ot, os, seq_a, seq_b, xhat_t, normed_t, k_t, kn_t, v_t, ad, ac, att_t, q_t, qn_t, e_cls, inv_c,
      u_s, xhat_s, normed_s, inv_s, k_s, kn_s, q_s, qn_s, v_s, a_s, att_s, log_s, tot, rows_s, y_hi, y_lo,
-     acc_q, acc_k, acc_v, acc_n, acc_g, d_cls) = scratch
+     acc_q, acc_k, acc_v, acc_n, acc_g, d_cls, masks) = scratch
     first = scal[1] == 1
-    tile = scal[0] >> 2
-    share = scal[0] & 3
+    tile = scal[0] & 3
+    share = scal[0] >> 2
+    lower = scal[2] == 0
     ones = head_ones()
+    lane_head = iota((PATCHES, D), 1) >> 5
+    for h in range(HEADS):
+        masks[h] = jnp.where(lane_head == h, 1.0, 0.0).astype(BF16)
     wt[...] = jnp.where(first, wqkv_a[0], wqkv_b[0])
     ws[...] = jnp.where(first, wqkv_b[0], wqkv_a[0])
     ot[...] = jnp.where(first, wout_a[0], wout_b[0])
@@ -179,7 +196,7 @@
     q_t[...] = kq_unit[16:]
     qn_t[...] = kq_inv[16:]
     v_t[ALL:, :] = qkv_c[:, 2 * D :].astype(BF16)
-    e_cls[...] = jnp.exp(logits_t(kq_unit[:16], spread(kq_unit[16:])))
+    e_cls[...] = jnp.exp(logits_t(kq_unit[:16], kq_unit[16:], masks))
 
     @pl.loop(0, CHUNKS)
     def _(c):
@@ -200,7 +217,7 @@
         k = k * k_inv
         k_t[rows, :] = k
         kn_t[rows, :] = k_inv
-        raised = jnp.exp(logits_t(k, spread(q_t[...])))
+        raised = jnp.exp(logits_t(k, q_t[...], masks))
         shown = (iota((ROWS, 128), 0) & 15) < counts[tile]
         e_dates = jnp.where(shown, raised, 0.0).reshape(SEQS, DATES, 128)
         e_class = e_cls[...]
@@ -249,7 +266,7 @@
         parts, held = [], []
         for b in range(CLASS_CHUNK):
             part = slice(b * PATCHES, b * PATCHES + PATCHES)
-            raised = jnp.exp(logits_t(k[part], spread(q[part])))
+            raised = jnp.exp(logits_t(k[part], q[part], masks))
             a = raised / jnp.sum(raised, axis=0, keepdims=True)
             held.append(a)
             parts.append(gathered_heads(dot_tn(a.astype(BF16), v[part])))
@@ -290,11 +307,11 @@
         for b in range(CLASS_CHUNK):
             part = slice(b * PATCHES, b * PATCHES + PATCHES)
             a = a_all[part]
-            wide = spread(d_att[part])
+            wide = spread(d_att[part], masks)
             da = rounded(dot_nt(v[part], wide))
             dv_parts.append(dot(a.astype(BF16), wide).astype(BF16))
             ds = SHARP * a * (da - jnp.sum(da * a, axis=0, keepdims=True))
-            q_hi, q_lo = split(spread(q[part]))
+            q_hi, q_lo = spread_pair(q[part], masks)
             dk_parts.append(three_pass(ds, q_hi, q_lo))
             dq_parts.append(gathered_heads(three_pass_tn(ds, k[part])))
         dv = stack(dv_parts)
@@ -331,12 +348,12 @@
     def _():
         x = normed_s[...]
         d_w = dot_tn(x, y_hi[0:ALL, :]) + dot_tn(x, y_lo[0:ALL, :])
-        put_tiles(out, d_w)
+        put_tiles(keep, give, lower, d_w)
 
     @pl.when(jnp.logical_and(scal[1] == 0, share == 3))
     def _():
         d_w = dot_tn(stack([w_hi, w_hi, w_mid, w_mid, zero]), stack([h_hi, h_mid, h_hi, h_mid, zero]))
-        put_tiles(out, d_w)
+        put_tiles(keep, give, lower, d_w)
 
     @pl.loop(0, CHUNKS)
     def _(c):
@@ -353,7 +370,7 @@
         da_class, da_dates, dv_class, dv_dates = [], [], [], []
         for s in range(SEQS):
             part = slice(s * 16, s * 16 + 16)
-            wide = spread(d_att[part])
+            wide = spread(d_att[part], masks)
             values = stack([v_class, v[part]])
             weights = stack([a_class[part], a_dates[part]]).astype(BF16)
             da = rounded(dot_nt(values, wide))
@@ -369,7 +386,7 @@
         )
         ds_c = SHARP * cube(a_class) * (cube(da_c) - both)
         ds_d = SHARP * cube(a_dates) * (cube(da_d) - both)
-        q_hi, q_lo = split(spread(q))
+        q_hi, q_lo = spread_pair(q, masks)
         dk = three_pass(stack([ds_d.reshape(ROWS, 128), ds_c.reshape(ROWS, 128)]), q_hi, q_lo)
         dq_parts = []
         for s in range(SEQS):
@@ -417,18 +434,19 @@
         y_lo[ALL:, :] = lo
         x = normed_t[...]
         d_w = dot_tn(x, y_hi[...]) + dot_tn(x, y_lo[...])
-        put_tiles(out, d_w)
+        put_tiles(keep, give, lower, d_w)
 
     @pl.when(jnp.logical_and(first, share == 3))
     def _():
-        put_tiles(out, dot_tn(att_t[...], y_hi[0:ALL, :]))
+        put_tiles(keep, give, lower, dot_tn(att_t[...], y_hi[0:ALL, :]))
 
     misc = jnp.where(share == 0, gain_grad, jnp.where(share == 1, d_head, rows_s[5:6, :]))
     for b in range(SHARE):
         row = d_cls[pl.ds(4 * share + b, 1), :]
         small = stack([row[:, :128], row[:, 128:], misc[:, :128], misc[:, 128:], jnp.zeros((4, 128), F32)])
-        for d in range(MEMBERS):
-            out[SHARE * d + b, 8:16, :] = small
+        for y in range(YS):
+            keep[TILES_DEV * y + b, 8:16, :] = small
+            give[TILES_DEV * y + b, 8:16, :] = small
 
 
 STEP_SCRATCH = [
@@ -441,6 +459,7 @@
     ((ALL, HEADS * PATCHES), F32), ((ALL, D), BF16), ((ALL, 128), F32), ((PATCHES, 128), F32), ((8, D), F32),
     ((ALL + 16, D), BF16), ((ALL + 16, D), BF16),
     ((16, D), F32), ((16, D), F32), ((16, D), F32), ((16, D), F32), ((16, D), F32), ((16, D), F32),
+    ((HEADS, PATCHES, D), BF16),
 ]
 
 
@@ -457,13 +476,12 @@
     lower = core[0] == 0
     for b in range(SHARE):
         for part in range(4):
-            own, far = mine[SHARE * b + part], other[SHARE * b + part]
+            own, far = mine[SHARE * part + b], other[SHARE * part + b]
             blocks = (jnp.where(lower, own, far), jnp.where(lower, far, own))
             for c in range(2):
                 for y in range(YS):
-                    n = (2 * y + c) * SHARE + b
                     tile = blocks[c][8 * y : 8 * y + 8]
-                    row, lane = 8 * (n // 2), 128 * (n % 2)
+                    row, lane = tile_at(y, c, b)
                     if part < 3:
                         d_qkv[0, row : row + 8, part * D + lane : part * D + lane + 128] = tile
                     else:
@@ -517,13 +535,14 @@
 ):
     first = (lax.axis_index("pipe") == 0).astype(I32)
     inner = lax.axis_index(INNER).astype(I32)
-    by_dest = jnp.repeat(pixels.reshape(TILES_DEV, PATCHES, D), SHARE, axis=0)
+    by_dest = jnp.tile(pixels.reshape(TILES_DEV, PATCHES, D), (SHARE, 1, 1))
     whole_tile = lax.all_to_all(by_dest, INNER, 0, 0, tiled=True)
-    (grads,) = call(
+    core = lax.axis_index("core").astype(I32)
+    keep, give = call(
         step,
         [SM] * 3 + [VM] * 11,
-        [((OWNERS, 16, 128), F32)],
-        jnp.stack([inner, first]),
+        [((OWNERS, 16, 128), F32)] * 2,
+        jnp.stack([inner, first, core]),
         clear_count,
         batch_slot,
         labels,
@@ -539,7 +558,8 @@
         head_vec.reshape(1, D),
         scratch=STEP_SCRATCH,
     )
-    parts = lax.all_to_all(grads, DP + ("b",), 0, 0, tiled=True)
+    given = lax.ppermute(give, "core", [(0, 1), (1, 0)])
+    parts = lax.all_to_all(keep + given, ("y", "b"), 0, 0, tiled=True)
     (total,) = call(reduce_tiles, [VM], [((YS, 16, 128), F32)], parts)
     blocks = lax.all_to_all(total, "y", 0, 0, tiled=True)
     (whole,) = call(assemble, [VM], [((MEMBERS, CHUNK, 128), F32)], blocks)
@@ -556,7 +576,7 @@
             ((1, D, D), F32),
             ((1, D), F32),
         ],
-        lax.axis_index("core").astype(I32)[None],
+        core[None],
         mine,
         other,
     )

time: 145 us -> 136 us (0.938)
  blocking collectives: 67.9 us -> 53.9 us
  starting transfers between devices: 27.9 us -> 31.8 us
    all_to_all x1, blocking collectives: 37 us -> 21.4 us  [whole_step(): parts = lax.all_to_all(keep + given, ('y', 'b'), 0, 0, tiled=True)]
    all_to_all x1, blocking collectives: 19.2 us -> 22.6 us  [whole_step(): mine = lax.all_to_all(whole, INNER, 0, 0, tiled=True)]
    ppermute x0 -> x1, starting transfers between devices: none -> 3.17 us  [whole_step(): given = lax.ppermute(give, 'core', [(0, 1), (1, 0)])]
    all_to_all x1, blocking collectives: 11.8 us -> 9.85 us  [whole_step(): blocks = lax.all_to_all(total, 'y', 0, 0, tiled=True)]
    another operation x0 -> x1, local copies, waits for them, and re-layouts: none -> 1.66 us  [whole_step(): by_dest = jnp.tile(pixels.reshape(TILES_DEV, PATCHES, D), (SHARE, 1, 1))]
    broadcast_in_dim x1 -> x0, local copies, waits for them, and re-layouts: 1.66 us -> none  [whole_step(): by_dest = jnp.repeat(pixels.reshape(TILES_DEV, PATCHES, D), SHARE, axis=0)]
  transfers between devices with their start and end apart: 5 -> 6, of which waited for: 3 -> 4; matrix products, arithmetic and copies ran while one was open for 0% -> 0% of each run, Pallas kernels for 0% -> 0%
where the time goes in v4:
time: 136 us; the launch traced here: 135 us
  blocking collectives  53.9 us (40%)
  Pallas kernels  32 us (24%)
  starting transfers between devices  31.8 us (23%)
  waiting for transfers between devices  14.3 us (11%)
  local copies, waits for them, and re-layouts  2.3 us (2%)
    pallas_call x4, Pallas kernels, call(): pl.pallas_call(body, out_shape=[jax.ShapeDtypeStruct(s, t) for s, t in ou...  32 us
    all_to_all x1, blocking collectives, whole_step(): mine = lax.all_to_all(whole, INNER, 0, 0, tiled=True)  22.6 us
    all_to_all x1, blocking collectives, whole_step(): parts = lax.all_to_all(keep + given, ('y', 'b'), 0, 0, tiled=True)  21.4 us
    all_to_all x1, starting transfers between devices, whole_step(): whole_tile = lax.all_to_all(by_dest, INNER, 0, 0, tiled=True)  13.5 us
    ppermute x3, waiting for transfers between devices, swap(): return lax.ppermute(v, 'pipe', [(0, 1), (1, 0)])  11.5 us
    all_to_all x1, blocking collectives, whole_step(): blocks = lax.all_to_all(total, 'y', 0, 0, tiled=True)  9.85 us
    ppermute x1, starting transfers between devices, whole_step(): other = lax.ppermute(mine, 'core', [(0, 1), (1, 0)])  7.59 us
    ppermute x3, starting transfers between devices, swap(): return lax.ppermute(v, 'pipe', [(0, 1), (1, 0)])  7.5 us
  transfers between devices with their start and end apart: 6, of which 4 were waited for; matrix products, arithmetic and copies ran while one was open for 0% of the time, Pallas kernels for 0%

profile of v4, /device:TPU:1, one launch (start us, length us, event | category | flops | bytes accessed | tf_op | source)
XLA Modules:
  0.0 135.5 jit_solution(2763257626663670919)
XLA Ops:
  0.6 1.7 %tile.11 = bf16[4,4,48,256]{3,2,1,0:T(8,128)(2,1)} broadcast(bf16[4,48,256]{2,1,0:T(8,128)(2,1)} %bitcast.10), dimensions={1,2,3} | broadcast | bytes 491520 | tf_op jit(solution)/shard_map/tile | solution.py:538
  2.3 13.5 %all-to-all-start = ((bf16[16,48,256]{2,1,0:T(8,128)(2,1)}), bf16[16,48,256]{2,1,0:T(8,128)(2,1)S(1)}, u32[]{:S(2)}, u32[]{:S(2)}) async-start(bf16[16,48,256]{2,1,0:T(8,128)(2,1)} %bitcast.4), calls=%async_computation | async-start | bytes 786432 | tf_op jit(solution)/shard_map/all_to_all | solution.py:539
  15.9 0.0 copy-start.8
  15.9 2.2 %collective-permute-start = (f32[1,256]{1,0:T(1,128)S(1)}, f32[1,256]{1,0:T(1,128)S(1)}, u32[]{:S(2)}, u32[]{:S(2)}) collective-permute-start(f32[1,256]{1,0:T(1,128)S(1)} %copy-done.4), channel_id=1, source_target_pairs={{0,256},{256,0},{1,257},{257,1},{2,258},{258,2},{3,259},{259,3},{4... | collective-permute-start | bytes 3080 | tf_op jit(solution)/shard_map/ppermute | solution.py:521
  18.1 3.1 %collective-permute-start.2 = (bf16[1,256,256]{2,1,0:T(8,128)(2,1)S(1)}, bf16[1,256,256]{2,1,0:T(8,128)(2,1)S(1)}, u32[]{:S(2)}, u32[]{:S(2)}) collective-permute-start(bf16[1,256,256]{2,1,0:T(8,128)(2,1)S(1)} %copy-done.1), channel_id=1, source_target_pairs={{0,256},{256,0},{1,257},{257,1},{2,258},{258,2},{3,259},{259,3},{4... | collective-permute-start | bytes 393224 | tf_op jit(solution)/shard_map/ppermute | solution.py:521
  21.2 2.2 %collective-permute-start.1 = (bf16[1,256,768]{2,1,0:T(8,128)(2,1)S(1)}, bf16[1,256,768]{2,1,0:T(8,128)(2,1)S(1)}, u32[]{:S(2)}, u32[]{:S(2)}) collective-permute-start(bf16[1,256,768]{2,1,0:T(8,128)(2,1)S(1)} %copy-done), channel_id=1, source_target_pairs={{0,256},{256,0},{1,257},{257,1},{2,258},{258,2},{3,259},{259,3},{4... | collective-permute-start | bytes 1179656 | tf_op jit(solution)/shard_map/ppermute | solution.py:521
  23.5 0.1 mul.38
  23.6 0.3 fusion.enc
  23.9 0.0 copy-start.2
  23.9 0.0 copy-start.7
  23.9 0.0 copy-start.3
  23.9 0.1 pad_add_fusion.scal
  24.0 2.5 %collective-permute-done.2.wout_b = bf16[1,256,256]{2,1,0:T(8,128)(2,1)S(1)} collective-permute-done((bf16[1,256,256]{2,1,0:T(8,128)(2,1)S(1)}, bf16[1,256,256]{2,1,0:T(8,128)(2,1)S(1)}, u32[]{:S(2)}, u32[]{:S(2)}) %collective-permute-start.2) | collective-permute-done | bytes 131104 | tf_op jit(solution)/shard_map/ppermute | solution.py:521
  26.6 9.0 %collective-permute-done.1.wqkv_b = bf16[1,256,768]{2,1,0:T(8,128)(2,1)S(1)} collective-permute-done((bf16[1,256,768]{2,1,0:T(8,128)(2,1)S(1)}, bf16[1,256,768]{2,1,0:T(8,128)(2,1)S(1)}, u32[]{:S(2)}, u32[]{:S(2)}) %collective-permute-start.1) | collective-permute-done | bytes 393248 | tf_op jit(solution)/shard_map/ppermute | solution.py:521
  35.6 30.8 %shard_map.145 = (f32[32,16,128]{2,1,0:T(8,128)S(1)}, f32[32,16,128]{2,1,0:T(8,128)S(1)}) custom-call(s32[3]{0:T(128)S(1)} %pad_add_fusion.scal, s32[4]{0:T(128)S(1)} %copy-done.6, s32[4]{0:T(128)S(1)} %copy-done.7, s32[4,48]{1,0:T(4,128)S(1)} %copy-done.3, bf16[16,48,256]{2,1,0:T(8,128)(2,1)S(1)} %all-to-all-done.pix, f32[64,256]{1,0:T(8,128)S(1)} %fusion.enc, ...), custom_call_target="tpu_custom_call" | custom-call | tf_op jit(solution)/shard_map/pallas_call | solution.py:503
  66.4 3.2 %collective-permute-start.3 = (f32[32,16,128]{2,1,0:T(8,128)S(1)}, f32[32,16,128]{2,1,0:T(8,128)S(1)}, u32[]{:S(2)}, u32[]{:S(2)}) collective-permute-start(f32[32,16,128]{2,1,0:T(8,128)S(1)} %get-tuple-element.15), channel_id=1, source_target_pairs={{0,16},{16,0},{1,17},{17,1},{2,18},{18,2},{3,19},{19,3},{4,20},{20... | collective-permute-start | bytes 786440 | tf_op jit(solution)/shard_map/ppermute | solution.py:561
  69.6 1.1 collective-permute-done.3
  70.7 21.4 %all_to_all.20.parts = f32[32,16,128]{2,1,0:T(8,128)S(1)} all-to-all(f32[32,16,128]{2,1,0:T(8,128)S(1)} %add.19), channel_id=1, replica_groups=mesh['pipe'=2,'y'=8,'core'=2,'r'=4,'b'=4] {'y','b'}, dimensions={0} | all-to-all | bytes 524288 | tf_op jit(solution)/shard_map/all_to_all | solution.py:562
  92.2 9.9 %all_to_all.21.blocks = f32[8,16,128]{2,1,0:T(8,128)S(1)} all-to-all(f32[8,16,128]{2,1,0:T(8,128)S(1)} %shard_map.146), channel_id=1, replica_groups=mesh['pipe'=2,'y'=8,'core'=2,'r'=4,'b'=4] {'y'}, dimensions={0} | all-to-all | bytes 131072 | tf_op jit(solution)/shard_map/all_to_all | solution.py:564
  102.1 22.6 %all_to_all.22.mine = f32[16,72,128]{2,1,0:T(8,128)S(1)} all-to-all(f32[16,72,128]{2,1,0:T(8,128)S(1)} %shard_map.147), channel_id=1, replica_groups=mesh['pipe'=2,'y'=8,'core'=2,'r'=4,'b'=4] {'r','b'}, dimensions={0} | all-to-all | bytes 1179648 | tf_op jit(solution)/shard_map/all_to_all | solution.py:566
  124.7 7.6 %collective-permute-start.4 = (f32[16,72,128]{2,1,0:T(8,128)S(1)}, f32[16,72,128]{2,1,0:T(8,128)S(1)}, u32[]{:S(2)}, u32[]{:S(2)}) collective-permute-start(f32[16,72,128]{2,1,0:T(8,128)S(1)} %all_to_all.22.mine), channel_id=1, source_target_pairs={{0,16},{16,0},{1,17},{17,1},{2,18},{18,2},{3,19},{19,3},{4,20},{20... | collective-permute-start | bytes 1769480 | tf_op jit(solution)/shard_map/ppermute | solution.py:567
  132.3 1.6 %collective-permute-done.4.other = f32[16,72,128]{2,1,0:T(8,128)S(1)} collective-permute-done((f32[16,72,128]{2,1,0:T(8,128)S(1)}, f32[16,72,128]{2,1,0:T(8,128)S(1)}, u32[]{:S(2)}, u32[]{:S(2)}) %collective-permute-start.4) | collective-permute-done | bytes 589856 | tf_op jit(solution)/shard_map/ppermute | solution.py:567
  133.9 1.1 shard_map.148
  135.0 0.5 slice_bitcast_fusion
  (22 shorter events, 0.2 us)
Async XLA Ops:
  2.3 13.6 %copy-start.4 = (f32[1,256]{1,0:T(1,128)S(1)}, f32[1,256]{1,0:T(1,128)}, u32[]{:S(2)}) copy-start(f32[1,256]{1,0:T(1,128)} %gain_a.1) | copy-start | bytes 3076
  2.3 15.8 %copy-start.1 = (bf16[1,256,256]{2,1,0:T(8,128)(2,1)S(1)}, bf16[1,256,256]{2,1,0:T(8,128)(2,1)}, u32[]{:S(2)}) copy-start(bf16[1,256,256]{2,1,0:T(8,128)(2,1)} %wout_a.1) | copy-start | bytes 393220
  2.3 18.9 %copy-start = (bf16[1,256,768]{2,1,0:T(8,128)(2,1)S(1)}, bf16[1,256,768]{2,1,0:T(8,128)(2,1)}, u32[]{:S(2)}) copy-start(bf16[1,256,768]{2,1,0:T(8,128)(2,1)} %wqkv_a.1) | copy-start | bytes 1179652
  2.3 33.2 %all-to-all-start = ((bf16[16,48,256]{2,1,0:T(8,128)(2,1)}), bf16[16,48,256]{2,1,0:T(8,128)(2,1)S(1)}, u32[]{:S(2)}, u32[]{:S(2)}) async-start(bf16[16,48,256]{2,1,0:T(8,128)(2,1)} %bitcast.4), calls=%async_computation | async-start | bytes 786432 | tf_op jit(solution)/shard_map/all_to_all | solution.py:539
  15.9 7.6 %copy-start.8 = (s32[4,16]{1,0:T(4,128)S(1)}, s32[4,16]{1,0:T(4,128)}, u32[]{:S(2)}) copy-start(s32[4,16]{1,0:T(4,128)} %param.11) | copy-start | bytes 772
  15.9 8.1 %collective-permute-start = (f32[1,256]{1,0:T(1,128)S(1)}, f32[1,256]{1,0:T(1,128)S(1)}, u32[]{:S(2)}, u32[]{:S(2)}) collective-permute-start(f32[1,256]{1,0:T(1,128)S(1)} %copy-done.4), channel_id=1, source_target_pairs={{0,256},{256,0},{1,257},{257,1},{2,258},{258,2},{3,259},{259,3},{4... | collective-permute-start | bytes 3080 | tf_op jit(solution)/shard_map/ppermute | solution.py:521
  18.1 8.4 %collective-permute-start.2 = (bf16[1,256,256]{2,1,0:T(8,128)(2,1)S(1)}, bf16[1,256,256]{2,1,0:T(8,128)(2,1)S(1)}, u32[]{:S(2)}, u32[]{:S(2)}) collective-permute-start(bf16[1,256,256]{2,1,0:T(8,128)(2,1)S(1)} %copy-done.1), channel_id=1, source_target_pairs={{0,256},{256,0},{1,257},{257,1},{2,258},{258,2},{3,259},{259,3},{4... | collective-permute-start | bytes 393224 | tf_op jit(solution)/shard_map/ppermute | solution.py:521
  21.2 14.3 %collective-permute-start.1 = (bf16[1,256,768]{2,1,0:T(8,128)(2,1)S(1)}, bf16[1,256,768]{2,1,0:T(8,128)(2,1)S(1)}, u32[]{:S(2)}, u32[]{:S(2)}) collective-permute-start(bf16[1,256,768]{2,1,0:T(8,128)(2,1)S(1)} %copy-done), channel_id=1, source_target_pairs={{0,256},{256,0},{1,257},{257,1},{2,258},{258,2},{3,259},{259,3},{4... | collective-permute-start | bytes 1179656 | tf_op jit(solution)/shard_map/ppermute | solution.py:521
  23.9 11.6 %copy-start.2 = (bf16[16,256]{1,0:T(8,128)(2,1)S(1)}, bf16[16,256]{1,0:T(8,128)(2,1)}, u32[]{:S(2)}) copy-start(bf16[16,256]{1,0:T(8,128)(2,1)} %cls.1) | copy-start | bytes 24580
  23.9 11.6 %copy-start.7 = (s32[4]{0:T(128)S(1)}, s32[4]{0:T(128)}, u32[]{:S(2)}) copy-start(s32[4]{0:T(128)} %slots.1) | copy-start | bytes 52
  23.9 11.6 %copy-start.3 = (s32[4,48]{1,0:T(4,128)S(1)}, s32[4,48]{1,0:T(4,128)}, u32[]{:S(2)}) copy-start(s32[4,48]{1,0:T(4,128)} %labels.1) | copy-start | bytes 2308
  24.0 11.5 %copy-start.5 = (f32[256]{0:T(256)S(1)}, f32[256]{0:T(256)}, u32[]{:S(2)}) copy-start(f32[256]{0:T(256)} %param.19) | copy-start | bytes 3076
  24.0 11.5 %copy-start.6 = (s32[4]{0:T(128)S(1)}, s32[4]{0:T(128)}, u32[]{:S(2)}) copy-start(s32[4]{0:T(128)} %counts.1) | copy-start | bytes 52
  66.4 4.3 %collective-permute-start.3 = (f32[32,16,128]{2,1,0:T(8,128)S(1)}, f32[32,16,128]{2,1,0:T(8,128)S(1)}, u32[]{:S(2)}, u32[]{:S(2)}) collective-permute-start(f32[32,16,128]{2,1,0:T(8,128)S(1)} %get-tuple-element.15), channel_id=1, source_target_pairs={{0,16},{16,0},{1,17},{17,1},{2,18},{18,2},{3,19},{19,3},{4,20},{20... | collective-permute-start | bytes 786440 | tf_op jit(solution)/shard_map/ppermute | solution.py:561
  124.7 9.2 %collective-permute-start.4 = (f32[16,72,128]{2,1,0:T(8,128)S(1)}, f32[16,72,128]{2,1,0:T(8,128)S(1)}, u32[]{:S(2)}, u32[]{:S(2)}) collective-permute-start(f32[16,72,128]{2,1,0:T(8,128)S(1)} %all_to_all.22.mine), channel_id=1, source_target_pairs={{0,16},{16,0},{1,17},{17,1},{2,18},{18,2},{3,19},{19,3},{4,20},{20... | collective-permute-start | bytes 1769480 | tf_op jit(solution)/shard_map/ppermute | solution.py:567

commit v5 on v4

--- a/solution.py
+++ b/solution.py
@@ -32,6 +32,7 @@
 SHARE = 4
 YS = 8
 OWNERS = 32
+CODE_TOP = 32000.0
 CHUNK = 72
 DP = ("y", "core")
 INNER = ("r", "b")
@@ -222,8 +223,9 @@
         e_dates = jnp.where(shown, raised, 0.0).reshape(SEQS, DATES, 128)
         e_class = e_cls[...]
         total = jnp.sum(e_dates, axis=1, keepdims=True) + jnp.sum(e_class, axis=0, keepdims=True)[None]
-        a_dates = e_dates / total
-        a_class = e_class[None] / total
+        total_inv = 1.0 / total
+        a_dates = e_dates * total_inv
+        a_class = e_class[None] * total_inv
         ad[rows, :] = a_dates.reshape(ROWS, 128)
         ac[rows, :] = a_class.reshape(ROWS, 128)
         v_class = v_t[ALL:, :]
@@ -263,15 +265,15 @@
         kn_s[rows, :] = kq_inv[:ROWS]
         qn_s[rows, :] = kq_inv[ROWS:]
         v_s[rows, :] = v
-        parts, held = [], []
-        for b in range(CLASS_CHUNK):
-            part = slice(b * PATCHES, b * PATCHES + PATCHES)
-            raised = jnp.exp(logits_t(k[part], q[part], masks))
-            a = raised / jnp.sum(raised, axis=0, keepdims=True)
-            held.append(a)
-            parts.append(gathered_heads(dot_tn(a.astype(BF16), v[part])))
-        a_s[rows, :] = stack(held)
-        att = stack(parts).astype(BF16)
+        part = [slice(b * PATCHES, b * PATCHES + PATCHES) for b in range(CLASS_CHUNK)]
+        raised = jnp.exp(stack([logits_t(k[p], q[p], masks) for p in part]))
+        raised = raised.reshape(CLASS_CHUNK, PATCHES, HEADS * PATCHES)
+        a = raised * (1.0 / jnp.sum(raised, axis=1, keepdims=True))
+        a = a.reshape(ROWS, HEADS * PATCHES)
+        a_s[rows, :] = a
+        a16 = a.astype(BF16)
+        wide = [dot_tn(a16[p], v[p]) for p in part]
+        att = stack([gathered_heads(m) for m in wide]).astype(BF16)
         att_s[rows, :] = att
         raw = jnp.sum(u * head[...] + att.astype(F32) * rows_s[0:1, :], axis=-1, keepdims=True)
         log_s[rows, :] = jnp.broadcast_to(CAP * jnp.tanh(raw / CAP), (ROWS, 128))
@@ -303,18 +305,19 @@
         k = k_s[rows, :]
         q = q_s[rows, :]
         a_all = a_s[rows, :]
-        dv_parts, dk_parts, dq_parts = [], [], []
-        for b in range(CLASS_CHUNK):
-            part = slice(b * PATCHES, b * PATCHES + PATCHES)
-            a = a_all[part]
-            wide = spread(d_att[part], masks)
-            da = rounded(dot_nt(v[part], wide))
-            dv_parts.append(dot(a.astype(BF16), wide).astype(BF16))
-            ds = SHARP * a * (da - jnp.sum(da * a, axis=0, keepdims=True))
-            q_hi, q_lo = spread_pair(q[part], masks)
-            dk_parts.append(three_pass(ds, q_hi, q_lo))
-            dq_parts.append(gathered_heads(three_pass_tn(ds, k[part])))
-        dv = stack(dv_parts)
+        part = [slice(b * PATCHES, b * PATCHES + PATCHES) for b in range(CLASS_CHUNK)]
+        a16 = a_all.astype(BF16)
+        da_parts, dv_parts = [], []
+        for p in part:
+            wide = spread(d_att[p], masks)
+            da_parts.append(dot_nt(v[p], wide))
+            dv_parts.append(dot(a16[p], wide))
+        dv = stack(dv_parts).astype(BF16)
+        cube = lambda m: m.reshape(CLASS_CHUNK, PATCHES, HEADS * PATCHES)
+        da, a = cube(rounded(stack(da_parts))), cube(a_all)
+        ds = (SHARP * a * (da - jnp.sum(da * a, axis=1, keepdims=True))).reshape(ROWS, HEADS * PATCHES)
+        dk_parts = [three_pass(ds[p], *spread_pair(q[p], masks)) for p in part]
+        dq_parts = [gathered_heads(m) for m in [three_pass_tn(ds[p], k[p]) for p in part]]
         unit = stack([k, q])
         scale = stack([kn_s[rows, :], qn_s[rows, :]])
         d_unit = stack(dk_parts + dq_parts)
@@ -463,20 +466,47 @@
 ]
 
 
+def encode(x, at):
+    rows = x.shape[1]
+    top = jnp.max(jnp.abs(x), axis=2, keepdims=True)
+    power = jnp.floor(jnp.log2(jnp.maximum(top, 1e-30))) + 1.0
+    coded = jnp.floor(x * (CODE_TOP * jnp.exp2(-power)) + 0.5)
+    eye = iota((1, rows, 128), 1) == iota((1, rows, 128), 2)
+    powers = jnp.sum(jnp.where(eye, power, 0.0), axis=1, keepdims=True)
+    coded = jnp.where(iota((1, rows, 128), 1) == at, powers, coded)
+    return coded.astype(I32).astype(jnp.int16)
+
+
+def decode(coded, at):
+    rows = coded.shape[1]
+    x = coded.astype(I32).astype(F32)
+    eye = iota((1, rows, 128), 1) == iota((1, rows, 128), 2)
+    power = jnp.sum(jnp.where(eye, x[:, at : at + 1, :], 0.0), axis=2, keepdims=True)
+    return x * (jnp.exp2(power) * (1.0 / CODE_TOP))
+
+
+def code_pair(keep, given, out):
+    out[...] = encode(keep[...] + given[...], 12)
+
+
 def reduce_tiles(parts, out):
-    out[...] = jnp.broadcast_to(jnp.sum(parts[...], axis=0)[None], (YS, 16, 128))
+    total = jnp.sum(decode(parts[...], 12), axis=0)
+    out[...] = jnp.broadcast_to(total[None], (YS, 16, 128))
 
 
 def assemble(blocks, out):
-    whole = stack([blocks[y, 0:8, :] for y in range(YS)] + [blocks[0, 8:16, :]])
-    out[...] = jnp.broadcast_to(whole[None], (MEMBERS, CHUNK, 128))
+    small = jnp.where(iota((8, 128), 0) < 4, blocks[0, 8:16, :], 0.0)
+    whole = stack([blocks[y, 0:8, :] for y in range(YS)] + [small])
+    out[...] = jnp.broadcast_to(encode(whole[None], 68), (MEMBERS, CHUNK, 128))
 
 
 def unpack(core, mine, other, loss, d_class, d_gain, d_qkv, d_out, d_head):
     lower = core[0] == 0
-    for b in range(SHARE):
-        for part in range(4):
-            own, far = mine[SHARE * part + b], other[SHARE * part + b]
+    for part in range(4):
+        spot = slice(SHARE * part, SHARE * part + SHARE)
+        owns, fars = decode(mine[spot], 68), decode(other[spot], 68)
+        for b in range(SHARE):
+            own, far = owns[b], fars[b]
             blocks = (jnp.where(lower, own, far), jnp.where(lower, far, own))
             for c in range(2):
                 for y in range(YS):
@@ -487,12 +517,13 @@
                     else:
                         d_out[0, row : row + 8, lane : lane + 128] = tile
             at = 4 * part + b
-            d_class[at : at + 1, :128] = own[64:65]
-            d_class[at : at + 1, 128:] = own[65:66]
+            small = blocks[0]
+            d_class[at : at + 1, :128] = small[64:65]
+            d_class[at : at + 1, 128:] = small[65:66]
             if b == 0 and part < 3:
                 ref = (d_gain, d_head, loss)[part]
-                ref[:, :128] = own[66:67]
-                ref[:, 128:] = own[67:68]
+                ref[:, :128] = small[66:67]
+                ref[:, 128:] = small[67:68]
 
 
 VM = pl.BlockSpec()
@@ -559,10 +590,11 @@
         scratch=STEP_SCRATCH,
     )
     given = lax.ppermute(give, "core", [(0, 1), (1, 0)])
-    parts = lax.all_to_all(keep + given, ("y", "b"), 0, 0, tiled=True)
+    (coded,) = call(code_pair, [VM, VM], [((OWNERS, 16, 128), jnp.int16)], keep, given)
+    parts = lax.all_to_all(coded, ("y", "b"), 0, 0, tiled=True)
     (total,) = call(reduce_tiles, [VM], [((YS, 16, 128), F32)], parts)
     blocks = lax.all_to_all(total, "y", 0, 0, tiled=True)
-    (whole,) = call(assemble, [VM], [((MEMBERS, CHUNK, 128), F32)], blocks)
+    (whole,) = call(assemble, [VM], [((MEMBERS, CHUNK, 128), jnp.int16)], blocks)
     mine = lax.all_to_all(whole, INNER, 0, 0, tiled=True)
     other = lax.ppermute(mine, "core", [(0, 1), (1, 0)])
     loss, d_class, d_gain, d_qkv, d_out, d_head = call(

time: 136 us -> 122 us (0.90)
  blocking collectives: 53.9 us -> 45.1 us
  Pallas kernels: 32 us -> 28.6 us
    all_to_all x1, blocking collectives: 22.6 us -> 16.3 us  [whole_step(): mine = lax.all_to_all(whole, INNER, 0, 0, tiled=True)]
    pallas_call x4 -> x5, Pallas kernels: 32 us -> 28.6 us  [call(): pl.pallas_call(body, out_shape=[jax.ShapeDtypeStruct(s, t) for s, t in ou...]
    all_to_all x1, blocking collectives: 21.4 us -> 19.2 us  [whole_step(): parts = lax.all_to_all(coded, ('y', 'b'), 0, 0, tiled=True)]
where the time goes in v5:
time: 122 us
  blocking collectives  45.1 us (37%)
  starting transfers between devices  30.8 us (25%)
  Pallas kernels  28.6 us (23%)
  waiting for transfers between devices  13.8 us (11%)
  local copies, waits for them, and re-layouts  2.3 us (2%)
    pallas_call x5, Pallas kernels, call(): pl.pallas_call(body, out_shape=[jax.ShapeDtypeStruct(s, t) for s, t in ou...  28.6 us
    all_to_all x1, blocking collectives, whole_step(): parts = lax.all_to_all(coded, ('y', 'b'), 0, 0, tiled=True)  19.2 us
    all_to_all x1, blocking collectives, whole_step(): mine = lax.all_to_all(whole, INNER, 0, 0, tiled=True)  16.3 us
    all_to_all x1, starting transfers between devices, whole_step(): whole_tile = lax.all_to_all(by_dest, INNER, 0, 0, tiled=True)  13.5 us
    ppermute x3, waiting for transfers between devices, swap(): return lax.ppermute(v, 'pipe', [(0, 1), (1, 0)])  11.5 us
    all_to_all x1, blocking collectives, whole_step(): blocks = lax.all_to_all(total, 'y', 0, 0, tiled=True)  9.67 us
    ppermute x3, starting transfers between devices, swap(): return lax.ppermute(v, 'pipe', [(0, 1), (1, 0)])  7.5 us
    ppermute x1, starting transfers between devices, whole_step(): other = lax.ppermute(mine, 'core', [(0, 1), (1, 0)])  6.56 us
  transfers between devices with their start and end apart: 6, of which 4 were waited for; matrix products, arithmetic and copies ran while one was open for 0% of the time, Pallas kernels for 0%

profile of v5, /device:TPU:1, one launch (start us, length us, event | category | flops | bytes accessed | tf_op | source)
XLA Modules:
  0.0 121.8 jit_solution(7062076602328701202)
XLA Ops:
  0.6 1.7 %tile.11 = bf16[4,4,48,256]{3,2,1,0:T(8,128)(2,1)} broadcast(bf16[4,48,256]{2,1,0:T(8,128)(2,1)} %bitcast.10), dimensions={1,2,3} | broadcast | bytes 491520 | tf_op jit(solution)/shard_map/tile | solution.py:569
  2.3 13.5 %all-to-all-start = ((bf16[16,48,256]{2,1,0:T(8,128)(2,1)}), bf16[16,48,256]{2,1,0:T(8,128)(2,1)S(1)}, u32[]{:S(2)}, u32[]{:S(2)}) async-start(bf16[16,48,256]{2,1,0:T(8,128)(2,1)} %bitcast.4), calls=%async_computation | async-start | bytes 786432 | tf_op jit(solution)/shard_map/all_to_all | solution.py:570
  15.9 2.2 %collective-permute-start = (f32[1,256]{1,0:T(1,128)S(1)}, f32[1,256]{1,0:T(1,128)S(1)}, u32[]{:S(2)}, u32[]{:S(2)}) collective-permute-start(f32[1,256]{1,0:T(1,128)S(1)} %copy-done.4), channel_id=1, source_target_pairs={{0,256},{256,0},{1,257},{257,1},{2,258},{258,2},{3,259},{259,3},{4... | collective-permute-start | bytes 3080 | tf_op jit(solution)/shard_map/ppermute | solution.py:552
  18.1 3.1 %collective-permute-start.2 = (bf16[1,256,256]{2,1,0:T(8,128)(2,1)S(1)}, bf16[1,256,256]{2,1,0:T(8,128)(2,1)S(1)}, u32[]{:S(2)}, u32[]{:S(2)}) collective-permute-start(bf16[1,256,256]{2,1,0:T(8,128)(2,1)S(1)} %copy-done.1), channel_id=1, source_target_pairs={{0,256},{256,0},{1,257},{257,1},{2,258},{258,2},{3,259},{259,3},{4... | collective-permute-start | bytes 393224 | tf_op jit(solution)/shard_map/ppermute | solution.py:552
  21.2 2.2 %collective-permute-start.1 = (bf16[1,256,768]{2,1,0:T(8,128)(2,1)S(1)}, bf16[1,256,768]{2,1,0:T(8,128)(2,1)S(1)}, u32[]{:S(2)}, u32[]{:S(2)}) collective-permute-start(bf16[1,256,768]{2,1,0:T(8,128)(2,1)S(1)} %copy-done), channel_id=1, source_target_pairs={{0,256},{256,0},{1,257},{257,1},{2,258},{258,2},{3,259},{259,3},{4... | collective-permute-start | bytes 1179656 | tf_op jit(solution)/shard_map/ppermute | solution.py:552
  23.5 0.1 mul.38
  23.6 0.3 fusion.enc
  23.9 0.0 copy-start.2
  23.9 0.1 pad_add_fusion.scal
  24.0 2.5 %collective-permute-done.2.wout_b = bf16[1,256,256]{2,1,0:T(8,128)(2,1)S(1)} collective-permute-done((bf16[1,256,256]{2,1,0:T(8,128)(2,1)S(1)}, bf16[1,256,256]{2,1,0:T(8,128)(2,1)S(1)}, u32[]{:S(2)}, u32[]{:S(2)}) %collective-permute-start.2) | collective-permute-done | bytes 131104 | tf_op jit(solution)/shard_map/ppermute | solution.py:552
  26.6 9.0 %collective-permute-done.1.wqkv_b = bf16[1,256,768]{2,1,0:T(8,128)(2,1)S(1)} collective-permute-done((bf16[1,256,768]{2,1,0:T(8,128)(2,1)S(1)}, bf16[1,256,768]{2,1,0:T(8,128)(2,1)S(1)}, u32[]{:S(2)}, u32[]{:S(2)}) %collective-permute-start.1) | collective-permute-done | bytes 393248 | tf_op jit(solution)/shard_map/ppermute | solution.py:552
  35.6 26.7 %shard_map.145 = (f32[32,16,128]{2,1,0:T(8,128)S(1)}, f32[32,16,128]{2,1,0:T(8,128)S(1)}) custom-call(s32[3]{0:T(128)S(1)} %pad_add_fusion.scal, s32[4]{0:T(128)S(1)} %copy-done.6, s32[4]{0:T(128)S(1)} %copy-done.7, s32[4,48]{1,0:T(4,128)S(1)} %copy-done.3, bf16[16,48,256]{2,1,0:T(8,128)(2,1)S(1)} %all-to-all-done.pix, f32[64,256]{1,0:T(8,128)S(1)} %fusion.enc, ...), custom_call_target="tpu_custom_call" | custom-call | tf_op jit(solution)/shard_map/pallas_call | solution.py:534
  62.3 3.2 %collective-permute-start.3 = (f32[32,16,128]{2,1,0:T(8,128)S(1)}, f32[32,16,128]{2,1,0:T(8,128)S(1)}, u32[]{:S(2)}, u32[]{:S(2)}) collective-permute-start(f32[32,16,128]{2,1,0:T(8,128)S(1)} %get-tuple-element.15), channel_id=1, source_target_pairs={{0,16},{16,0},{1,17},{17,1},{2,18},{18,2},{3,19},{19,3},{4,20},{20... | collective-permute-start | bytes 786440 | tf_op jit(solution)/shard_map/ppermute | solution.py:592
  65.5 1.1 collective-permute-done.3.given
  66.6 0.3 shard_map.146
  66.9 19.2 %all_to_all.20.parts = s16[32,16,128]{2,1,0:T(8,128)(2,1)S(1)} all-to-all(s16[32,16,128]{2,1,0:T(8,128)(2,1)S(1)} %shard_map.146), channel_id=1, replica_groups=mesh['pipe'=2,'y'=8,'core'=2,'r'=4,'b'=4] {'y','b'}, dimensions={0} | all-to-all | bytes 262144 | tf_op jit(solution)/shard_map/all_to_all | solution.py:594
  86.0 0.2 shard_map.147
  86.2 9.7 %all_to_all.21.blocks = f32[8,16,128]{2,1,0:T(8,128)S(1)} all-to-all(f32[8,16,128]{2,1,0:T(8,128)S(1)} %shard_map.147), channel_id=1, replica_groups=mesh['pipe'=2,'y'=8,'core'=2,'r'=4,'b'=4] {'y'}, dimensions={0} | all-to-all | bytes 131072 | tf_op jit(solution)/shard_map/all_to_all | solution.py:596
  95.9 0.1 shard_map.148
  96.0 16.3 %all_to_all.22.mine = s16[16,72,128]{2,1,0:T(8,128)(2,1)S(1)} all-to-all(s16[16,72,128]{2,1,0:T(8,128)(2,1)S(1)} %shard_map.148), channel_id=1, replica_groups=mesh['pipe'=2,'y'=8,'core'=2,'r'=4,'b'=4] {'r','b'}, dimensions={0} | all-to-all | bytes 589824 | tf_op jit(solution)/shard_map/all_to_all | solution.py:598
  112.3 6.6 %collective-permute-start.4 = (s16[16,72,128]{2,1,0:T(8,128)(2,1)S(1)}, s16[16,72,128]{2,1,0:T(8,128)(2,1)S(1)}, u32[]{:S(2)}, u32[]{:S(2)}) collective-permute-start(s16[16,72,128]{2,1,0:T(8,128)(2,1)S(1)} %all_to_all.22.mine), channel_id=1, source_target_pairs={{0,16},{16,0},{1,17},{17,1},{2,18},{18,2},{3,19},{19,3},{4,20},{20... | collective-permute-start | bytes 884744 | tf_op jit(solution)/shard_map/ppermute | solution.py:599
  118.8 1.2 collective-permute-done.4.other
  120.0 1.3 %shard_map.149 = (f32[1,256]{1,0:T(1,128)S(1)}, f32[16,256]{1,0:T(8,128)}, f32[1,256]{1,0:T(1,128)}, f32[1,256,768]{2,1,0:T(8,128)}, f32[1,256,256]{2,1,0:T(8,128)}, /*index=5*/f32[1,256]{1,0:T(1,128)}) custom-call(s32[1]{0:T(128)} %bitcast.core, s16[16,72,128]{2,1,0:T(8,128)(2,1)S(1)} %all_to_all.22.mine, s16[16,72,128]{2,1,0:T(8,128)(2,1)S(1)} %collective-permute-done.4.other), custom_call_target="tpu_custom_call" | custom-call | tf_op jit(solution)/shard_map/pallas_call | solution.py:534
  121.3 0.5 slice_bitcast_fusion
  (22 shorter events, 0.1 us)
Async XLA Ops:
  2.3 13.6 %copy-start.4 = (f32[1,256]{1,0:T(1,128)S(1)}, f32[1,256]{1,0:T(1,128)}, u32[]{:S(2)}) copy-start(f32[1,256]{1,0:T(1,128)} %gain_a.1) | copy-start | bytes 3076
  2.3 15.8 %copy-start.1 = (bf16[1,256,256]{2,1,0:T(8,128)(2,1)S(1)}, bf16[1,256,256]{2,1,0:T(8,128)(2,1)}, u32[]{:S(2)}) copy-start(bf16[1,256,256]{2,1,0:T(8,128)(2,1)} %wout_a.1) | copy-start | bytes 393220
  2.3 18.9 %copy-start = (bf16[1,256,768]{2,1,0:T(8,128)(2,1)S(1)}, bf16[1,256,768]{2,1,0:T(8,128)(2,1)}, u32[]{:S(2)}) copy-start(bf16[1,256,768]{2,1,0:T(8,128)(2,1)} %wqkv_a.1) | copy-start | bytes 1179652
  2.3 33.2 %all-to-all-start = ((bf16[16,48,256]{2,1,0:T(8,128)(2,1)}), bf16[16,48,256]{2,1,0:T(8,128)(2,1)S(1)}, u32[]{:S(2)}, u32[]{:S(2)}) async-start(bf16[16,48,256]{2,1,0:T(8,128)(2,1)} %bitcast.4), calls=%async_computation | async-start | bytes 786432 | tf_op jit(solution)/shard_map/all_to_all | solution.py:570
  15.9 7.6 %copy-start.8 = (s32[4,16]{1,0:T(4,128)S(1)}, s32[4,16]{1,0:T(4,128)}, u32[]{:S(2)}) copy-start(s32[4,16]{1,0:T(4,128)} %param.11) | copy-start | bytes 772
  15.9 8.1 %collective-permute-start = (f32[1,256]{1,0:T(1,128)S(1)}, f32[1,256]{1,0:T(1,128)S(1)}, u32[]{:S(2)}, u32[]{:S(2)}) collective-permute-start(f32[1,256]{1,0:T(1,128)S(1)} %copy-done.4), channel_id=1, source_target_pairs={{0,256},{256,0},{1,257},{257,1},{2,258},{258,2},{3,259},{259,3},{4... | collective-permute-start | bytes 3080 | tf_op jit(solution)/shard_map/ppermute | solution.py:552
  18.1 8.4 %collective-permute-start.2 = (bf16[1,256,256]{2,1,0:T(8,128)(2,1)S(1)}, bf16[1,256,256]{2,1,0:T(8,128)(2,1)S(1)}, u32[]{:S(2)}, u32[]{:S(2)}) collective-permute-start(bf16[1,256,256]{2,1,0:T(8,128)(2,1)S(1)} %copy-done.1), channel_id=1, source_target_pairs={{0,256},{256,0},{1,257},{257,1},{2,258},{258,2},{3,259},{259,3},{4... | collective-permute-start | bytes 393224 | tf_op jit(solution)/shard_map/ppermute | solution.py:552
  21.2 14.3 %collective-permute-start.1 = (bf16[1,256,768]{2,1,0:T(8,128)(2,1)S(1)}, bf16[1,256,768]{2,1,0:T(8,128)(2,1)S(1)}, u32[]{:S(2)}, u32[]{:S(2)}) collective-permute-start(bf16[1,256,768]{2,1,0:T(8,128)(2,1)S(1)} %copy-done), channel_id=1, source_target_pairs={{0,256},{256,0},{1,257},{257,1},{2,258},{258,2},{3,259},{259,3},{4... | collective-permute-start | bytes 1179656 | tf_op jit(solution)/shard_map/ppermute | solution.py:552
  23.9 11.6 %copy-start.2 = (bf16[16,256]{1,0:T(8,128)(2,1)S(1)}, bf16[16,256]{1,0:T(8,128)(2,1)}, u32[]{:S(2)}) copy-start(bf16[16,256]{1,0:T(8,128)(2,1)} %cls.1) | copy-start | bytes 24580
  23.9 11.6 %copy-start.7 = (s32[4]{0:T(128)S(1)}, s32[4]{0:T(128)}, u32[]{:S(2)}) copy-start(s32[4]{0:T(128)} %slots.1) | copy-start | bytes 52
  23.9 11.6 %copy-start.3 = (s32[4,48]{1,0:T(4,128)S(1)}, s32[4,48]{1,0:T(4,128)}, u32[]{:S(2)}) copy-start(s32[4,48]{1,0:T(4,128)} %labels.1) | copy-start | bytes 2308
  24.0 11.5 %copy-start.5 = (f32[256]{0:T(256)S(1)}, f32[256]{0:T(256)}, u32[]{:S(2)}) copy-start(f32[256]{0:T(256)} %param.19) | copy-start | bytes 3076
  24.0 11.5 %copy-start.6 = (s32[4]{0:T(128)S(1)}, s32[4]{0:T(128)}, u32[]{:S(2)}) copy-start(s32[4]{0:T(128)} %counts.1) | copy-start | bytes 52
  62.3 4.3 %collective-permute-start.3 = (f32[32,16,128]{2,1,0:T(8,128)S(1)}, f32[32,16,128]{2,1,0:T(8,128)S(1)}, u32[]{:S(2)}, u32[]{:S(2)}) collective-permute-start(f32[32,16,128]{2,1,0:T(8,128)S(1)} %get-tuple-element.15), channel_id=1, source_target_pairs={{0,16},{16,0},{1,17},{17,1},{2,18},{18,2},{3,19},{19,3},{4,20},{20... | collective-permute-start | bytes 786440 | tf_op jit(solution)/shard_map/ppermute | solution.py:592
  112.3 7.8 %collective-permute-start.4 = (s16[16,72,128]{2,1,0:T(8,128)(2,1)S(1)}, s16[16,72,128]{2,1,0:T(8,128)(2,1)S(1)}, u32[]{:S(2)}, u32[]{:S(2)}) collective-permute-start(s16[16,72,128]{2,1,0:T(8,128)(2,1)S(1)} %all_to_all.22.mine), channel_id=1, source_target_pairs={{0,16},{16,0},{1,17},{17,1},{2,18},{18,2},{3,19},{19,3},{4,20},{20... | collective-permute-start | bytes 884744 | tf_op jit(solution)/shard_map/ppermute | solution.py:599

commit v6 on v5

--- a/solution.py
+++ b/solution.py
@@ -100,26 +100,16 @@
     return SHARP * (both[:n] + both[n:] + dot_nt(k_hi, q_lo))
 
 
-def three_pass(x, w_hi, w_lo):
-    n = x.shape[0]
-    x_hi, x_lo = split(x)
+def three_pass(x_hi, x_lo, w_hi, w_lo):
+    n = x_hi.shape[0]
     both = dot(jnp.concatenate([x_hi, x_lo], axis=0), w_hi)
     return both[:n] + both[n:] + dot(x_hi, w_lo)
 
 
-def three_pass_tn(x, y):
-    x_hi, x_lo = split(x)
-    y_hi, y_lo = split(y)
+def three_pass_tn(x_hi, x_lo, y_hi, y_lo):
     return dot_tn(
         jnp.concatenate([x_hi, x_hi, x_lo], axis=0), jnp.concatenate([y_hi, y_lo, y_hi], axis=0)
     )
-
-
-def wide_dot_nt(x, w):
-    n = x.shape[0]
-    hi, lo = split(x)
-    both = dot_nt(jnp.concatenate([hi, lo], axis=0), w)
-    return both[:n] + both[n:]
 
 
 def stack(parts):
@@ -151,10 +141,10 @@
 
 
 def step(
-    scal, counts, slots, labels, pix, enc, cls, gain_a, gain_b, wqkv_a, wqkv_b, wout_a, wout_b, head, keep, give, *scratch
+    scal, counts, slots, labels, pix, enc, cls, gain_a, gain_b, wqkv_a, wout_a, half_a, half_b, head, keep, give, *scratch
 ):
     (wt, ws, ot, os, seq_a, seq_b, xhat_t, normed_t, k_t, kn_t, v_t, ad, ac, att_t, q_t, qn_t, e_cls, inv_c,
-     u_s, xhat_s, normed_s, inv_s, k_s, kn_s, q_s, qn_s, v_s, a_s, att_s, log_s, tot, rows_s, y_hi, y_lo,
+     u_s, xhat_s, normed_s, inv_s, k_s, kn_s, q_s, qn_s, v_s, a_s, att_s, log_s, tot, rows_s, y_w,
      acc_q, acc_k, acc_v, acc_n, acc_g, d_cls, masks) = scratch
     first = scal[1] == 1
     tile = scal[0] & 3
@@ -164,10 +154,13 @@
     lane_head = iota((PATCHES, D), 1) >> 5
     for h in range(HEADS):
         masks[h] = jnp.where(lane_head == h, 1.0, 0.0).astype(BF16)
-    wt[...] = jnp.where(first, wqkv_a[0], wqkv_b[0])
-    ws[...] = jnp.where(first, wqkv_b[0], wqkv_a[0])
-    ot[...] = jnp.where(first, wout_a[0], wout_b[0])
-    os[...] = jnp.where(first, wout_b[0], wout_a[0])
+    for i in range(2):
+        at = slice(128 * i, 128 * i + 128)
+        far = jnp.where(scal[2] == i, half_a[...], half_b[...])
+        wt[at, :] = jnp.where(first, wqkv_a[0, at, :], far[:, : 3 * D])
+        ws[at, :] = jnp.where(first, far[:, : 3 * D], wqkv_a[0, at, :])
+        ot[at, :] = jnp.where(first, wout_a[0, at, :], far[:, 3 * D :])
+        os[at, :] = jnp.where(first, far[:, 3 * D :], wout_a[0, at, :])
     gain_t = jnp.where(first, gain_a[...], gain_b[...])
     gain_s = jnp.where(first, gain_b[...], gain_a[...])
     head_row = head[...]
@@ -316,22 +309,23 @@
         cube = lambda m: m.reshape(CLASS_CHUNK, PATCHES, HEADS * PATCHES)
         da, a = cube(rounded(stack(da_parts))), cube(a_all)
         ds = (SHARP * a * (da - jnp.sum(da * a, axis=1, keepdims=True))).reshape(ROWS, HEADS * PATCHES)
-        dk_parts = [three_pass(ds[p], *spread_pair(q[p], masks)) for p in part]
-        dq_parts = [gathered_heads(m) for m in [three_pass_tn(ds[p], k[p]) for p in part]]
+        d_hi, d_lo = split(ds)
+        k_hi, k_lo = split(k)
+        dk_parts = [three_pass(d_hi[p], d_lo[p], *spread_pair(q[p], masks)) for p in part]
+        wide = [three_pass_tn(d_hi[p], d_lo[p], k_hi[p], k_lo[p]) for p in part]
+        dq_parts = [gathered_heads(m) for m in wide]
         unit = stack([k, q])
         scale = stack([kn_s[rows, :], qn_s[rows, :]])
         d_unit = stack(dk_parts + dq_parts)
         d_raw = scale * (d_unit - unit * head_sums(d_unit * unit, head_ones()))
         dk_raw, dq_raw = d_raw[:ROWS], d_raw[ROWS:]
         c_v = rounded(dot_nt(dv, ws[:, 2 * D :]))
-        c_k = rounded(wide_dot_nt(dk_raw, ws[:, D : 2 * D]))
-        c_q = rounded(wide_dot_nt(dq_raw, ws[:, :D]))
+        dk16, dq16 = dk_raw.astype(BF16), dq_raw.astype(BF16)
+        c_k = rounded(dot_nt(dk16, ws[:, D : 2 * D]))
+        c_q = rounded(dot_nt(dq16, ws[:, :D]))
         dn = rounded(rounded(c_v + c_k) + c_q)
         rows_s[4:5, :] += jnp.sum(dn * xhat, axis=0, keepdims=True)
-        y = jnp.where(share == 0, dq_raw, jnp.where(share == 1, dk_raw, dv.astype(F32)))
-        hi, lo = split(y)
-        y_hi[rows, :] = hi
-        y_lo[rows, :] = lo
+        y_w[rows, :] = jnp.where(share == 0, dq16, jnp.where(share == 1, dk16, dv))
         z = dn * rows_s[7:8, :]
         dx = inv_s[rows, 0:1] * (z - xhat * jnp.mean(z * xhat, axis=-1, keepdims=True))
         u_s[rows, :] = rounded(d_raw_logit * head[...] + dx)
@@ -350,7 +344,7 @@
     @pl.when(jnp.logical_and(scal[1] == 0, share < 3))
     def _():
         x = normed_s[...]
-        d_w = dot_tn(x, y_hi[0:ALL, :]) + dot_tn(x, y_lo[0:ALL, :])
+        d_w = dot_tn(x, y_w[0:ALL, :])
         put_tiles(keep, give, lower, d_w)
 
     @pl.when(jnp.logical_and(scal[1] == 0, share == 3))
@@ -390,12 +384,16 @@
         ds_c = SHARP * cube(a_class) * (cube(da_c) - both)
         ds_d = SHARP * cube(a_dates) * (cube(da_d) - both)
         q_hi, q_lo = spread_pair(q, masks)
-        dk = three_pass(stack([ds_d.reshape(ROWS, 128), ds_c.reshape(ROWS, 128)]), q_hi, q_lo)
+        d_hi, d_lo = split(stack([ds_d.reshape(ROWS, 128), ds_c.reshape(ROWS, 128)]))
+        dk = three_pass(d_hi, d_lo, q_hi, q_lo)
+        k_hi, k_lo = split(k)
+        kc_hi, kc_lo = split(k_class)
         dq_parts = []
         for s in range(SEQS):
-            ds_s = stack([ds_c[s], ds_d[s]])
-            k_all = stack([k_class, k[s * 16 : s * 16 + 16]])
-            dq_parts.append(gathered_heads(three_pass_tn(ds_s, k_all)))
+            at, far = slice(s * 16, s * 16 + 16), slice(ROWS + s * 16, ROWS + s * 16 + 16)
+            ds_s = [stack([m[at], m[far]]) for m in (d_hi, d_lo)]
+            k_all = [stack([k_hi[at], kc_hi]), stack([k_lo[at], kc_lo])]
+            dq_parts.append(gathered_heads(three_pass_tn(*ds_s, *k_all)))
         unit = stack([k] + [k_class] * SEQS + [q] * SEQS)
         scale = stack([kn_t[rows, :]] + [kn_t[ALL:, :]] * SEQS + [qn_t[...]] * SEQS)
         d_unit = stack([dk] + dq_parts)
@@ -403,8 +401,9 @@
         dk_raw, dq_raw = d_raw[: 2 * ROWS], d_raw[2 * ROWS :]
         dv = stack(dv_dates + dv_class)
         c_v = rounded(dot_nt(dv, wt[:, 2 * D :]))
-        c_k = rounded(wide_dot_nt(dk_raw, wt[:, D : 2 * D]))
-        c_q = rounded(wide_dot_nt(dq_raw, wt[:, :D]))
+        dk16 = dk_raw.astype(BF16)
+        c_k = rounded(dot_nt(dk16, wt[:, D : 2 * D]))
+        c_q = rounded(dot_nt(dq_raw.astype(BF16), wt[:, :D]))
         dn = rounded(c_v + c_k)
         rows_s[3:4, :] += jnp.sum(dn[:ROWS] * xhat_t[rows, :], axis=0, keepdims=True)
         acc_n[...] += fold(rounded(dn[ROWS:] + c_q))
@@ -412,14 +411,12 @@
         acc_q[...] += fold(dq_raw)
         acc_k[...] += fold(dk_raw[ROWS:])
         acc_v[...] += fold(dv[ROWS:].astype(F32))
-        of_dates = jnp.where(share == 1, dk_raw[:ROWS], dv[:ROWS].astype(F32))
-        y = jnp.where(share == 0, 0.0, jnp.where(share == 3, g.astype(F32), of_dates))
-        hi, lo = split(y)
+        of_dates = jnp.where(share == 1, dk16[:ROWS], dv[:ROWS])
+        y = jnp.where(share == 3, g, jnp.where(share == 0, jnp.zeros_like(g), of_dates))
 
         @pl.when(first)
         def _():
-            y_hi[rows, :] = hi
-            y_lo[rows, :] = lo
+            y_w[rows, :] = y
 
     dn_c = acc_n[...]
     xhat_c = xhat_t[ALL:, :]
@@ -433,15 +430,13 @@
     def _():
         y = jnp.where(share == 0, acc_q[...], jnp.where(share == 1, acc_k[...], acc_v[...]))
         hi, lo = split(y)
-        y_hi[ALL:, :] = hi
-        y_lo[ALL:, :] = lo
-        x = normed_t[...]
-        d_w = dot_tn(x, y_hi[...]) + dot_tn(x, y_lo[...])
+        y_w[ALL:, :] = hi
+        d_w = dot_tn(normed_t[...], y_w[...]) + dot_tn(normed_t[ALL:, :], lo)
         put_tiles(keep, give, lower, d_w)
 
     @pl.when(jnp.logical_and(first, share == 3))
     def _():
-        put_tiles(keep, give, lower, dot_tn(att_t[...], y_hi[0:ALL, :]))
+        put_tiles(keep, give, lower, dot_tn(att_t[...], y_w[0:ALL, :]))
 
     misc = jnp.where(share == 0, gain_grad, jnp.where(share == 1, d_head, rows_s[5:6, :]))
     for b in range(SHARE):
@@ -460,7 +455,7 @@
     ((ALL, D), F32), ((ALL, D), F32), ((ALL, D), BF16), ((ALL, 128), F32),
     ((ALL, D), F32), ((ALL, D), F32), ((ALL, D), F32), ((ALL, D), F32), ((ALL, D), BF16),
     ((ALL, HEADS * PATCHES), F32), ((ALL, D), BF16), ((ALL, 128), F32), ((PATCHES, 128), F32), ((8, D), F32),
-    ((ALL + 16, D), BF16), ((ALL + 16, D), BF16),
+    ((ALL + 16, D), BF16),
     ((16, D), F32), ((16, D), F32), ((16, D), F32), ((16, D), F32), ((16, D), F32), ((16, D), F32),
     ((HEADS, PATCHES, D), BF16),
 ]
@@ -483,6 +478,21 @@
     eye = iota((1, rows, 128), 1) == iota((1, rows, 128), 2)
     power = jnp.sum(jnp.where(eye, x[:, at : at + 1, :], 0.0), axis=2, keepdims=True)
     return x * (jnp.exp2(power) * (1.0 / CODE_TOP))
+
+
+def prepare(core, pixels, wqkv, wout, half, by_dest, sems):
+    rows = pl.ds(pl.multiple_of(core[0] * 128, 128), 128)
+    copies = [
+        pltpu.make_async_copy(wqkv.at[0, rows, :], half.at[:, 0 : 3 * D], sems.at[0]),
+        pltpu.make_async_copy(wout.at[0, rows, :], half.at[:, 3 * D : 4 * D], sems.at[1]),
+    ]
+    for r in range(SHARE):
+        to = by_dest.at[pl.ds(TILES_DEV * r, TILES_DEV)]
+        copies.append(pltpu.make_async_copy(pixels, to, sems.at[2 + r]))
+    for copy in copies:
+        copy.start()
+    for copy in copies:
+        copy.wait()
 
 
 def code_pair(keep, given, out):
@@ -566,9 +576,22 @@
 ):
     first = (lax.axis_index("pipe") == 0).astype(I32)
     inner = lax.axis_index(INNER).astype(I32)
-    by_dest = jnp.tile(pixels.reshape(TILES_DEV, PATCHES, D), (SHARE, 1, 1))
+    core = lax.axis_index("core").astype(I32)
+    any_space = pl.BlockSpec(memory_space=pl.ANY)
+    half, by_dest = pl.pallas_call(
+        prepare,
+        out_shape=[
+            jax.ShapeDtypeStruct((128, 4 * D), BF16),
+            jax.ShapeDtypeStruct((MEMBERS, PATCHES, D), BF16),
+        ],
+        in_specs=[SM, any_space, any_space, any_space],
+        out_specs=[any_space] * 2,
+        scratch_shapes=[pltpu.SemaphoreType.DMA((6,))],
+        name="prepare",
+    )(core[None], pixels.reshape(TILES_DEV, PATCHES, D), wqkv, wout)
     whole_tile = lax.all_to_all(by_dest, INNER, 0, 0, tiled=True)
-    core = lax.axis_index("core").astype(I32)
+    half = swap(half)
+    other_half = lax.ppermute(half, "core", [(0, 1), (1, 0)])
     keep, give = call(
         step,
         [SM] * 3 + [VM] * 11,
@@ -583,9 +606,9 @@
         section_gain,
         swap(section_gain),
         wqkv,
-        swap(wqkv),
         wout,
-        swap(wout),
+        half,
+        other_half,
         head_vec.reshape(1, D),
         scratch=STEP_SCRATCH,
     )

time: 122 us -> 137 us (1.12)
  Pallas kernels: 28.6 us -> 48.6 us
  waiting for transfers between devices: 13.8 us -> 8.67 us
    pallas_call x0 -> x1, Pallas kernels: none -> 21 us  [whole_step(): pl.pallas_call(prepare, out_shape=[jax.ShapeDtypeStruct((128, 4 * D), BF1...]
    ppermute x3 -> x2, waiting for transfers between devices: 11.5 us -> 5.64 us  [swap(): return lax.ppermute(v, 'pipe', [(0, 1), (1, 0)])]
    ppermute x0 -> x1, starting transfers between devices: none -> 3.94 us  [whole_step(): other_half = lax.ppermute(half, 'core', [(0, 1), (1, 0)])]
    ppermute x3 -> x2, starting transfers between devices: 7.5 us -> 5.28 us  [swap(): return lax.ppermute(v, 'pipe', [(0, 1), (1, 0)])]
    another operation x1 -> x0, local copies, waits for them, and re-layouts: 1.66 us -> none  [whole_step(): by_dest = jnp.tile(pixels.reshape(TILES_DEV, PATCHES, D), (SHARE, 1, 1))]
where the time goes in v6:
time: 137 us; the launch traced here: 136 us
  Pallas kernels  48.6 us (35%)
  blocking collectives  44.9 us (33%)
  starting transfers between devices  31.6 us (23%)
  waiting for transfers between devices  8.67 us (6%)
    pallas_call x5, Pallas kernels, call(): pl.pallas_call(body, out_shape=[jax.ShapeDtypeStruct(s, t) for s, t in ou...  27.6 us
    pallas_call x1, Pallas kernels, whole_step(): pl.pallas_call(prepare, out_shape=[jax.ShapeDtypeStruct((128, 4 * D), BF1...  21 us
    all_to_all x1, blocking collectives, whole_step(): parts = lax.all_to_all(coded, ('y', 'b'), 0, 0, tiled=True)  19.5 us
    all_to_all x1, blocking collectives, whole_step(): mine = lax.all_to_all(whole, INNER, 0, 0, tiled=True)  15.8 us
    all_to_all x1, starting transfers between devices, whole_step(): whole_tile = lax.all_to_all(by_dest, INNER, 0, 0, tiled=True)  13.6 us
    all_to_all x1, blocking collectives, whole_step(): blocks = lax.all_to_all(total, 'y', 0, 0, tiled=True)  9.67 us
    ppermute x1, starting transfers between devices, whole_step(): other = lax.ppermute(mine, 'core', [(0, 1), (1, 0)])  6.56 us
    ppermute x2, waiting for transfers between devices, swap(): return lax.ppermute(v, 'pipe', [(0, 1), (1, 0)])  5.64 us
  transfers between devices with their start and end apart: 6, of which 4 were waited for; matrix products, arithmetic and copies ran while one was open for 0% of the time, Pallas kernels for 0%

profile of v6, /device:TPU:1, one launch (start us, length us, event | category | flops | bytes accessed | tf_op | source)
XLA Modules:
  0.0 136.4 jit_solution(8447682617440941194)
XLA Ops:
  0.6 21.0 %prepare.1 = (bf16[128,1024]{1,0:T(8,128)(2,1)}, bf16[16,48,256]{2,1,0:T(8,128)(2,1)}) custom-call(s32[1]{0:T(128)} %bitcast.core, bf16[4,48,256]{2,1,0:T(8,128)(2,1)} %bitcast.9, bf16[1,256,768]{2,1,0:T(8,128)(2,1)} %wqkv_a.1, bf16[1,256,256]{2,1,0:T(8,128)(2,1)} %wout_a.1), custom_call_target="tpu_custom_call" | custom-call | tf_op jit(solution)/shard_map/prepare/pallas_call | solution.py:581
  21.7 13.6 %all-to-all-start = ((bf16[16,48,256]{2,1,0:T(8,128)(2,1)}), bf16[16,48,256]{2,1,0:T(8,128)(2,1)S(1)}, u32[]{:S(2)}, u32[]{:S(2)}) async-start(bf16[16,48,256]{2,1,0:T(8,128)(2,1)} %get-tuple-element.16), calls=%async_computation | async-start | bytes 786432 | tf_op jit(solution)/shard_map/all_to_all | solution.py:592
  35.3 2.2 %collective-permute-start.1 = (bf16[128,1024]{1,0:T(8,128)(2,1)S(1)}, bf16[128,1024]{1,0:T(8,128)(2,1)S(1)}, u32[]{:S(2)}, u32[]{:S(2)}) collective-permute-start(bf16[128,1024]{1,0:T(8,128)(2,1)S(1)} %copy-done.9), channel_id=1, source_target_pairs={{0,256},{256,0},{1,257},{257,1},{2,258},{258,2},{3,259},{259,3},{4... | collective-permute-start | bytes 786440 | tf_op jit(solution)/shard_map/ppermute | solution.py:562
  37.5 3.1 %collective-permute-start = (f32[1,256]{1,0:T(1,128)S(1)}, f32[1,256]{1,0:T(1,128)S(1)}, u32[]{:S(2)}, u32[]{:S(2)}) collective-permute-start(f32[1,256]{1,0:T(1,128)S(1)} %copy-done.4), channel_id=1, source_target_pairs={{0,256},{256,0},{1,257},{257,1},{2,258},{258,2},{3,259},{259,3},{4... | collective-permute-start | bytes 3080 | tf_op jit(solution)/shard_map/ppermute | solution.py:562
  40.6 0.7 copy-done.8
  41.3 0.1 mul.38
  41.4 5.6 %collective-permute-done.1.half_a = bf16[128,1024]{1,0:T(8,128)(2,1)S(1)} collective-permute-done((bf16[128,1024]{1,0:T(8,128)(2,1)S(1)}, bf16[128,1024]{1,0:T(8,128)(2,1)S(1)}, u32[]{:S(2)}, u32[]{:S(2)}) %collective-permute-start.1) | collective-permute-done | bytes 262176 | tf_op jit(solution)/shard_map/ppermute | solution.py:562
  47.0 3.9 %collective-permute-start.2 = (bf16[128,1024]{1,0:T(8,128)(2,1)S(1)}, bf16[128,1024]{1,0:T(8,128)(2,1)S(1)}, u32[]{:S(2)}, u32[]{:S(2)}) collective-permute-start(bf16[128,1024]{1,0:T(8,128)(2,1)S(1)} %collective-permute-done.1.half_a), channel_id=1, source_target_pairs={{0,16},{16,0},{1,17},{17,1},{2,18},{18,2},{3,19},{19,3},{4,20},{20... | collective-permute-start | bytes 786440 | tf_op jit(solution)/shard_map/ppermute | solution.py:594
  51.0 0.3 fusion.enc
  51.3 0.1 pad_add_fusion.scal
  51.4 0.7 collective-permute-done.2.half_b
  52.2 25.8 %shard_map.145 = (f32[32,16,128]{2,1,0:T(8,128)S(1)}, f32[32,16,128]{2,1,0:T(8,128)S(1)}) custom-call(s32[3]{0:T(128)S(1)} %pad_add_fusion.scal, s32[4]{0:T(128)S(1)} %copy-done.6, s32[4]{0:T(128)S(1)} %copy-done.7, s32[4,48]{1,0:T(4,128)S(1)} %copy-done.3, bf16[16,48,256]{2,1,0:T(8,128)(2,1)S(1)} %all-to-all-done.pix, f32[64,256]{1,0:T(8,128)S(1)} %fusion.enc, ...), custom_call_target="tpu_custom_call" | custom-call | tf_op jit(solution)/shard_map/pallas_call | solution.py:544
  78.0 2.3 %collective-permute-start.3 = (f32[32,16,128]{2,1,0:T(8,128)S(1)}, f32[32,16,128]{2,1,0:T(8,128)S(1)}, u32[]{:S(2)}, u32[]{:S(2)}) collective-permute-start(f32[32,16,128]{2,1,0:T(8,128)S(1)} %get-tuple-element.19), channel_id=1, source_target_pairs={{0,16},{16,0},{1,17},{17,1},{2,18},{18,2},{3,19},{19,3},{4,20},{20... | collective-permute-start | bytes 786440 | tf_op jit(solution)/shard_map/ppermute | solution.py:615
  80.3 1.1 collective-permute-done.3.given
  81.4 0.3 shard_map.146
  81.6 19.5 %all_to_all.20.parts = s16[32,16,128]{2,1,0:T(8,128)(2,1)S(1)} all-to-all(s16[32,16,128]{2,1,0:T(8,128)(2,1)S(1)} %shard_map.146), channel_id=1, replica_groups=mesh['pipe'=2,'y'=8,'core'=2,'r'=4,'b'=4] {'y','b'}, dimensions={0} | all-to-all | bytes 262144 | tf_op jit(solution)/shard_map/all_to_all | solution.py:617
  101.1 0.2 shard_map.147
  101.3 9.7 %all_to_all.21.blocks = f32[8,16,128]{2,1,0:T(8,128)S(1)} all-to-all(f32[8,16,128]{2,1,0:T(8,128)S(1)} %shard_map.147), channel_id=1, replica_groups=mesh['pipe'=2,'y'=8,'core'=2,'r'=4,'b'=4] {'y'}, dimensions={0} | all-to-all | bytes 131072 | tf_op jit(solution)/shard_map/all_to_all | solution.py:619
  111.0 0.1 shard_map.148
  111.1 15.8 %all_to_all.22.mine = s16[16,72,128]{2,1,0:T(8,128)(2,1)S(1)} all-to-all(s16[16,72,128]{2,1,0:T(8,128)(2,1)S(1)} %shard_map.148), channel_id=1, replica_groups=mesh['pipe'=2,'y'=8,'core'=2,'r'=4,'b'=4] {'r','b'}, dimensions={0} | all-to-all | bytes 589824 | tf_op jit(solution)/shard_map/all_to_all | solution.py:621
  126.8 6.6 %collective-permute-start.4 = (s16[16,72,128]{2,1,0:T(8,128)(2,1)S(1)}, s16[16,72,128]{2,1,0:T(8,128)(2,1)S(1)}, u32[]{:S(2)}, u32[]{:S(2)}) collective-permute-start(s16[16,72,128]{2,1,0:T(8,128)(2,1)S(1)} %all_to_all.22.mine), channel_id=1, source_target_pairs={{0,16},{16,0},{1,17},{17,1},{2,18},{18,2},{3,19},{19,3},{4,20},{20... | collective-permute-start | bytes 884744 | tf_op jit(solution)/shard_map/ppermute | solution.py:622
  133.4 1.2 collective-permute-done.4.other
  134.6 1.3 shard_map.149
  135.9 0.5 slice_bitcast_fusion
  (24 shorter events, 0.1 us)
Async XLA Ops:
  21.7 13.6 %copy-start.9 = (bf16[128,1024]{1,0:T(8,128)(2,1)S(1)}, bf16[128,1024]{1,0:T(8,128)(2,1)}, u32[]{:S(2)}) copy-start(bf16[128,1024]{1,0:T(8,128)(2,1)} %get-tuple-element.17) | copy-start | bytes 786436
  21.7 30.5 %copy-start = (bf16[1,256,768]{2,1,0:T(8,128)(2,1)S(1)}, bf16[1,256,768]{2,1,0:T(8,128)(2,1)}, u32[]{:S(2)}) copy-start(bf16[1,256,768]{2,1,0:T(8,128)(2,1)} %wqkv_a.1) | copy-start | bytes 1179652
  21.7 30.4 %copy-start.1 = (bf16[1,256,256]{2,1,0:T(8,128)(2,1)S(1)}, bf16[1,256,256]{2,1,0:T(8,128)(2,1)}, u32[]{:S(2)}) copy-start(bf16[1,256,256]{2,1,0:T(8,128)(2,1)} %wout_a.1) | copy-start | bytes 393220
  21.7 30.4 %all-to-all-start = ((bf16[16,48,256]{2,1,0:T(8,128)(2,1)}), bf16[16,48,256]{2,1,0:T(8,128)(2,1)S(1)}, u32[]{:S(2)}, u32[]{:S(2)}) async-start(bf16[16,48,256]{2,1,0:T(8,128)(2,1)} %get-tuple-element.16), calls=%async_computation | async-start | bytes 786432 | tf_op jit(solution)/shard_map/all_to_all | solution.py:592
  35.3 2.3 %copy-start.4 = (f32[1,256]{1,0:T(1,128)S(1)}, f32[1,256]{1,0:T(1,128)}, u32[]{:S(2)}) copy-start(f32[1,256]{1,0:T(1,128)} %gain_a.1) | copy-start | bytes 3076
  35.3 11.7 %collective-permute-start.1 = (bf16[128,1024]{1,0:T(8,128)(2,1)S(1)}, bf16[128,1024]{1,0:T(8,128)(2,1)S(1)}, u32[]{:S(2)}, u32[]{:S(2)}) collective-permute-start(bf16[128,1024]{1,0:T(8,128)(2,1)S(1)} %copy-done.9), channel_id=1, source_target_pairs={{0,256},{256,0},{1,257},{257,1},{2,258},{258,2},{3,259},{259,3},{4... | collective-permute-start | bytes 786440 | tf_op jit(solution)/shard_map/ppermute | solution.py:562
  37.5 13.9 %collective-permute-start = (f32[1,256]{1,0:T(1,128)S(1)}, f32[1,256]{1,0:T(1,128)S(1)}, u32[]{:S(2)}, u32[]{:S(2)}) collective-permute-start(f32[1,256]{1,0:T(1,128)S(1)} %copy-done.4), channel_id=1, source_target_pairs={{0,256},{256,0},{1,257},{257,1},{2,258},{258,2},{3,259},{259,3},{4... | collective-permute-start | bytes 3080 | tf_op jit(solution)/shard_map/ppermute | solution.py:562
  40.6 0.7 copy-start.8
  47.0 5.1 %collective-permute-start.2 = (bf16[128,1024]{1,0:T(8,128)(2,1)S(1)}, bf16[128,1024]{1,0:T(8,128)(2,1)S(1)}, u32[]{:S(2)}, u32[]{:S(2)}) collective-permute-start(bf16[128,1024]{1,0:T(8,128)(2,1)S(1)} %collective-permute-done.1.half_a), channel_id=1, source_target_pairs={{0,16},{16,0},{1,17},{17,1},{2,18},{18,2},{3,19},{19,3},{4,20},{20... | collective-permute-start | bytes 786440 | tf_op jit(solution)/shard_map/ppermute | solution.py:594
  51.0 1.2 copy-start.2
  51.3 0.8 copy-start.7
  51.3 0.8 copy-start.3
  51.4 0.7 copy-start.5
  51.4 0.8 copy-start.6
  78.0 3.4 %collective-permute-start.3 = (f32[32,16,128]{2,1,0:T(8,128)S(1)}, f32[32,16,128]{2,1,0:T(8,128)S(1)}, u32[]{:S(2)}, u32[]{:S(2)}) collective-permute-start(f32[32,16,128]{2,1,0:T(8,128)S(1)} %get-tuple-element.19), channel_id=1, source_target_pairs={{0,16},{16,0},{1,17},{17,1},{2,18},{18,2},{3,19},{19,3},{4,20},{20... | collective-permute-start | bytes 786440 | tf_op jit(solution)/shard_map/ppermute | solution.py:615
  126.8 7.8 %collective-permute-start.4 = (s16[16,72,128]{2,1,0:T(8,128)(2,1)S(1)}, s16[16,72,128]{2,1,0:T(8,128)(2,1)S(1)}, u32[]{:S(2)}, u32[]{:S(2)}) collective-permute-start(s16[16,72,128]{2,1,0:T(8,128)(2,1)S(1)} %all_to_all.22.mine), channel_id=1, source_target_pairs={{0,16},{16,0},{1,17},{17,1},{2,18},{18,2},{3,19},{19,3},{4,20},{20... | collective-permute-start | bytes 884744 | tf_op jit(solution)/shard_map/ppermute | solution.py:622

commit v7 on v6

--- a/solution.py
+++ b/solution.py
@@ -141,7 +141,7 @@
 
 
 def step(
-    scal, counts, slots, labels, pix, enc, cls, gain_a, gain_b, wqkv_a, wout_a, half_a, half_b, head, keep, give, *scratch
+    scal, counts, slots, labels, pix, enc, cls, gain_a, gain_b, wqkv_a, wqkv_b, wout_a, wout_b, head, keep, give, *scratch
 ):
     (wt, ws, ot, os, seq_a, seq_b, xhat_t, normed_t, k_t, kn_t, v_t, ad, ac, att_t, q_t, qn_t, e_cls, inv_c,
      u_s, xhat_s, normed_s, inv_s, k_s, kn_s, q_s, qn_s, v_s, a_s, att_s, log_s, tot, rows_s, y_w,
@@ -154,13 +154,10 @@
     lane_head = iota((PATCHES, D), 1) >> 5
     for h in range(HEADS):
         masks[h] = jnp.where(lane_head == h, 1.0, 0.0).astype(BF16)
-    for i in range(2):
-        at = slice(128 * i, 128 * i + 128)
-        far = jnp.where(scal[2] == i, half_a[...], half_b[...])
-        wt[at, :] = jnp.where(first, wqkv_a[0, at, :], far[:, : 3 * D])
-        ws[at, :] = jnp.where(first, far[:, : 3 * D], wqkv_a[0, at, :])
-        ot[at, :] = jnp.where(first, wout_a[0, at, :], far[:, 3 * D :])
-        os[at, :] = jnp.where(first, far[:, 3 * D :], wout_a[0, at, :])
+    wt[...] = jnp.where(first, wqkv_a[0], wqkv_b[0])
+    ws[...] = jnp.where(first, wqkv_b[0], wqkv_a[0])
+    ot[...] = jnp.where(first, wout_a[0], wout_b[0])
+    os[...] = jnp.where(first, wout_b[0], wout_a[0])
     gain_t = jnp.where(first, gain_a[...], gain_b[...])
     gain_s = jnp.where(first, gain_b[...], gain_a[...])
     head_row = head[...]
@@ -480,21 +477,6 @@
     return x * (jnp.exp2(power) * (1.0 / CODE_TOP))
 
 
-def prepare(core, pixels, wqkv, wout, half, by_dest, sems):
-    rows = pl.ds(pl.multiple_of(core[0] * 128, 128), 128)
-    copies = [
-        pltpu.make_async_copy(wqkv.at[0, rows, :], half.at[:, 0 : 3 * D], sems.at[0]),
-        pltpu.make_async_copy(wout.at[0, rows, :], half.at[:, 3 * D : 4 * D], sems.at[1]),
-    ]
-    for r in range(SHARE):
-        to = by_dest.at[pl.ds(TILES_DEV * r, TILES_DEV)]
-        copies.append(pltpu.make_async_copy(pixels, to, sems.at[2 + r]))
-    for copy in copies:
-        copy.start()
-    for copy in copies:
-        copy.wait()
-
-
 def code_pair(keep, given, out):
     out[...] = encode(keep[...] + given[...], 12)
 
@@ -532,8 +514,11 @@
             d_class[at : at + 1, 128:] = small[65:66]
             if b == 0 and part < 3:
                 ref = (d_gain, d_head, loss)[part]
-                ref[:, :128] = small[66:67]
-                ref[:, 128:] = small[67:68]
+                if part == 2:
+                    ref[...] = small[66:67, :MICRO]
+                else:
+                    ref[:, :128] = small[66:67]
+                    ref[:, 128:] = small[67:68]
 
 
 VM = pl.BlockSpec()
@@ -576,22 +561,9 @@
 ):
     first = (lax.axis_index("pipe") == 0).astype(I32)
     inner = lax.axis_index(INNER).astype(I32)
+    by_dest = jnp.tile(pixels.reshape(TILES_DEV, PATCHES, D), (SHARE, 1, 1))
+    whole_tile = lax.all_to_all(by_dest, INNER, 0, 0, tiled=True)
     core = lax.axis_index("core").astype(I32)
-    any_space = pl.BlockSpec(memory_space=pl.ANY)
-    half, by_dest = pl.pallas_call(
-        prepare,
-        out_shape=[
-            jax.ShapeDtypeStruct((128, 4 * D), BF16),
-            jax.ShapeDtypeStruct((MEMBERS, PATCHES, D), BF16),
-        ],
-        in_specs=[SM, any_space, any_space, any_space],
-        out_specs=[any_space] * 2,
-        scratch_shapes=[pltpu.SemaphoreType.DMA((6,))],
-        name="prepare",
-    )(core[None], pixels.reshape(TILES_DEV, PATCHES, D), wqkv, wout)
-    whole_tile = lax.all_to_all(by_dest, INNER, 0, 0, tiled=True)
-    half = swap(half)
-    other_half = lax.ppermute(half, "core", [(0, 1), (1, 0)])
     keep, give = call(
         step,
         [SM] * 3 + [VM] * 11,
@@ -606,9 +578,9 @@
         section_gain,
         swap(section_gain),
         wqkv,
+        swap(wqkv),
         wout,
-        half,
-        other_half,
+        swap(wout),
         head_vec.reshape(1, D),
         scratch=STEP_SCRATCH,
     )
@@ -624,7 +596,7 @@
         unpack,
         [SM, VM, VM],
         [
-            ((1, D), F32),
+            ((1, MICRO), F32),
             ((16, D), F32),
             ((1, D), F32),
             ((1, D, 3 * D), F32),
@@ -635,7 +607,7 @@
         mine,
         other,
     )
-    return (loss[0, :MICRO], d_class, d_gain, d_qkv, d_out, d_head.reshape(D))
+    return (loss.reshape(MICRO), d_class, d_gain, d_qkv, d_out, d_head.reshape(D))
 
 
 def solution(mesh):

time: 137 us -> 121 us (0.88)
  Pallas kernels: 48.6 us -> 27.6 us
  waiting for transfers between devices: 8.67 us -> 13.8 us
    pallas_call x1 -> x0, Pallas kernels: 21 us -> none  [whole_step(): pl.pallas_call(prepare, out_shape=[jax.ShapeDtypeStruct((128, 4 * D), BF1...]
    ppermute x2 -> x3, waiting for transfers between devices: 5.64 us -> 11.5 us  [swap(): return lax.ppermute(v, 'pipe', [(0, 1), (1, 0)])]
    ppermute x1 -> x0, starting transfers between devices: 3.94 us -> none  [whole_step(): other_half = lax.ppermute(half, 'core', [(0, 1), (1, 0)])]
    ppermute x2 -> x3, starting transfers between devices: 5.28 us -> 7.5 us  [swap(): return lax.ppermute(v, 'pipe', [(0, 1), (1, 0)])]
    another operation x0 -> x1, local copies, waits for them, and re-layouts: none -> 1.66 us  [whole_step(): by_dest = jnp.tile(pixels.reshape(TILES_DEV, PATCHES, D), (SHARE, 1, 1))]
where the time goes in v7:
time: 121 us; the launch traced here: 120 us
  blocking collectives  45.2 us (37%)
  starting transfers between devices  30.8 us (25%)
  Pallas kernels  27.6 us (23%)
  waiting for transfers between devices  13.8 us (11%)
  local copies, waits for them, and re-layouts  1.79 us (1%)
    pallas_call x5, Pallas kernels, call(): pl.pallas_call(body, out_shape=[jax.ShapeDtypeStruct(s, t) for s, t in ou...  27.6 us
    all_to_all x1, blocking collectives, whole_step(): parts = lax.all_to_all(coded, ('y', 'b'), 0, 0, tiled=True)  19.2 us
    all_to_all x1, blocking collectives, whole_step(): mine = lax.all_to_all(whole, INNER, 0, 0, tiled=True)  16.4 us
    all_to_all x1, starting transfers between devices, whole_step(): whole_tile = lax.all_to_all(by_dest, INNER, 0, 0, tiled=True)  13.5 us
    ppermute x3, waiting for transfers between devices, swap(): return lax.ppermute(v, 'pipe', [(0, 1), (1, 0)])  11.5 us
    all_to_all x1, blocking collectives, whole_step(): blocks = lax.all_to_all(total, 'y', 0, 0, tiled=True)  9.67 us
    ppermute x3, starting transfers between devices, swap(): return lax.ppermute(v, 'pipe', [(0, 1), (1, 0)])  7.5 us
    ppermute x1, starting transfers between devices, whole_step(): other = lax.ppermute(mine, 'core', [(0, 1), (1, 0)])  6.56 us
  transfers between devices with their start and end apart: 6, of which 4 were waited for; matrix products, arithmetic and copies ran while one was open for 0% of the time, Pallas kernels for 0%

profile of v7, /device:TPU:1, one launch (start us, length us, event | category | flops | bytes accessed | tf_op | source)
XLA Modules:
  0.0 120.5 jit_solution(158106856477243697)
XLA Ops:
  0.6 1.7 %tile.11 = bf16[4,4,48,256]{3,2,1,0:T(8,128)(2,1)} broadcast(bf16[4,48,256]{2,1,0:T(8,128)(2,1)} %bitcast.9), dimensions={1,2,3} | broadcast | bytes 491520 | tf_op jit(solution)/shard_map/tile | solution.py:564
  2.3 13.5 %all-to-all-start = ((bf16[16,48,256]{2,1,0:T(8,128)(2,1)}), bf16[16,48,256]{2,1,0:T(8,128)(2,1)S(1)}, u32[]{:S(2)}, u32[]{:S(2)}) async-start(bf16[16,48,256]{2,1,0:T(8,128)(2,1)} %bitcast.4), calls=%async_computation | async-start | bytes 786432 | tf_op jit(solution)/shard_map/all_to_all | solution.py:565
  15.9 0.0 copy-start.8
  15.9 2.2 %collective-permute-start = (f32[1,256]{1,0:T(1,128)S(1)}, f32[1,256]{1,0:T(1,128)S(1)}, u32[]{:S(2)}, u32[]{:S(2)}) collective-permute-start(f32[1,256]{1,0:T(1,128)S(1)} %copy-done.4), channel_id=1, source_target_pairs={{0,256},{256,0},{1,257},{257,1},{2,258},{258,2},{3,259},{259,3},{4... | collective-permute-start | bytes 3080 | tf_op jit(solution)/shard_map/ppermute | solution.py:547
  18.1 3.1 %collective-permute-start.2 = (bf16[1,256,256]{2,1,0:T(8,128)(2,1)S(1)}, bf16[1,256,256]{2,1,0:T(8,128)(2,1)S(1)}, u32[]{:S(2)}, u32[]{:S(2)}) collective-permute-start(bf16[1,256,256]{2,1,0:T(8,128)(2,1)S(1)} %copy-done.1), channel_id=1, source_target_pairs={{0,256},{256,0},{1,257},{257,1},{2,258},{258,2},{3,259},{259,3},{4... | collective-permute-start | bytes 393224 | tf_op jit(solution)/shard_map/ppermute | solution.py:547
  21.2 2.2 %collective-permute-start.1 = (bf16[1,256,768]{2,1,0:T(8,128)(2,1)S(1)}, bf16[1,256,768]{2,1,0:T(8,128)(2,1)S(1)}, u32[]{:S(2)}, u32[]{:S(2)}) collective-permute-start(bf16[1,256,768]{2,1,0:T(8,128)(2,1)S(1)} %copy-done), channel_id=1, source_target_pairs={{0,256},{256,0},{1,257},{257,1},{2,258},{258,2},{3,259},{259,3},{4... | collective-permute-start | bytes 1179656 | tf_op jit(solution)/shard_map/ppermute | solution.py:547
  23.5 0.1 mul.38
  23.6 0.3 fusion.enc
  23.9 0.0 copy-start.2
  23.9 0.1 pad_add_fusion.scal
  24.0 2.5 %collective-permute-done.2.wout_b = bf16[1,256,256]{2,1,0:T(8,128)(2,1)S(1)} collective-permute-done((bf16[1,256,256]{2,1,0:T(8,128)(2,1)S(1)}, bf16[1,256,256]{2,1,0:T(8,128)(2,1)S(1)}, u32[]{:S(2)}, u32[]{:S(2)}) %collective-permute-start.2) | collective-permute-done | bytes 131104 | tf_op jit(solution)/shard_map/ppermute | solution.py:547
  26.6 9.0 %collective-permute-done.1.wqkv_b = bf16[1,256,768]{2,1,0:T(8,128)(2,1)S(1)} collective-permute-done((bf16[1,256,768]{2,1,0:T(8,128)(2,1)S(1)}, bf16[1,256,768]{2,1,0:T(8,128)(2,1)S(1)}, u32[]{:S(2)}, u32[]{:S(2)}) %collective-permute-start.1) | collective-permute-done | bytes 393248 | tf_op jit(solution)/shard_map/ppermute | solution.py:547
  35.6 25.8 %shard_map.145 = (f32[32,16,128]{2,1,0:T(8,128)S(1)}, f32[32,16,128]{2,1,0:T(8,128)S(1)}) custom-call(s32[3]{0:T(128)S(1)} %pad_add_fusion.scal, s32[4]{0:T(128)S(1)} %copy-done.6, s32[4]{0:T(128)S(1)} %copy-done.7, s32[4,48]{1,0:T(4,128)S(1)} %copy-done.3, bf16[16,48,256]{2,1,0:T(8,128)(2,1)S(1)} %all-to-all-done.pix, f32[64,256]{1,0:T(8,128)S(1)} %fusion.enc, ...), custom_call_target="tpu_custom_call" | custom-call | tf_op jit(solution)/shard_map/pallas_call | solution.py:529
  61.3 3.2 %collective-permute-start.3 = (f32[32,16,128]{2,1,0:T(8,128)S(1)}, f32[32,16,128]{2,1,0:T(8,128)S(1)}, u32[]{:S(2)}, u32[]{:S(2)}) collective-permute-start(f32[32,16,128]{2,1,0:T(8,128)S(1)} %get-tuple-element.15), channel_id=1, source_target_pairs={{0,16},{16,0},{1,17},{17,1},{2,18},{18,2},{3,19},{19,3},{4,20},{20... | collective-permute-start | bytes 786440 | tf_op jit(solution)/shard_map/ppermute | solution.py:587
  64.5 1.1 collective-permute-done.3.given
  65.7 0.3 shard_map.146
  65.9 19.2 %all_to_all.20.parts = s16[32,16,128]{2,1,0:T(8,128)(2,1)S(1)} all-to-all(s16[32,16,128]{2,1,0:T(8,128)(2,1)S(1)} %shard_map.146), channel_id=1, replica_groups=mesh['pipe'=2,'y'=8,'core'=2,'r'=4,'b'=4] {'y','b'}, dimensions={0} | all-to-all | bytes 262144 | tf_op jit(solution)/shard_map/all_to_all | solution.py:589
  85.1 0.2 shard_map.147
  85.3 9.7 %all_to_all.21.blocks = f32[8,16,128]{2,1,0:T(8,128)S(1)} all-to-all(f32[8,16,128]{2,1,0:T(8,128)S(1)} %shard_map.147), channel_id=1, replica_groups=mesh['pipe'=2,'y'=8,'core'=2,'r'=4,'b'=4] {'y'}, dimensions={0} | all-to-all | bytes 131072 | tf_op jit(solution)/shard_map/all_to_all | solution.py:591
  94.9 0.1 shard_map.148
  95.1 16.4 %all_to_all.22.mine = s16[16,72,128]{2,1,0:T(8,128)(2,1)S(1)} all-to-all(s16[16,72,128]{2,1,0:T(8,128)(2,1)S(1)} %shard_map.148), channel_id=1, replica_groups=mesh['pipe'=2,'y'=8,'core'=2,'r'=4,'b'=4] {'r','b'}, dimensions={0} | all-to-all | bytes 589824 | tf_op jit(solution)/shard_map/all_to_all | solution.py:593
  111.4 6.6 %collective-permute-start.4 = (s16[16,72,128]{2,1,0:T(8,128)(2,1)S(1)}, s16[16,72,128]{2,1,0:T(8,128)(2,1)S(1)}, u32[]{:S(2)}, u32[]{:S(2)}) collective-permute-start(s16[16,72,128]{2,1,0:T(8,128)(2,1)S(1)} %all_to_all.22.mine), channel_id=1, source_target_pairs={{0,16},{16,0},{1,17},{17,1},{2,18},{18,2},{3,19},{19,3},{4,20},{20... | collective-permute-start | bytes 884744 | tf_op jit(solution)/shard_map/ppermute | solution.py:594
  118.0 1.2 collective-permute-done.4.other
  119.2 1.3 %shard_map.149 = (f32[1,4]{1,0:T(1,128)}, f32[16,256]{1,0:T(8,128)}, f32[1,256]{1,0:T(1,128)}, f32[1,256,768]{2,1,0:T(8,128)}, f32[1,256,256]{2,1,0:T(8,128)}, /*index=5*/f32[1,256]{1,0:T(1,128)}) custom-call(s32[1]{0:T(128)} %bitcast.core, s16[16,72,128]{2,1,0:T(8,128)(2,1)S(1)} %all_to_all.22.mine, s16[16,72,128]{2,1,0:T(8,128)(2,1)S(1)} %collective-permute-done.4.other), custom_call_target="tpu_custom_call" | custom-call | tf_op jit(solution)/shard_map/pallas_call | solution.py:529
  (21 shorter events, 0.1 us)
Async XLA Ops:
  2.3 13.6 %copy-start.4 = (f32[1,256]{1,0:T(1,128)S(1)}, f32[1,256]{1,0:T(1,128)}, u32[]{:S(2)}) copy-start(f32[1,256]{1,0:T(1,128)} %gain_a.1) | copy-start | bytes 3076
  2.3 15.8 %copy-start.1 = (bf16[1,256,256]{2,1,0:T(8,128)(2,1)S(1)}, bf16[1,256,256]{2,1,0:T(8,128)(2,1)}, u32[]{:S(2)}) copy-start(bf16[1,256,256]{2,1,0:T(8,128)(2,1)} %wout_a.1) | copy-start | bytes 393220
  2.3 18.9 %copy-start = (bf16[1,256,768]{2,1,0:T(8,128)(2,1)S(1)}, bf16[1,256,768]{2,1,0:T(8,128)(2,1)}, u32[]{:S(2)}) copy-start(bf16[1,256,768]{2,1,0:T(8,128)(2,1)} %wqkv_a.1) | copy-start | bytes 1179652
  2.3 33.2 %all-to-all-start = ((bf16[16,48,256]{2,1,0:T(8,128)(2,1)}), bf16[16,48,256]{2,1,0:T(8,128)(2,1)S(1)}, u32[]{:S(2)}, u32[]{:S(2)}) async-start(bf16[16,48,256]{2,1,0:T(8,128)(2,1)} %bitcast.4), calls=%async_computation | async-start | bytes 786432 | tf_op jit(solution)/shard_map/all_to_all | solution.py:565
  15.9 7.6 %copy-start.8 = (s32[4,16]{1,0:T(4,128)S(1)}, s32[4,16]{1,0:T(4,128)}, u32[]{:S(2)}) copy-start(s32[4,16]{1,0:T(4,128)} %param.11) | copy-start | bytes 772
  15.9 8.1 %collective-permute-start = (f32[1,256]{1,0:T(1,128)S(1)}, f32[1,256]{1,0:T(1,128)S(1)}, u32[]{:S(2)}, u32[]{:S(2)}) collective-permute-start(f32[1,256]{1,0:T(1,128)S(1)} %copy-done.4), channel_id=1, source_target_pairs={{0,256},{256,0},{1,257},{257,1},{2,258},{258,2},{3,259},{259,3},{4... | collective-permute-start | bytes 3080 | tf_op jit(solution)/shard_map/ppermute | solution.py:547
  18.1 8.4 %collective-permute-start.2 = (bf16[1,256,256]{2,1,0:T(8,128)(2,1)S(1)}, bf16[1,256,256]{2,1,0:T(8,128)(2,1)S(1)}, u32[]{:S(2)}, u32[]{:S(2)}) collective-permute-start(bf16[1,256,256]{2,1,0:T(8,128)(2,1)S(1)} %copy-done.1), channel_id=1, source_target_pairs={{0,256},{256,0},{1,257},{257,1},{2,258},{258,2},{3,259},{259,3},{4... | collective-permute-start | bytes 393224 | tf_op jit(solution)/shard_map/ppermute | solution.py:547
  21.2 14.3 %collective-permute-start.1 = (bf16[1,256,768]{2,1,0:T(8,128)(2,1)S(1)}, bf16[1,256,768]{2,1,0:T(8,128)(2,1)S(1)}, u32[]{:S(2)}, u32[]{:S(2)}) collective-permute-start(bf16[1,256,768]{2,1,0:T(8,128)(2,1)S(1)} %copy-done), channel_id=1, source_target_pairs={{0,256},{256,0},{1,257},{257,1},{2,258},{258,2},{3,259},{259,3},{4... | collective-permute-start | bytes 1179656 | tf_op jit(solution)/shard_map/ppermute | solution.py:547
  23.9 11.6 %copy-start.2 = (bf16[16,256]{1,0:T(8,128)(2,1)S(1)}, bf16[16,256]{1,0:T(8,128)(2,1)}, u32[]{:S(2)}) copy-start(bf16[16,256]{1,0:T(8,128)(2,1)} %cls.1) | copy-start | bytes 24580
  23.9 11.6 %copy-start.7 = (s32[4]{0:T(128)S(1)}, s32[4]{0:T(128)}, u32[]{:S(2)}) copy-start(s32[4]{0:T(128)} %slots.1) | copy-start | bytes 52
  23.9 11.6 %copy-start.3 = (s32[4,48]{1,0:T(4,128)S(1)}, s32[4,48]{1,0:T(4,128)}, u32[]{:S(2)}) copy-start(s32[4,48]{1,0:T(4,128)} %labels.1) | copy-start | bytes 2308
  24.0 11.5 %copy-start.5 = (f32[256]{0:T(256)S(1)}, f32[256]{0:T(256)}, u32[]{:S(2)}) copy-start(f32[256]{0:T(256)} %param.19) | copy-start | bytes 3076
  24.0 11.5 %copy-start.6 = (s32[4]{0:T(128)S(1)}, s32[4]{0:T(128)}, u32[]{:S(2)}) copy-start(s32[4]{0:T(128)} %counts.1) | copy-start | bytes 52
  61.3 4.3 %collective-permute-start.3 = (f32[32,16,128]{2,1,0:T(8,128)S(1)}, f32[32,16,128]{2,1,0:T(8,128)S(1)}, u32[]{:S(2)}, u32[]{:S(2)}) collective-permute-start(f32[32,16,128]{2,1,0:T(8,128)S(1)} %get-tuple-element.15), channel_id=1, source_target_pairs={{0,16},{16,0},{1,17},{17,1},{2,18},{18,2},{3,19},{19,3},{4,20},{20... | collective-permute-start | bytes 786440 | tf_op jit(solution)/shard_map/ppermute | solution.py:587
  111.4 7.8 %collective-permute-start.4 = (s16[16,72,128]{2,1,0:T(8,128)(2,1)S(1)}, s16[16,72,128]{2,1,0:T(8,128)(2,1)S(1)}, u32[]{:S(2)}, u32[]{:S(2)}) collective-permute-start(s16[16,72,128]{2,1,0:T(8,128)(2,1)S(1)} %all_to_all.22.mine), channel_id=1, source_target_pairs={{0,16},{16,0},{1,17},{17,1},{2,18},{18,2},{3,19},{19,3},{4,20},{20... | collective-permute-start | bytes 884744 | tf_op jit(solution)/shard_map/ppermute | solution.py:594

commit v8 on v7

--- a/solution.py
+++ b/solution.py
@@ -478,18 +478,20 @@
 
 
 def code_pair(keep, given, out):
-    out[...] = encode(keep[...] + given[...], 12)
-
-
-def reduce_tiles(parts, out):
-    total = jnp.sum(decode(parts[...], 12), axis=0)
-    out[...] = jnp.broadcast_to(total[None], (YS, 16, 128))
-
-
-def assemble(blocks, out):
-    small = jnp.where(iota((8, 128), 0) < 4, blocks[0, 8:16, :], 0.0)
-    whole = stack([blocks[y, 0:8, :] for y in range(YS)] + [small])
-    out[...] = jnp.broadcast_to(encode(whole[None], 68), (MEMBERS, CHUNK, 128))
+    x = keep[...] + given[...]
+    spare = iota((8, 128), 0) < 4
+    chunks = []
+    for b in range(TILES_DEV):
+        tiles = [x[TILES_DEV * y + b, 0:8, :] for y in range(YS)]
+        chunks.append(stack(tiles + [jnp.where(spare, x[b, 8:16, :], 0.0)])[None])
+    coded = encode(jnp.concatenate(chunks, axis=0), 68)
+    for y in range(YS):
+        out[TILES_DEV * y : TILES_DEV * y + TILES_DEV] = coded
+
+
+def merge(parts, out):
+    total = jnp.sum(decode(parts[...], 68), axis=0)
+    out[...] = jnp.broadcast_to(encode(total[None], 68), (MEMBERS, CHUNK, 128))
 
 
 def unpack(core, mine, other, loss, d_class, d_gain, d_qkv, d_out, d_head):
@@ -585,11 +587,9 @@
         scratch=STEP_SCRATCH,
     )
     given = lax.ppermute(give, "core", [(0, 1), (1, 0)])
-    (coded,) = call(code_pair, [VM, VM], [((OWNERS, 16, 128), jnp.int16)], keep, given)
+    (coded,) = call(code_pair, [VM, VM], [((OWNERS, CHUNK, 128), jnp.int16)], keep, given)
     parts = lax.all_to_all(coded, ("y", "b"), 0, 0, tiled=True)
-    (total,) = call(reduce_tiles, [VM], [((YS, 16, 128), F32)], parts)
-    blocks = lax.all_to_all(total, "y", 0, 0, tiled=True)
-    (whole,) = call(assemble, [VM], [((MEMBERS, CHUNK, 128), jnp.int16)], blocks)
+    (whole,) = call(merge, [VM], [((MEMBERS, CHUNK, 128), jnp.int16)], parts)
     mine = lax.all_to_all(whole, INNER, 0, 0, tiled=True)
     other = lax.ppermute(mine, "core", [(0, 1), (1, 0)])
     loss, d_class, d_gain, d_qkv, d_out, d_head = call(

time: 121 us -> 119 us (0.983)
  blocking collectives: 45.2 us -> 43.9 us
    all_to_all x1 -> x0, blocking collectives: 9.67 us -> none  [whole_step(): blocks = lax.all_to_all(total, 'y', 0, 0, tiled=True)]
    all_to_all x1, blocking collectives: 19.2 us -> 27.5 us  [whole_step(): parts = lax.all_to_all(coded, ('y', 'b'), 0, 0, tiled=True)]
    pallas_call x5 -> x4, Pallas kernels: 27.6 us -> 27.8 us  [call(): pl.pallas_call(body, out_shape=[jax.ShapeDtypeStruct(s, t) for s, t in ou...]
where the time goes in v8:
time: 119 us
  blocking collectives  43.9 us (37%)
  starting transfers between devices  30 us (25%)
  Pallas kernels  27.8 us (23%)
  waiting for transfers between devices  13.8 us (12%)
  local copies, waits for them, and re-layouts  1.79 us (2%)
    pallas_call x4, Pallas kernels, call(): pl.pallas_call(body, out_shape=[jax.ShapeDtypeStruct(s, t) for s, t in ou...  27.8 us
    all_to_all x1, blocking collectives, whole_step(): parts = lax.all_to_all(coded, ('y', 'b'), 0, 0, tiled=True)  27.5 us
    all_to_all x1, blocking collectives, whole_step(): mine = lax.all_to_all(whole, INNER, 0, 0, tiled=True)  16.5 us
    all_to_all x1, starting transfers between devices, whole_step(): whole_tile = lax.all_to_all(by_dest, INNER, 0, 0, tiled=True)  13.5 us
    ppermute x3, waiting for transfers between devices, swap(): return lax.ppermute(v, 'pipe', [(0, 1), (1, 0)])  11.5 us
    ppermute x3, starting transfers between devices, swap(): return lax.ppermute(v, 'pipe', [(0, 1), (1, 0)])  7.5 us
    ppermute x1, starting transfers between devices, whole_step(): other = lax.ppermute(mine, 'core', [(0, 1), (1, 0)])  5.73 us
    ppermute x1, starting transfers between devices, whole_step(): given = lax.ppermute(give, 'core', [(0, 1), (1, 0)])  3.17 us
  transfers between devices with their start and end apart: 6, of which 4 were waited for; matrix products, arithmetic and copies ran while one was open for 0% of the time, Pallas kernels for 0%

profile of v8, /device:TPU:1, one launch (start us, length us, event | category | flops | bytes accessed | tf_op | source)
XLA Modules:
  0.0 118.5 jit_solution(14371606194285529256)
XLA Ops:
  0.6 1.7 %tile.11 = bf16[4,4,48,256]{3,2,1,0:T(8,128)(2,1)} broadcast(bf16[4,48,256]{2,1,0:T(8,128)(2,1)} %bitcast.9), dimensions={1,2,3} | broadcast | bytes 491520 | tf_op jit(solution)/shard_map/tile | solution.py:566
  2.3 13.5 %all-to-all-start = ((bf16[16,48,256]{2,1,0:T(8,128)(2,1)}), bf16[16,48,256]{2,1,0:T(8,128)(2,1)S(1)}, u32[]{:S(2)}, u32[]{:S(2)}) async-start(bf16[16,48,256]{2,1,0:T(8,128)(2,1)} %bitcast.4), calls=%async_computation | async-start | bytes 786432 | tf_op jit(solution)/shard_map/all_to_all | solution.py:567
  15.9 0.0 copy-start.8
  15.9 2.2 %collective-permute-start = (f32[1,256]{1,0:T(1,128)S(1)}, f32[1,256]{1,0:T(1,128)S(1)}, u32[]{:S(2)}, u32[]{:S(2)}) collective-permute-start(f32[1,256]{1,0:T(1,128)S(1)} %copy-done.4), channel_id=1, source_target_pairs={{0,256},{256,0},{1,257},{257,1},{2,258},{258,2},{3,259},{259,3},{4... | collective-permute-start | bytes 3080 | tf_op jit(solution)/shard_map/ppermute | solution.py:549
  18.1 3.1 %collective-permute-start.2 = (bf16[1,256,256]{2,1,0:T(8,128)(2,1)S(1)}, bf16[1,256,256]{2,1,0:T(8,128)(2,1)S(1)}, u32[]{:S(2)}, u32[]{:S(2)}) collective-permute-start(bf16[1,256,256]{2,1,0:T(8,128)(2,1)S(1)} %copy-done.1), channel_id=1, source_target_pairs={{0,256},{256,0},{1,257},{257,1},{2,258},{258,2},{3,259},{259,3},{4... | collective-permute-start | bytes 393224 | tf_op jit(solution)/shard_map/ppermute | solution.py:549
  21.2 2.2 %collective-permute-start.1 = (bf16[1,256,768]{2,1,0:T(8,128)(2,1)S(1)}, bf16[1,256,768]{2,1,0:T(8,128)(2,1)S(1)}, u32[]{:S(2)}, u32[]{:S(2)}) collective-permute-start(bf16[1,256,768]{2,1,0:T(8,128)(2,1)S(1)} %copy-done), channel_id=1, source_target_pairs={{0,256},{256,0},{1,257},{257,1},{2,258},{258,2},{3,259},{259,3},{4... | collective-permute-start | bytes 1179656 | tf_op jit(solution)/shard_map/ppermute | solution.py:549
  23.5 0.1 mul.38
  23.6 0.3 fusion.enc
  23.9 0.0 copy-start.2
  23.9 0.0 copy-start.7
  23.9 0.0 copy-start.3
  23.9 0.1 pad_add_fusion.scal
  24.0 2.5 %collective-permute-done.2.wout_b = bf16[1,256,256]{2,1,0:T(8,128)(2,1)S(1)} collective-permute-done((bf16[1,256,256]{2,1,0:T(8,128)(2,1)S(1)}, bf16[1,256,256]{2,1,0:T(8,128)(2,1)S(1)}, u32[]{:S(2)}, u32[]{:S(2)}) %collective-permute-start.2) | collective-permute-done | bytes 131104 | tf_op jit(solution)/shard_map/ppermute | solution.py:549
  26.6 9.0 %collective-permute-done.1.wqkv_b = bf16[1,256,768]{2,1,0:T(8,128)(2,1)S(1)} collective-permute-done((bf16[1,256,768]{2,1,0:T(8,128)(2,1)S(1)}, bf16[1,256,768]{2,1,0:T(8,128)(2,1)S(1)}, u32[]{:S(2)}, u32[]{:S(2)}) %collective-permute-start.1) | collective-permute-done | bytes 393248 | tf_op jit(solution)/shard_map/ppermute | solution.py:549
  35.6 25.8 %shard_map.145 = (f32[32,16,128]{2,1,0:T(8,128)S(1)}, f32[32,16,128]{2,1,0:T(8,128)S(1)}) custom-call(s32[3]{0:T(128)S(1)} %pad_add_fusion.scal, s32[4]{0:T(128)S(1)} %copy-done.6, s32[4]{0:T(128)S(1)} %copy-done.7, s32[4,48]{1,0:T(4,128)S(1)} %copy-done.3, bf16[16,48,256]{2,1,0:T(8,128)(2,1)S(1)} %all-to-all-done.pix, f32[64,256]{1,0:T(8,128)S(1)} %fusion.enc, ...), custom_call_target="tpu_custom_call" | custom-call | tf_op jit(solution)/shard_map/pallas_call | solution.py:531
  61.3 3.2 %collective-permute-start.3 = (f32[32,16,128]{2,1,0:T(8,128)S(1)}, f32[32,16,128]{2,1,0:T(8,128)S(1)}, u32[]{:S(2)}, u32[]{:S(2)}) collective-permute-start(f32[32,16,128]{2,1,0:T(8,128)S(1)} %get-tuple-element.15), channel_id=1, source_target_pairs={{0,16},{16,0},{1,17},{17,1},{2,18},{18,2},{3,19},{19,3},{4,20},{20... | collective-permute-start | bytes 786440 | tf_op jit(solution)/shard_map/ppermute | solution.py:589
  64.5 1.1 collective-permute-done.3.given
  65.7 0.2 shard_map.146
  65.9 27.5 %all_to_all.15.parts = s16[32,72,128]{2,1,0:T(8,128)(2,1)S(1)} all-to-all(s16[32,72,128]{2,1,0:T(8,128)(2,1)S(1)} %shard_map.146), channel_id=1, replica_groups=mesh['pipe'=2,'y'=8,'core'=2,'r'=4,'b'=4] {'y','b'}, dimensions={0} | all-to-all | bytes 1179648 | tf_op jit(solution)/shard_map/all_to_all | solution.py:591
  93.3 0.5 shard_map.147
  93.8 16.5 %all_to_all.16.mine = s16[16,72,128]{2,1,0:T(8,128)(2,1)S(1)} all-to-all(s16[16,72,128]{2,1,0:T(8,128)(2,1)S(1)} %shard_map.147), channel_id=1, replica_groups=mesh['pipe'=2,'y'=8,'core'=2,'r'=4,'b'=4] {'r','b'}, dimensions={0} | all-to-all | bytes 589824 | tf_op jit(solution)/shard_map/all_to_all | solution.py:593
  110.3 5.7 %collective-permute-start.4 = (s16[16,72,128]{2,1,0:T(8,128)(2,1)S(1)}, s16[16,72,128]{2,1,0:T(8,128)(2,1)S(1)}, u32[]{:S(2)}, u32[]{:S(2)}) collective-permute-start(s16[16,72,128]{2,1,0:T(8,128)(2,1)S(1)} %all_to_all.16.mine), channel_id=1, source_target_pairs={{0,16},{16,0},{1,17},{17,1},{2,18},{18,2},{3,19},{19,3},{4,20},{20... | collective-permute-start | bytes 884744 | tf_op jit(solution)/shard_map/ppermute | solution.py:594
  116.0 1.2 %collective-permute-done.4.other = s16[16,72,128]{2,1,0:T(8,128)(2,1)S(1)} collective-permute-done((s16[16,72,128]{2,1,0:T(8,128)(2,1)S(1)}, s16[16,72,128]{2,1,0:T(8,128)(2,1)S(1)}, u32[]{:S(2)}, u32[]{:S(2)}) %collective-permute-start.4) | collective-permute-done | bytes 294944 | tf_op jit(solution)/shard_map/ppermute | solution.py:594
  117.2 1.3 %shard_map.148 = (f32[1,4]{1,0:T(1,128)}, f32[16,256]{1,0:T(8,128)}, f32[1,256]{1,0:T(1,128)}, f32[1,256,768]{2,1,0:T(8,128)}, f32[1,256,256]{2,1,0:T(8,128)}, /*index=5*/f32[1,256]{1,0:T(1,128)}) custom-call(s32[1]{0:T(128)} %bitcast.core, s16[16,72,128]{2,1,0:T(8,128)(2,1)S(1)} %all_to_all.16.mine, s16[16,72,128]{2,1,0:T(8,128)(2,1)S(1)} %collective-permute-done.4.other), custom_call_target="tpu_custom_call" | custom-call | tf_op jit(solution)/shard_map/pallas_call | solution.py:531
  (19 shorter events, 0.1 us)
Async XLA Ops:
  2.3 13.6 %copy-start.4 = (f32[1,256]{1,0:T(1,128)S(1)}, f32[1,256]{1,0:T(1,128)}, u32[]{:S(2)}) copy-start(f32[1,256]{1,0:T(1,128)} %gain_a.1) | copy-start | bytes 3076
  2.3 15.8 %copy-start.1 = (bf16[1,256,256]{2,1,0:T(8,128)(2,1)S(1)}, bf16[1,256,256]{2,1,0:T(8,128)(2,1)}, u32[]{:S(2)}) copy-start(bf16[1,256,256]{2,1,0:T(8,128)(2,1)} %wout_a.1) | copy-start | bytes 393220
  2.3 18.9 %copy-start = (bf16[1,256,768]{2,1,0:T(8,128)(2,1)S(1)}, bf16[1,256,768]{2,1,0:T(8,128)(2,1)}, u32[]{:S(2)}) copy-start(bf16[1,256,768]{2,1,0:T(8,128)(2,1)} %wqkv_a.1) | copy-start | bytes 1179652
  2.3 33.2 %all-to-all-start = ((bf16[16,48,256]{2,1,0:T(8,128)(2,1)}), bf16[16,48,256]{2,1,0:T(8,128)(2,1)S(1)}, u32[]{:S(2)}, u32[]{:S(2)}) async-start(bf16[16,48,256]{2,1,0:T(8,128)(2,1)} %bitcast.4), calls=%async_computation | async-start | bytes 786432 | tf_op jit(solution)/shard_map/all_to_all | solution.py:567
  15.9 7.6 %copy-start.8 = (s32[4,16]{1,0:T(4,128)S(1)}, s32[4,16]{1,0:T(4,128)}, u32[]{:S(2)}) copy-start(s32[4,16]{1,0:T(4,128)} %param.11) | copy-start | bytes 772
  15.9 8.1 %collective-permute-start = (f32[1,256]{1,0:T(1,128)S(1)}, f32[1,256]{1,0:T(1,128)S(1)}, u32[]{:S(2)}, u32[]{:S(2)}) collective-permute-start(f32[1,256]{1,0:T(1,128)S(1)} %copy-done.4), channel_id=1, source_target_pairs={{0,256},{256,0},{1,257},{257,1},{2,258},{258,2},{3,259},{259,3},{4... | collective-permute-start | bytes 3080 | tf_op jit(solution)/shard_map/ppermute | solution.py:549
  18.1 8.4 %collective-permute-start.2 = (bf16[1,256,256]{2,1,0:T(8,128)(2,1)S(1)}, bf16[1,256,256]{2,1,0:T(8,128)(2,1)S(1)}, u32[]{:S(2)}, u32[]{:S(2)}) collective-permute-start(bf16[1,256,256]{2,1,0:T(8,128)(2,1)S(1)} %copy-done.1), channel_id=1, source_target_pairs={{0,256},{256,0},{1,257},{257,1},{2,258},{258,2},{3,259},{259,3},{4... | collective-permute-start | bytes 393224 | tf_op jit(solution)/shard_map/ppermute | solution.py:549
  21.2 14.3 %collective-permute-start.1 = (bf16[1,256,768]{2,1,0:T(8,128)(2,1)S(1)}, bf16[1,256,768]{2,1,0:T(8,128)(2,1)S(1)}, u32[]{:S(2)}, u32[]{:S(2)}) collective-permute-start(bf16[1,256,768]{2,1,0:T(8,128)(2,1)S(1)} %copy-done), channel_id=1, source_target_pairs={{0,256},{256,0},{1,257},{257,1},{2,258},{258,2},{3,259},{259,3},{4... | collective-permute-start | bytes 1179656 | tf_op jit(solution)/shard_map/ppermute | solution.py:549
  23.9 11.6 %copy-start.2 = (bf16[16,256]{1,0:T(8,128)(2,1)S(1)}, bf16[16,256]{1,0:T(8,128)(2,1)}, u32[]{:S(2)}) copy-start(bf16[16,256]{1,0:T(8,128)(2,1)} %cls.1) | copy-start | bytes 24580
  23.9 11.6 %copy-start.7 = (s32[4]{0:T(128)S(1)}, s32[4]{0:T(128)}, u32[]{:S(2)}) copy-start(s32[4]{0:T(128)} %slots.1) | copy-start | bytes 52
  23.9 11.6 %copy-start.3 = (s32[4,48]{1,0:T(4,128)S(1)}, s32[4,48]{1,0:T(4,128)}, u32[]{:S(2)}) copy-start(s32[4,48]{1,0:T(4,128)} %labels.1) | copy-start | bytes 2308
  24.0 11.5 %copy-start.5 = (f32[256]{0:T(256)S(1)}, f32[256]{0:T(256)}, u32[]{:S(2)}) copy-start(f32[256]{0:T(256)} %param.19) | copy-start | bytes 3076
  24.0 11.5 %copy-start.6 = (s32[4]{0:T(128)S(1)}, s32[4]{0:T(128)}, u32[]{:S(2)}) copy-start(s32[4]{0:T(128)} %counts.1) | copy-start | bytes 52
  61.3 4.3 %collective-permute-start.3 = (f32[32,16,128]{2,1,0:T(8,128)S(1)}, f32[32,16,128]{2,1,0:T(8,128)S(1)}, u32[]{:S(2)}, u32[]{:S(2)}) collective-permute-start(f32[32,16,128]{2,1,0:T(8,128)S(1)} %get-tuple-element.15), channel_id=1, source_target_pairs={{0,16},{16,0},{1,17},{17,1},{2,18},{18,2},{3,19},{19,3},{4,20},{20... | collective-permute-start | bytes 786440 | tf_op jit(solution)/shard_map/ppermute | solution.py:589
  110.3 6.9 %collective-permute-start.4 = (s16[16,72,128]{2,1,0:T(8,128)(2,1)S(1)}, s16[16,72,128]{2,1,0:T(8,128)(2,1)S(1)}, u32[]{:S(2)}, u32[]{:S(2)}) collective-permute-start(s16[16,72,128]{2,1,0:T(8,128)(2,1)S(1)} %all_to_all.16.mine), channel_id=1, source_target_pairs={{0,16},{16,0},{1,17},{17,1},{2,18},{18,2},{3,19},{19,3},{4,20},{20... | collective-permute-start | bytes 884744 | tf_op jit(solution)/shard_map/ppermute | solution.py:594
